TPU v7x, 512 devices: a whole 4x4x16 slice. The times are simulated.
512 devices in a mesh: ctx: 64 (over z_hi, y, x, core), tp: 8 (over z_lo).
Axes of the slice: x: 4, y: 4, z: 16 (z_hi: 2, z_lo: 8; z = z_hi * 8 + z_lo), core: 2. Of those that a mesh axis runs over, the one named last changes fastest.
Arguments:
- k_feature: bfloat16 [32, 524288], P('tp', 'ctx'), may hold values from -6 to 6
- v_feature: bfloat16 [32, 524288], P('tp', 'ctx'), may hold values from -6 to 6
- q_feature: bfloat16 [32, 524288], P('tp', 'ctx'), may hold values from -6 to 6
- spectrum: bfloat16 [2, 32, 1024, 1024], P(None, 'tp', 'ctx'), may hold values from -6 to 6
- skip_gain: float32 [32], P('tp'), may hold values from -1 to 1
- out_weight: bfloat16 [32, 64], replicated, may hold values from -1 to 1
Outputs:
- mixed: bfloat16 [64, 524288], P('tp', 'ctx')
All inputs are finite; a program needn't handle non-finite values.
Results may differ from a plain program's by a relative error of at most 0.015.
Values may be sent and summed in bfloat16 or wider, within the bound.
A program may use at most 64 MiB of HBM per device.

v0:
```python
import math

import jax
import jax.numpy as jnp
from jax import lax
from jax.sharding import PartitionSpec as P


def fourier_tables(length_all):
    split = 1 << (int(math.log2(length_all)) // 2)
    rows_hi = length_all // split
    scale = 2.0 * math.pi / length_all
    columns = jnp.arange(length_all, dtype=jnp.int32)
    low = jnp.arange(split, dtype=jnp.int32)
    high = jnp.arange(rows_hi, dtype=jnp.int32)
    angle_low = (low[:, None] * columns[None, :] % length_all).astype(jnp.float32) * scale
    angle_high = (split * high[:, None] * columns[None, :] % length_all).astype(jnp.float32) * scale
    cos_low, sin_low = jnp.cos(angle_low)[None], jnp.sin(angle_low)[None]
    cos_high, sin_high = jnp.cos(angle_high)[:, None], jnp.sin(angle_high)[:, None]
    cosine = (cos_high * cos_low - sin_high * sin_low).reshape(length_all, length_all)
    sine = (sin_high * cos_low + cos_high * sin_low).reshape(length_all, length_all)
    return lax.optimization_barrier((cosine.astype(jnp.bfloat16), sine.astype(jnp.bfloat16)))


def twist_tables(left_index, right_index, length_all):
    phase_index = left_index[:, None] * right_index[None, :] % length_all
    angles = phase_index.astype(jnp.float32) * (2.0 * math.pi / length_all)
    return (jnp.cos(angles), jnp.sin(angles))


def contract(form, left, right):
    return jnp.einsum(form, left, right, preferred_element_type=jnp.float32)


def local(k_feature, v_feature, q_feature, spectrum, skip_gain, out_weight):
    channels, tokens = k_feature.shape
    block_order = spectrum.shape[3]
    length_all = block_order * block_order
    ctx_count = lax.axis_size("ctx")
    tp_count = lax.axis_size("tp")
    slab_width = block_order // ctx_count
    rows_here = tokens // block_order
    ctx_index = lax.axis_index("ctx")
    product = (k_feature.astype(jnp.float32) * v_feature.astype(jnp.float32)).astype(jnp.bfloat16)
    cosine_full, sine_full = fourier_tables(block_order)
    cosine_half = cosine_full[: block_order // 2]
    sine_half = sine_full[: block_order // 2]
    positions = jnp.arange(block_order, dtype=jnp.int32)
    local_ticks = ctx_index * slab_width + jnp.arange(slab_width, dtype=jnp.int32)
    grid_rows = lax.all_to_all(
        product.reshape(channels, rows_here, block_order),
        "ctx",
        split_axis=2,
        concat_axis=1,
        tiled=True,
    )
    first_real = contract("cij,ia->caj", grid_rows, cosine_half)
    first_imag = -contract("cij,ia->caj", grid_rows, sine_half)
    twist_cosine, twist_sine = twist_tables(positions, local_ticks, length_all)
    spread_real = (first_real * twist_cosine + first_imag * twist_sine).astype(jnp.bfloat16)
    spread_imag = (first_imag * twist_cosine - first_real * twist_sine).astype(jnp.bfloat16)
    block_real, block_imag = (
        lax.all_to_all(spread_real, "ctx", split_axis=1, concat_axis=2, tiled=True),
        lax.all_to_all(spread_imag, "ctx", split_axis=1, concat_axis=2, tiled=True),
    )
    freq_real = contract("caj,jb->cab", block_real, cosine_full) + contract(
        "caj,jb->cab", block_imag, sine_full
    )
    freq_imag = contract("caj,jb->cab", block_imag, cosine_full) - contract(
        "caj,jb->cab", block_real, sine_full
    )
    resp_real = spectrum[0].astype(jnp.float32)
    resp_imag = spectrum[1].astype(jnp.float32)
    shaped_real = (freq_real * resp_real - freq_imag * resp_imag).astype(jnp.bfloat16)
    shaped_imag = (freq_real * resp_imag + freq_imag * resp_real).astype(jnp.bfloat16)
    inner_real = contract("cab,bj->caj", shaped_real, cosine_full) - contract(
        "cab,bj->caj", shaped_imag, sine_full
    )
    inner_imag = contract("cab,bj->caj", shaped_imag, cosine_full) + contract(
        "cab,bj->caj", shaped_real, sine_full
    )
    twist_cosine, twist_sine = twist_tables(local_ticks, positions, length_all)
    back_real = (inner_real * twist_cosine - inner_imag * twist_sine).astype(jnp.bfloat16)
    back_imag = (inner_imag * twist_cosine + inner_real * twist_sine).astype(jnp.bfloat16)
    summed = contract(
        "ia,caj->cij",
        cosine_half,
        lax.all_to_all(back_real, "ctx", split_axis=2, concat_axis=1, tiled=True),
    ) - contract(
        "ia,caj->cij",
        sine_half,
        lax.all_to_all(back_imag, "ctx", split_axis=2, concat_axis=1, tiled=True),
    )
    spatial = (summed * (1.0 / length_all)).astype(jnp.bfloat16)
    convolved = lax.all_to_all(spatial, "ctx", split_axis=1, concat_axis=2, tiled=True).reshape(
        channels, tokens
    )
    gated_rows = (
        q_feature.astype(jnp.float32)
        * (convolved.astype(jnp.float32) + skip_gain[:, None] * product.astype(jnp.float32))
    ).astype(jnp.bfloat16)
    gated_all = lax.all_gather(gated_rows, "tp", axis=0, tiled=True)
    outs_here = out_weight.shape[1] // tp_count
    tp_index = lax.axis_index("tp")
    my_weight = lax.dynamic_slice_in_dim(out_weight, tp_index * outs_here, outs_here, 1)
    return jnp.dot(my_weight.T, gated_all, preferred_element_type=jnp.float32).astype(jnp.bfloat16)


def solution(mesh):
    placed = (
        P("tp", "ctx"),
        P("tp", "ctx"),
        P("tp", "ctx"),
        P(None, "tp", "ctx", None),
        P("tp"),
        P(),
    )
    return jax.shard_map(
        local, mesh=mesh, in_specs=placed, out_specs=P("tp", "ctx"), check_vma=False
    )
```

profile of v0, /device:TPU:6, one launch (start us, length us, event | category | flops | bytes accessed | tf_op | source)
XLA Modules:
  0.0 239.1 jit_solution(14384974882966536340)
XLA Ops:
  0.0 0.9 multiply_convert_fusion.1
  1.6 0.7 copy.41
  2.2 1.8 reshape.247
  4.0 21.2 %all-to-all-start = ((bf16[64,2,256]{2,1,0:T(2,128)(2,1)}), bf16[64,2,256]{2,1,0:T(2,128)(2,1)S(1)}, u32[]{:S(2)}, u32[]{:S(2)}) async-start(bf16[64,2,256]{2,1,0:T(2,128)(2,1)} %reshape.247), calls=%async_computation | async-start | bytes 131072 | tf_op jit(solution)/shard_map/all_to_all | solution.py:50
  25.8 0.6 fusion.72
  26.4 2.7 %add_convert_fusion = (bf16[32,32,1024]{2,1,0:T(8,128)(2,1)}, bf16[32,32,1024]{2,1,0:T(8,128)(2,1)S(1)}) fusion(f32[32,1024]{1,0:T(8,128)S(1)} %get-tuple-element.23, f32[32,1024]{1,0:T(8,128)S(1)} %get-tuple-element.22, f32[32,1024]{1,0:T(8,128)S(1)} %get-tuple-element.24, f32[32,1024]{1,0:T(8,128)S(1)} %get-tuple-element.21), kind=kLoop, calls=%fused_computation.1 | loop fusion | flops 8388608 | bytes 4718592 | tf_op jit(solution)/shard_map/convert_element_type | solution.py:22
  29.4 10.9 %all-to-all-done = bf16[64,2,256]{2,1,0:T(2,128)(2,1)S(1)} async-done(((bf16[64,2,256]{2,1,0:T(2,128)(2,1)}), bf16[64,2,256]{2,1,0:T(2,128)(2,1)S(1)}, u32[]{:S(2)}, u32[]{:S(2)}) %all-to-all-start) | async-done | bytes 65568 | tf_op jit(solution)/shard_map/all_to_all | solution.py:50
  40.3 1.2 reshape.248
  41.5 1.4 copy.63
  42.9 1.2 copy.44
  44.1 1.5 fusion.35
  46.0 0.7 copy.46
  46.7 1.8 reshape.249
  48.6 6.7 %all-to-all-start.1 = ((bf16[64,2,512]{2,1,0:T(2,128)(2,1)}), bf16[64,2,512]{2,1,0:T(2,128)(2,1)S(1)}, u32[]{:S(2)}, u32[]{:S(2)}) async-start(bf16[64,2,512]{2,1,0:T(2,128)(2,1)} %reshape.249), calls=%async_computation.1 | async-start | bytes 262144 | tf_op jit(solution)/shard_map/all_to_all | solution.py:63
  55.2 0.7 copy.49
  55.9 1.8 reshape.251
  57.7 13.0 %all-to-all-done.1 = bf16[64,2,512]{2,1,0:T(2,128)(2,1)S(1)} async-done(((bf16[64,2,512]{2,1,0:T(2,128)(2,1)}), bf16[64,2,512]{2,1,0:T(2,128)(2,1)S(1)}, u32[]{:S(2)}, u32[]{:S(2)}) %all-to-all-start.1) | async-done | bytes 131104 | tf_op jit(solution)/shard_map/all_to_all | solution.py:63
  70.8 7.0 %all-to-all-start.2 = ((bf16[64,2,512]{2,1,0:T(2,128)(2,1)}), bf16[64,2,512]{2,1,0:T(2,128)(2,1)}, u32[]{:S(2)}, u32[]{:S(2)}) async-start(bf16[64,2,512]{2,1,0:T(2,128)(2,1)} %reshape.251), calls=%async_computation.2 | async-start | bytes 262144 | tf_op jit(solution)/shard_map/all_to_all | solution.py:64
  77.8 1.0 fusion.76
  78.8 0.7 reshape.250
  79.5 1.7 copy.81
  81.2 3.0 %all_to_all.79 = bf16[4,16,1024]{2,1,0:T(8,128)(2,1)S(1)} reshape(bf16[4,16,64,16]{3,2,1,0:T(8,128)(2,1)} %bitcast.151) | data formatting | bytes 262144 | tf_op jit(solution)/shard_map/all_to_all | solution.py:63
  84.1 2.1 fusion.4
  86.2 8.3 %all-to-all-done.2 = bf16[64,2,512]{2,1,0:T(2,128)(2,1)} async-done(((bf16[64,2,512]{2,1,0:T(2,128)(2,1)}), bf16[64,2,512]{2,1,0:T(2,128)(2,1)}, u32[]{:S(2)}, u32[]{:S(2)}) %all-to-all-start.2) | async-done | bytes 131104 | tf_op jit(solution)/shard_map/all_to_all | solution.py:64
  94.5 2.6 %reshape.252 = bf16[1024,4,16]{2,1,0:T(4,128)(2,1)S(1)} reshape(bf16[64,2,512]{2,1,0:T(2,128)(2,1)} %all-to-all-done.2) | data formatting | bytes 262144
  97.1 1.7 copy.80
  98.8 3.0 %all_to_all.83 = bf16[4,16,1024]{2,1,0:T(8,128)(2,1)S(1)} reshape(bf16[4,16,64,16]{3,2,1,0:T(8,128)(2,1)} %bitcast.153) | data formatting | bytes 262144 | tf_op jit(solution)/shard_map/all_to_all | solution.py:64
  101.8 2.1 fusion.6
  105.0 1.0 copy-done.1
  108.0 0.7 copy.52
  108.7 1.8 reshape.253
  110.5 9.4 %all-to-all-start.3 = ((bf16[64,2,512]{2,1,0:T(2,128)(2,1)}), bf16[64,2,512]{2,1,0:T(2,128)(2,1)S(1)}, u32[]{:S(2)}, u32[]{:S(2)}) async-start(bf16[64,2,512]{2,1,0:T(2,128)(2,1)} %reshape.253), calls=%async_computation.3 | async-start | bytes 262144 | tf_op jit(solution)/shard_map/all_to_all | solution.py:88
  120.0 0.7 copy.55
  120.7 1.8 reshape.255
  122.4 14.2 %all-to-all-done.3 = bf16[64,2,512]{2,1,0:T(2,128)(2,1)S(1)} async-done(((bf16[64,2,512]{2,1,0:T(2,128)(2,1)}), bf16[64,2,512]{2,1,0:T(2,128)(2,1)S(1)}, u32[]{:S(2)}, u32[]{:S(2)}) %all-to-all-start.3) | async-done | bytes 131104 | tf_op jit(solution)/shard_map/all_to_all | solution.py:88
  136.7 5.7 %all-to-all-start.4 = ((bf16[64,2,512]{2,1,0:T(2,128)(2,1)}), bf16[64,2,512]{2,1,0:T(2,128)(2,1)S(1)}, u32[]{:S(2)}, u32[]{:S(2)}) async-start(bf16[64,2,512]{2,1,0:T(2,128)(2,1)} %reshape.255), calls=%async_computation.4 | async-start | bytes 262144 | tf_op jit(solution)/shard_map/all_to_all | solution.py:92
  142.3 0.7 reshape.254
  143.1 1.7 copy.79
  144.7 3.0 %all_to_all.87 = bf16[4,1024,16]{1,2,0:T(8,128)(2,1)S(1)} reshape(bf16[4,64,16,16]{2,1,3,0:T(8,128)(2,1)} %bitcast.155) | data formatting | bytes 262144 | tf_op jit(solution)/shard_map/all_to_all | solution.py:88
  148.1 10.9 %all-to-all-done.4 = bf16[64,2,512]{2,1,0:T(2,128)(2,1)S(1)} async-done(((bf16[64,2,512]{2,1,0:T(2,128)(2,1)}), bf16[64,2,512]{2,1,0:T(2,128)(2,1)S(1)}, u32[]{:S(2)}, u32[]{:S(2)}) %all-to-all-start.4) | async-done | bytes 131104 | tf_op jit(solution)/shard_map/all_to_all | solution.py:92
  159.1 0.7 reshape.256
  159.8 1.7 copy.78
  161.4 3.0 %all_to_all.91 = bf16[4,1024,16]{1,2,0:T(8,128)(2,1)S(1)} reshape(bf16[4,64,16,16]{2,1,3,0:T(8,128)(2,1)} %bitcast.157) | data formatting | bytes 262144 | tf_op jit(solution)/shard_map/all_to_all | solution.py:92
  165.2 1.1 reshape.257
  166.3 6.7 %all-to-all-start.5 = ((bf16[64,2,256]{2,1,0:T(2,128)(2,1)}), bf16[64,2,256]{2,1,0:T(2,128)(2,1)S(1)}, u32[]{:S(2)}, u32[]{:S(2)}) async-start(bf16[64,2,256]{2,1,0:T(2,128)(2,1)} %reshape.257), calls=%async_computation.5 | async-start | bytes 131072 | tf_op jit(solution)/shard_map/all_to_all | solution.py:95
  173.0 15.5 %all-to-all-done.5 = bf16[64,2,256]{2,1,0:T(2,128)(2,1)S(1)} async-done(((bf16[64,2,256]{2,1,0:T(2,128)(2,1)}), bf16[64,2,256]{2,1,0:T(2,128)(2,1)S(1)}, u32[]{:S(2)}, u32[]{:S(2)}) %all-to-all-start.5) | async-done | bytes 65568 | tf_op jit(solution)/shard_map/all_to_all | solution.py:95
  190.3 47.7 %all-gather = bf16[8,4,8192]{2,1,0:T(4,128)(2,1)S(1)} all-gather(bf16[1,4,8192]{2,1,0:T(4,128)(2,1)S(1)} %fusion.64), channel_id=1, replica_groups=mesh['ctx'=64,'tp'=8] {'tp'}, dimensions={0}, use_global_device_ids=true | all-gather | bytes 589824 | tf_op jit(solution)/shard_map/all_gather | solution.py:102
  238.1 1.0 convolution_convert_fusion
  (42 shorter events, 8.0 us)
Async XLA Ops:
  0.0 238.1 %copy-start = (bf16[32,64]{1,0:T(8,128)(2,1)S(1)}, bf16[32,64]{1,0:T(8,128)(2,1)}, u32[]{:S(2)}) copy-start(bf16[32,64]{1,0:T(8,128)(2,1)} %param.11) | copy-start | bytes 12292
  0.9 0.6 copy-start.3
  4.0 36.3 %all-to-all-start = ((bf16[64,2,256]{2,1,0:T(2,128)(2,1)}), bf16[64,2,256]{2,1,0:T(2,128)(2,1)S(1)}, u32[]{:S(2)}, u32[]{:S(2)}) async-start(bf16[64,2,256]{2,1,0:T(2,128)(2,1)} %reshape.247), calls=%async_computation | async-start | bytes 131072 | tf_op jit(solution)/shard_map/all_to_all | solution.py:50
  48.6 22.2 %all-to-all-start.1 = ((bf16[64,2,512]{2,1,0:T(2,128)(2,1)}), bf16[64,2,512]{2,1,0:T(2,128)(2,1)S(1)}, u32[]{:S(2)}, u32[]{:S(2)}) async-start(bf16[64,2,512]{2,1,0:T(2,128)(2,1)} %reshape.249), calls=%async_computation.1 | async-start | bytes 262144 | tf_op jit(solution)/shard_map/all_to_all | solution.py:63
  70.8 23.7 %all-to-all-start.2 = ((bf16[64,2,512]{2,1,0:T(2,128)(2,1)}), bf16[64,2,512]{2,1,0:T(2,128)(2,1)}, u32[]{:S(2)}, u32[]{:S(2)}) async-start(bf16[64,2,512]{2,1,0:T(2,128)(2,1)} %reshape.251), calls=%async_computation.2 | async-start | bytes 262144 | tf_op jit(solution)/shard_map/all_to_all | solution.py:64
  101.7 2.6 %copy-start.7 = (bf16[2,4,16,1024]{3,2,1,0:T(8,128)(2,1)S(1)}, bf16[2,4,16,1024]{3,2,1,0:T(8,128)(2,1)}, u32[]{:S(2)}) copy-start(bf16[2,4,16,1024]{3,2,1,0:T(8,128)(2,1)} %param.9) | copy-start | bytes 786436
  104.4 1.6 copy-start.1
  106.5 1.0 copy-start.5
  106.5 1.0 copy-start.6
  110.5 26.1 %all-to-all-start.3 = ((bf16[64,2,512]{2,1,0:T(2,128)(2,1)}), bf16[64,2,512]{2,1,0:T(2,128)(2,1)S(1)}, u32[]{:S(2)}, u32[]{:S(2)}) async-start(bf16[64,2,512]{2,1,0:T(2,128)(2,1)} %reshape.253), calls=%async_computation.3 | async-start | bytes 262144 | tf_op jit(solution)/shard_map/all_to_all | solution.py:88
  136.7 22.4 %all-to-all-start.4 = ((bf16[64,2,512]{2,1,0:T(2,128)(2,1)}), bf16[64,2,512]{2,1,0:T(2,128)(2,1)S(1)}, u32[]{:S(2)}, u32[]{:S(2)}) async-start(bf16[64,2,512]{2,1,0:T(2,128)(2,1)} %reshape.255), calls=%async_computation.4 | async-start | bytes 262144 | tf_op jit(solution)/shard_map/all_to_all | solution.py:92
  148.1 16.3 %copy-start.2 = (bf16[32,32,1024]{2,1,0:T(8,128)(2,1)S(1)}, bf16[32,32,1024]{2,1,0:T(8,128)(2,1)}, u32[]{:S(2)}) copy-start(bf16[32,32,1024]{2,1,0:T(8,128)(2,1)} %get-tuple-element.15) | copy-start | bytes 6291460
  166.3 22.2 %all-to-all-start.5 = ((bf16[64,2,256]{2,1,0:T(2,128)(2,1)}), bf16[64,2,256]{2,1,0:T(2,128)(2,1)S(1)}, u32[]{:S(2)}, u32[]{:S(2)}) async-start(bf16[64,2,256]{2,1,0:T(2,128)(2,1)} %reshape.257), calls=%async_computation.5 | async-start | bytes 131072 | tf_op jit(solution)/shard_map/all_to_all | solution.py:95
  189.1 1.0 copy-start.4
  189.1 1.0 copy-start.8
  189.1 1.0 copy-start.9
where the time goes:
time: 241 us; the launch traced here: 239 us
  waiting for transfers between devices  72.9 us (30%)
  starting transfers between devices  56.7 us (24%)
  blocking collectives  47.7 us (20%)
  local copies, waits for them, and re-layouts  44.2 us (18%)
  matrix products  10.9 us (5%)
  other arithmetic  6.24 us (3%)
    all_gather x1, blocking collectives, local(): gated_all = lax.all_gather(gated_rows, 'tp', axis=0, tiled=True)  47.7 us
    all_to_all x1, starting transfers between devices, local(): lax.all_to_all(product.reshape(channels, rows_here, block_order), 'ctx',...  21.2 us
    unnamed x34, local copies, waits for them, and re-layouts  18.2 us
    all_to_all x1, waiting for transfers between devices, local(): lax.all_to_all(spatial, 'ctx', split_axis=1, concat_axis=2, tiled=True)  15.5 us
    all_to_all x1, waiting for transfers between devices, local(): lax.all_to_all(back_real, 'ctx', split_axis=2, concat_axis=1, tiled=True)  14.2 us
    all_to_all x1, waiting for transfers between devices, local(): lax.all_to_all(spread_real, 'ctx', split_axis=1, concat_axis=2, tiled=True)  13 us
    all_to_all x1, waiting for transfers between devices, local(): lax.all_to_all(product.reshape(channels, rows_here, block_order), 'ctx',...  10.9 us
    all_to_all x1, waiting for transfers between devices, local(): lax.all_to_all(back_imag, 'ctx', split_axis=2, concat_axis=1, tiled=True)  10.9 us
  transfers between devices with their start and end apart: 6, of which 6 were waited for; matrix products, arithmetic and copies ran while one was open for 7% of the time, Pallas kernels for 0%

commit v1 on v0

--- a/solution.py
+++ b/solution.py
@@ -1,9 +1,77 @@
+import functools
 import math
 
 import jax
 import jax.numpy as jnp
 from jax import lax
+from jax.experimental import pallas as pl
+from jax.experimental.pallas import tpu as pltpu
 from jax.sharding import PartitionSpec as P
+
+MESH = pl.DeviceIdType.MESH
+
+
+def _exchange_kernel(axis, gather, x_ref, y_ref, land, send_sem, recv_sem, local_sem):
+    count = land.shape[0]
+    me = lax.axis_index(axis)
+    barrier = pltpu.get_barrier_semaphore()
+
+    def greet(step, carry):
+        peer = lax.rem(me + step, count)
+        pl.semaphore_signal(barrier, 1, device_id={axis: peer}, device_id_type=MESH)
+        return carry
+
+    lax.fori_loop(1, count, greet, 0)
+    pl.semaphore_wait(barrier, count - 1)
+
+    def piece(peer):
+        return x_ref if gather else x_ref.at[peer]
+
+    def outgoing(peer):
+        return pltpu.make_async_remote_copy(
+            src_ref=piece(peer), dst_ref=land.at[me], send_sem=send_sem.at[peer],
+            recv_sem=recv_sem.at[me], device_id={axis: peer}, device_id_type=MESH)
+
+    def incoming(source):
+        return pltpu.make_async_remote_copy(
+            src_ref=piece(source), dst_ref=land.at[source], send_sem=send_sem.at[source],
+            recv_sem=recv_sem.at[source], device_id={axis: source}, device_id_type=MESH)
+
+    def send(step, carry):
+        outgoing(lax.rem(me + step, count)).start()
+        return carry
+
+    lax.fori_loop(1, count, send, 0)
+    local = pltpu.make_async_copy(piece(me), land.at[me], local_sem)
+    local.start()
+
+    def finish(step, carry):
+        outgoing(lax.rem(me + step, count)).wait_send()
+        incoming(lax.rem(me + count - step, count)).wait_recv()
+        return carry
+
+    lax.fori_loop(1, count, finish, 0)
+    local.wait()
+    y_ref[...] = land[...]
+
+
+def exchange(x, axis, gather, collective):
+    count = lax.axis_size(axis)
+    chunk = x.shape if gather else x.shape[1:]
+    full = (count,) + tuple(chunk)
+    return pl.pallas_call(
+        functools.partial(_exchange_kernel, axis, gather),
+        out_shape=jax.ShapeDtypeStruct(full, x.dtype),
+        in_specs=[pl.BlockSpec(memory_space=pltpu.VMEM)],
+        out_specs=pl.BlockSpec(memory_space=pltpu.VMEM),
+        scratch_shapes=[
+            pltpu.VMEM(full, x.dtype),
+            pltpu.SemaphoreType.DMA((count,)),
+            pltpu.SemaphoreType.DMA((count,)),
+            pltpu.SemaphoreType.DMA,
+        ],
+        compiler_params=pltpu.CompilerParams(collective_id=collective, has_side_effects=True),
+    )(x)
 
 
 def fourier_tables(length_all):
@@ -40,29 +108,37 @@
     tp_count = lax.axis_size("tp")
     slab_width = block_order // ctx_count
     rows_here = tokens // block_order
+    half_rows = block_order // 2
     ctx_index = lax.axis_index("ctx")
     product = (k_feature.astype(jnp.float32) * v_feature.astype(jnp.float32)).astype(jnp.bfloat16)
     cosine_full, sine_full = fourier_tables(block_order)
-    cosine_half = cosine_full[: block_order // 2]
-    sine_half = sine_full[: block_order // 2]
+    cosine_half = cosine_full[:half_rows]
+    sine_half = sine_full[:half_rows]
     positions = jnp.arange(block_order, dtype=jnp.int32)
     local_ticks = ctx_index * slab_width + jnp.arange(slab_width, dtype=jnp.int32)
-    grid_rows = lax.all_to_all(
-        product.reshape(channels, rows_here, block_order),
-        "ctx",
-        split_axis=2,
-        concat_axis=1,
-        tiled=True,
+
+    outgoing = product.reshape(channels, rows_here, ctx_count, slab_width).transpose(2, 0, 1, 3)
+    arrived = exchange(outgoing.reshape(ctx_count, channels, -1), "ctx", False, 0)
+    grid_rows = (
+        arrived.reshape(ctx_count, channels, rows_here, slab_width)
+        .transpose(1, 0, 2, 3)
+        .reshape(channels, half_rows, slab_width)
     )
     first_real = contract("cij,ia->caj", grid_rows, cosine_half)
     first_imag = -contract("cij,ia->caj", grid_rows, sine_half)
     twist_cosine, twist_sine = twist_tables(positions, local_ticks, length_all)
     spread_real = (first_real * twist_cosine + first_imag * twist_sine).astype(jnp.bfloat16)
     spread_imag = (first_imag * twist_cosine - first_real * twist_sine).astype(jnp.bfloat16)
-    block_real, block_imag = (
-        lax.all_to_all(spread_real, "ctx", split_axis=1, concat_axis=2, tiled=True),
-        lax.all_to_all(spread_imag, "ctx", split_axis=1, concat_axis=2, tiled=True),
-    )
+
+    spread = jnp.stack([spread_real, spread_imag])
+    outgoing = spread.reshape(2, channels, ctx_count, slab_width, slab_width).transpose(2, 0, 1, 3, 4)
+    arrived = exchange(outgoing.reshape(ctx_count, -1, 128), "ctx", False, 1)
+    block = (
+        arrived.reshape(ctx_count, 2, channels, slab_width, slab_width)
+        .transpose(1, 2, 3, 0, 4)
+        .reshape(2, channels, slab_width, block_order)
+    )
+    block_real, block_imag = block[0], block[1]
     freq_real = contract("caj,jb->cab", block_real, cosine_full) + contract(
         "caj,jb->cab", block_imag, sine_full
     )
@@ -82,24 +158,32 @@
     twist_cosine, twist_sine = twist_tables(local_ticks, positions, length_all)
     back_real = (inner_real * twist_cosine - inner_imag * twist_sine).astype(jnp.bfloat16)
     back_imag = (inner_imag * twist_cosine + inner_real * twist_sine).astype(jnp.bfloat16)
-    summed = contract(
-        "ia,caj->cij",
-        cosine_half,
-        lax.all_to_all(back_real, "ctx", split_axis=2, concat_axis=1, tiled=True),
-    ) - contract(
-        "ia,caj->cij",
-        sine_half,
-        lax.all_to_all(back_imag, "ctx", split_axis=2, concat_axis=1, tiled=True),
+
+    back = jnp.stack([back_real, back_imag])
+    outgoing = back.reshape(2, channels, slab_width, ctx_count, slab_width).transpose(3, 0, 1, 2, 4)
+    arrived = exchange(outgoing.reshape(ctx_count, -1, 128), "ctx", False, 2)
+    columns = (
+        arrived.reshape(ctx_count, 2, channels, slab_width, slab_width)
+        .transpose(1, 2, 0, 3, 4)
+        .reshape(2, channels, block_order, slab_width)
+    )
+    summed = contract("ia,caj->cij", cosine_half, columns[0]) - contract(
+        "ia,caj->cij", sine_half, columns[1]
     )
     spatial = (summed * (1.0 / length_all)).astype(jnp.bfloat16)
-    convolved = lax.all_to_all(spatial, "ctx", split_axis=1, concat_axis=2, tiled=True).reshape(
-        channels, tokens
+
+    outgoing = spatial.reshape(channels, ctx_count, rows_here, slab_width).transpose(1, 0, 2, 3)
+    arrived = exchange(outgoing.reshape(ctx_count, channels, -1), "ctx", False, 3)
+    convolved = (
+        arrived.reshape(ctx_count, channels, rows_here, slab_width)
+        .transpose(1, 2, 0, 3)
+        .reshape(channels, tokens)
     )
     gated_rows = (
         q_feature.astype(jnp.float32)
         * (convolved.astype(jnp.float32) + skip_gain[:, None] * product.astype(jnp.float32))
     ).astype(jnp.bfloat16)
-    gated_all = lax.all_gather(gated_rows, "tp", axis=0, tiled=True)
+    gated_all = exchange(gated_rows, "tp", True, 4).reshape(tp_count * channels, tokens)
     outs_here = out_weight.shape[1] // tp_count
     tp_index = lax.axis_index("tp")
     my_weight = lax.dynamic_slice_in_dim(out_weight, tp_index * outs_here, outs_here, 1)

time: 241 us -> 189 us (0.78)
  the two profiles are of different devices: /device:TPU:6 before, /device:TPU:64 now
where the time goes in v1:
time: 189 us; the launch traced here: 188 us
  Pallas kernels  138 us (73%)
  local copies, waits for them, and re-layouts  30.5 us (16%)
  matrix products  11.7 us (6%)
  other arithmetic  7.48 us (4%)
    pallas_call x5, Pallas kernels, exchange(): pl.pallas_call(functools.partial(_exchange_kernel, axis, gather), out_sha...  138 us
    dot_general x10, matrix products, contract(): return jnp.einsum(form, left, right, preferred_element_type=jnp.float32)  8.93 us

profile of v1, /device:TPU:64, one launch (start us, length us, event | category | flops | bytes accessed | tf_op | source)
XLA Modules:
  0.0 187.8 jit_solution(16124504970289620801)
XLA Ops:
  0.0 0.6 fusion.71
  0.6 0.5 fusion.68
  1.2 2.7 %add_convert_fusion = (bf16[32,32,1024]{2,1,0:T(8,128)(2,1)}, bf16[32,32,1024]{2,1,0:T(8,128)(2,1)S(1)}) fusion(f32[32,1024]{1,0:T(8,128)S(1)} %get-tuple-element.27, f32[32,1024]{1,0:T(8,128)S(1)} %get-tuple-element.26, f32[32,1024]{1,0:T(8,128)S(1)} %get-tuple-element.28, f32[32,1024]{1,0:T(8,128)S(1)} %get-tuple-element.25), kind=kLoop, calls=%fused_computation.1 | loop fusion | flops 8388608 | bytes 4718592 | tf_op jit(solution)/shard_map/convert_element_type | solution.py:90
  4.5 0.7 copy.64.x_ref
  5.2 25.2 %shard_map.64 = bf16[64,4,128]{2,1,0:T(4,128)(2,1)} custom-call(bf16[64,4,128]{2,1,0:T(4,128)(2,1)} %copy.64.x_ref), custom_call_target="tpu_custom_call" | custom-call | tf_op jit(solution)/shard_map/pallas_call | solution.py:62
  30.4 1.0 copy.65
  32.3 1.5 fusion.35
  34.2 0.8 stack.18
  35.5 0.8 stack.19
  36.3 1.1 copy.70
  37.5 1.1 pad_maximum_fusion
  38.5 1.0 copy.71.x_ref
  39.5 25.6 %shard_map.65 = bf16[64,16,128]{2,1,0:T(8,128)(2,1)} custom-call(bf16[64,16,128]{2,1,0:T(8,128)(2,1)} %copy.71.x_ref), custom_call_target="tpu_custom_call" | custom-call | tf_op jit(solution)/shard_map/pallas_call | solution.py:62
  65.2 1.3 copy.72
  66.4 0.7 fusion.81
  67.1 0.5 copy.74
  67.6 1.8 squeeze.15
  69.4 2.8 %fusion.6 = f32[4,16,1024]{2,1,0:T(8,128)} fusion(bf16[4,16,1024]{2,1,0:T(8,128)(2,1)S(1)} %squeeze.15, bf16[1024,1024]{1,0:T(8,128)(2,1)} %bitcast.122), kind=kOutput, calls=%fused_computation.9 | convolution fusion | flops 134217728 | bytes 2490368 | tf_op jit(solution)/shard_map/caj,jb->cab/dot_general | solution.py:100
  72.2 1.4 copy.73
  73.6 1.8 squeeze.14
  75.4 1.6 fusion.16
  77.1 0.5 fusion.4
  77.6 0.6 fusion.41
  78.1 0.5 fusion
  78.6 0.5 fusion.2
  79.1 0.5 fusion.22
  79.9 0.5 subtract_convert_fusion.1
  80.5 0.8 stack.21
  81.7 0.8 stack.22
  82.6 1.1 copy.76
  83.6 1.1 pad_maximum_fusion.1
  84.7 1.0 copy.77.x_ref
  85.7 32.0 %shard_map.66 = bf16[64,16,128]{2,1,0:T(8,128)(2,1)} custom-call(bf16[64,16,128]{2,1,0:T(8,128)(2,1)} %copy.77.x_ref), custom_call_target="tpu_custom_call" | custom-call | tf_op jit(solution)/shard_map/pallas_call | solution.py:62
  117.7 1.3 copy.78
  118.9 0.7 fusion.80
  119.7 1.4 copy.79
  121.1 1.8 squeeze.16
  122.9 1.1 fusion.32
  124.0 0.5 copy.80
  124.5 1.8 squeeze.17
  127.4 0.7 copy.83.x_ref
  128.2 25.5 %shard_map.67 = bf16[64,4,128]{2,1,0:T(4,128)(2,1)} custom-call(bf16[64,4,128]{2,1,0:T(4,128)(2,1)} %copy.83.x_ref), custom_call_target="tpu_custom_call" | custom-call | tf_op jit(solution)/shard_map/pallas_call | solution.py:62
  153.6 1.0 copy.84
  155.0 0.6 reshape.295
  155.6 0.7 multiply_convert_fusion.x_ref
  156.3 29.3 %shard_map.68 = bf16[8,4,8192]{2,1,0:T(4,128)(2,1)} custom-call(bf16[4,8192]{1,0:T(4,128)(2,1)} %multiply_convert_fusion.x_ref), custom_call_target="tpu_custom_call" | custom-call | tf_op jit(solution)/shard_map/pallas_call | solution.py:62
  185.6 1.2 reshape.292
  186.8 1.0 convolution_convert_fusion
  (39 shorter events, 4.6 us)
Async XLA Ops:
  0.0 186.8 %copy-start = (bf16[32,64]{1,0:T(8,128)(2,1)S(1)}, bf16[32,64]{1,0:T(8,128)(2,1)}, u32[]{:S(2)}) copy-start(bf16[32,64]{1,0:T(8,128)(2,1)} %param.11) | copy-start | bytes 12292
  1.1 2.7 %copy-start.7 = (bf16[4,8192]{1,0:T(4,128)(2,1)S(1)}, bf16[4,8192]{1,0:T(4,128)(2,1)}, u32[]{:S(2)}) copy-start(bf16[4,8192]{1,0:T(4,128)(2,1)} %param.7) | copy-start | bytes 196612
  1.1 2.7 %copy-start.8 = (bf16[4,8192]{1,0:T(4,128)(2,1)S(1)}, bf16[4,8192]{1,0:T(4,128)(2,1)}, u32[]{:S(2)}) copy-start(bf16[4,8192]{1,0:T(4,128)(2,1)} %param.6) | copy-start | bytes 196612
  3.9 28.4 %copy-start.3 = (bf16[4,8192]{1,0:T(4,128)(2,1)}, bf16[4,8192]{1,0:T(4,128)(2,1)S(1)}, u32[]{:S(2)}) copy-start(bf16[4,8192]{1,0:T(4,128)(2,1)S(1)} %multiply_convert_fusion.1) | copy-start | bytes 196612
  75.4 1.7 copy-start.1
  75.4 2.2 %copy-start.6 = (bf16[2,4,16,1024]{3,2,1,0:T(8,128)(2,1)S(1)}, bf16[2,4,16,1024]{3,2,1,0:T(8,128)(2,1)}, u32[]{:S(2)}) copy-start(bf16[2,4,16,1024]{3,2,1,0:T(8,128)(2,1)} %param.9) | copy-start | bytes 786436
  124.0 2.3 %copy-start.2 = (bf16[32,32,1024]{2,1,0:T(8,128)(2,1)S(1)}, bf16[32,32,1024]{2,1,0:T(8,128)(2,1)}, u32[]{:S(2)}) copy-start(bf16[32,32,1024]{2,1,0:T(8,128)(2,1)} %get-tuple-element.19) | copy-start | bytes 6291460
  124.0 2.3 %copy-start.5 = (f32[4,16,512]{2,1,0:T(8,128)S(1)}, f32[4,16,512]{2,1,0:T(8,128)}, u32[]{:S(2)}) copy-start(f32[4,16,512]{2,1,0:T(8,128)} %fusion.32) | copy-start | bytes 393220
  126.8 28.8 %copy-start.4 = (bf16[4,8192]{1,0:T(4,128)(2,1)S(1)}, bf16[4,8192]{1,0:T(4,128)(2,1)}, u32[]{:S(2)}) copy-start(bf16[4,8192]{1,0:T(4,128)(2,1)} %copy-done.3) | copy-start | bytes 196612
  126.8 28.8 %copy-start.9 = (bf16[4,8192]{1,0:T(4,128)(2,1)S(1)}, bf16[4,8192]{1,0:T(4,128)(2,1)}, u32[]{:S(2)}) copy-start(bf16[4,8192]{1,0:T(4,128)(2,1)} %param.8) | copy-start | bytes 196612
  126.8 28.8 %copy-start.10 = (f32[4]{0:T(128)S(1)}, f32[4]{0:T(128)}, u32[]{:S(2)}) copy-start(f32[4]{0:T(128)} %param.10) | copy-start | bytes 52

commit v2 on v1

--- a/solution.py
+++ b/solution.py
@@ -106,77 +106,76 @@
     length_all = block_order * block_order
     ctx_count = lax.axis_size("ctx")
     tp_count = lax.axis_size("tp")
-    slab_width = block_order // ctx_count
+    slab = block_order // ctx_count
     rows_here = tokens // block_order
     half_rows = block_order // 2
+    lanes = channels * slab
     ctx_index = lax.axis_index("ctx")
     product = (k_feature.astype(jnp.float32) * v_feature.astype(jnp.float32)).astype(jnp.bfloat16)
     cosine_full, sine_full = fourier_tables(block_order)
-    cosine_half = cosine_full[:half_rows]
-    sine_half = sine_full[:half_rows]
+    both_full = jnp.stack([cosine_full, sine_full])
+    both_half = both_full[:, :half_rows]
     positions = jnp.arange(block_order, dtype=jnp.int32)
-    local_ticks = ctx_index * slab_width + jnp.arange(slab_width, dtype=jnp.int32)
-
-    outgoing = product.reshape(channels, rows_here, ctx_count, slab_width).transpose(2, 0, 1, 3)
-    arrived = exchange(outgoing.reshape(ctx_count, channels, -1), "ctx", False, 0)
-    grid_rows = (
-        arrived.reshape(ctx_count, channels, rows_here, slab_width)
-        .transpose(1, 0, 2, 3)
-        .reshape(channels, half_rows, slab_width)
-    )
-    first_real = contract("cij,ia->caj", grid_rows, cosine_half)
-    first_imag = -contract("cij,ia->caj", grid_rows, sine_half)
+    local_ticks = ctx_index * slab + jnp.arange(slab, dtype=jnp.int32)
     twist_cosine, twist_sine = twist_tables(positions, local_ticks, length_all)
-    spread_real = (first_real * twist_cosine + first_imag * twist_sine).astype(jnp.bfloat16)
-    spread_imag = (first_imag * twist_cosine - first_real * twist_sine).astype(jnp.bfloat16)
-
-    spread = jnp.stack([spread_real, spread_imag])
-    outgoing = spread.reshape(2, channels, ctx_count, slab_width, slab_width).transpose(2, 0, 1, 3, 4)
-    arrived = exchange(outgoing.reshape(ctx_count, -1, 128), "ctx", False, 1)
+    twist_cosine = jnp.tile(twist_cosine, (1, channels))
+    twist_sine = jnp.tile(twist_sine, (1, channels))
+
+    outgoing = product.reshape(channels, rows_here, ctx_count, slab).transpose(2, 1, 0, 3)
+    arrived = exchange(outgoing.reshape(ctx_count, -1, 128), "ctx", False, 0)
+    grid_rows = arrived.reshape(half_rows, lanes)
+    first = contract("sia,ik->sak", both_half, grid_rows)
+    spread = jnp.concatenate(
+        [
+            first[0] * twist_cosine - first[1] * twist_sine,
+            -first[1] * twist_cosine - first[0] * twist_sine,
+        ],
+        axis=1,
+    ).astype(jnp.bfloat16)
+
+    arrived = exchange(spread.reshape(ctx_count, slab, 2 * lanes), "ctx", False, 1)
     block = (
-        arrived.reshape(ctx_count, 2, channels, slab_width, slab_width)
-        .transpose(1, 2, 3, 0, 4)
-        .reshape(2, channels, slab_width, block_order)
-    )
-    block_real, block_imag = block[0], block[1]
-    freq_real = contract("caj,jb->cab", block_real, cosine_full) + contract(
-        "caj,jb->cab", block_imag, sine_full
-    )
-    freq_imag = contract("caj,jb->cab", block_imag, cosine_full) - contract(
-        "caj,jb->cab", block_real, sine_full
-    )
-    resp_real = spectrum[0].astype(jnp.float32)
-    resp_imag = spectrum[1].astype(jnp.float32)
-    shaped_real = (freq_real * resp_real - freq_imag * resp_imag).astype(jnp.bfloat16)
-    shaped_imag = (freq_real * resp_imag + freq_imag * resp_real).astype(jnp.bfloat16)
-    inner_real = contract("cab,bj->caj", shaped_real, cosine_full) - contract(
-        "cab,bj->caj", shaped_imag, sine_full
-    )
-    inner_imag = contract("cab,bj->caj", shaped_imag, cosine_full) + contract(
-        "cab,bj->caj", shaped_real, sine_full
-    )
-    twist_cosine, twist_sine = twist_tables(local_ticks, positions, length_all)
-    back_real = (inner_real * twist_cosine - inner_imag * twist_sine).astype(jnp.bfloat16)
-    back_imag = (inner_imag * twist_cosine + inner_real * twist_sine).astype(jnp.bfloat16)
-
-    back = jnp.stack([back_real, back_imag])
-    outgoing = back.reshape(2, channels, slab_width, ctx_count, slab_width).transpose(3, 0, 1, 2, 4)
-    arrived = exchange(outgoing.reshape(ctx_count, -1, 128), "ctx", False, 2)
+        arrived.reshape(ctx_count, slab, 2, channels, slab)
+        .transpose(0, 4, 2, 3, 1)
+        .reshape(block_order, 2 * lanes)
+    )
+    freq = contract("sbj,jk->sbk", both_full, block)
+    freq_real = freq[0, :, :lanes] + freq[1, :, lanes:]
+    freq_imag = freq[0, :, lanes:] - freq[1, :, :lanes]
+    response = spectrum.reshape(2, lanes, block_order).transpose(0, 2, 1).astype(jnp.float32)
+    shaped = jnp.concatenate(
+        [
+            freq_real * response[0] - freq_imag * response[1],
+            freq_real * response[1] + freq_imag * response[0],
+        ],
+        axis=1,
+    ).astype(jnp.bfloat16)
+    inner = contract("sjb,bk->sjk", both_full, shaped)
+    inner_real = inner[0, :, :lanes] - inner[1, :, lanes:]
+    inner_imag = inner[0, :, lanes:] + inner[1, :, :lanes]
+    back = jnp.concatenate(
+        [
+            inner_real * twist_cosine - inner_imag * twist_sine,
+            inner_imag * twist_cosine + inner_real * twist_sine,
+        ],
+        axis=1,
+    ).astype(jnp.bfloat16)
+
+    arrived = exchange(back.reshape(ctx_count, slab, 2 * lanes), "ctx", False, 2)
     columns = (
-        arrived.reshape(ctx_count, 2, channels, slab_width, slab_width)
-        .transpose(1, 2, 0, 3, 4)
-        .reshape(2, channels, block_order, slab_width)
-    )
-    summed = contract("ia,caj->cij", cosine_half, columns[0]) - contract(
-        "ia,caj->cij", sine_half, columns[1]
-    )
-    spatial = (summed * (1.0 / length_all)).astype(jnp.bfloat16)
-
-    outgoing = spatial.reshape(channels, ctx_count, rows_here, slab_width).transpose(1, 0, 2, 3)
-    arrived = exchange(outgoing.reshape(ctx_count, channels, -1), "ctx", False, 3)
+        arrived.reshape(ctx_count, slab, 2, channels, slab)
+        .transpose(0, 4, 2, 3, 1)
+        .reshape(block_order, 2 * lanes)
+    )
+    summed = contract("sia,ak->sik", both_half, columns)
+    spatial = ((summed[0, :, :lanes] - summed[1, :, lanes:]) * (1.0 / length_all)).astype(
+        jnp.bfloat16
+    )
+
+    arrived = exchange(spatial.reshape(ctx_count, -1, 128), "ctx", False, 3)
     convolved = (
-        arrived.reshape(ctx_count, channels, rows_here, slab_width)
-        .transpose(1, 2, 0, 3)
+        arrived.reshape(ctx_count, rows_here, channels, slab)
+        .transpose(2, 1, 0, 3)
         .reshape(channels, tokens)
     )
     gated_rows = (

time: 189 us -> 195 us (1.032)
  other arithmetic: 7.48 us -> 12.7 us
  local copies, waits for them, and re-layouts: 30.5 us -> 35.3 us
  matrix products: 11.7 us -> 8.32 us
    reshape x6 -> x5, local copies, waits for them, and re-layouts: 4 us -> 12.1 us  [the longest x1 4.7 us: local(): block = arrived.reshape(ctx_count, slab, 2, channels, slab).transpose(0,...]
    squeeze x4 -> x0, local copies, waits for them, and re-layouts: 7.17 us -> none  [the longest x2 3.58 us: local(): block_real, block_imag = (block[0], block[1])]
    transpose x3, local copies, waits for them, and re-layouts: 0.9 us -> 4.74 us  [the longest x1 2.71 us: local(): block = arrived.reshape(ctx_count, slab, 2, channels, slab).transpose(0,...]
    another operation x8 -> x6, local copies, waits for them, and re-layouts: 6.32 us -> 3.68 us  [the longest x3 1.84 us: local(): twist_cosine = jnp.tile(twist_cosine, (1, channels))]
    add x0 -> x1, local copies, waits for them, and re-layouts: none -> 1.97 us  [local(): inner_imag = inner[0, :, lanes:] + inner[1, :, :lanes]]
    dot_general x10 -> x4, matrix products: 8.93 us -> 7.34 us  [contract(): return jnp.einsum(form, left, right, preferred_element_type=jnp.float32)]
    slice x6 -> x3, local copies, waits for them, and re-layouts: 5.24 us -> 3.76 us  [the longest x2 2.74 us: local(): first[1] * twist_sine]
where the time goes in v2:
time: 195 us; the launch traced here: 194 us
  Pallas kernels  137 us (70%)
  local copies, waits for them, and re-layouts  35.3 us (18%)
  other arithmetic  12.7 us (7%)
  matrix products  8.32 us (4%)
    pallas_call x5, Pallas kernels, exchange(): pl.pallas_call(functools.partial(_exchange_kernel, axis, gather), out_sha...  137 us
    dot_general x4, matrix products, contract(): return jnp.einsum(form, left, right, preferred_element_type=jnp.float32)  7.34 us
    reshape x1, local copies, waits for them, and re-layouts, local(): block = arrived.reshape(ctx_count, slab, 2, channels, slab).transpose(0,...  4.7 us
    reshape x1, local copies, waits for them, and re-layouts, local(): columns = arrived.reshape(ctx_count, slab, 2, channels, slab).transpose(0...  4.7 us

profile of v2, /device:TPU:64, one launch (start us, length us, event | category | flops | bytes accessed | tf_op | source)
XLA Modules:
  0.0 193.8 jit_solution(9398039301369099894)
XLA Ops:
  0.0 1.0 multiply_convert_fusion.1
  1.0 0.3 fusion.34
  1.3 0.6 fusion.31
  2.0 1.2 fusion.28
  3.2 0.4 reshape.248
  3.6 0.2 copy.39
  3.8 0.7 copy.40.x_ref
  4.5 25.2 %shard_map.64 = bf16[64,4,128]{2,1,0:T(4,128)(2,1)} custom-call(bf16[64,4,128]{2,1,0:T(4,128)(2,1)} %copy.40.x_ref), custom_call_target="tpu_custom_call" | custom-call | tf_op jit(solution)/shard_map/pallas_call | solution.py:62
  29.8 1.6 reshape.250
  31.4 0.9 convert_bitcast_fusion
  32.2 0.7 tile.21
  32.9 1.1 copy.45
  34.0 0.7 tile.9
  34.8 1.1 copy.43
  35.9 2.4 %add_convert_fusion = (bf16[32,32,1024]{2,1,0:T(8,128)(2,1)S(1)}, bf16[32,32,1024]{2,1,0:T(8,128)(2,1)S(1)}) fusion(f32[32,1024]{1,0:T(8,128)} %get-tuple-element.25, f32[32,1024]{1,0:T(8,128)S(1)} %get-tuple-element.24, f32[32,1024]{1,0:T(8,128)} %get-tuple-element.26, f32[32,1024]{1,0:T(8,128)S(1)} %get-tuple-element.23), kind=kLoop, calls=%fused_computation.2 | loop fusion | flops 8388608 | bytes 4718592 | tf_op jit(solution)/shard_map/convert_element_type | solution.py:90
  38.3 0.5 fusion.3
  38.8 0.8 copy-done.1
  39.6 0.8 fusion.41
  40.4 2.0 %copy.44 = f32[1,1024,64]{2,1,0:T(8,128)} copy(f32[1,1024,64]{1,2,0:T(8,128)} %get-tuple-element.17) | data formatting | bytes 524288 | tf_op jit(solution)/shard_map/slice | solution.py:130
  42.4 1.0 copy.42
  43.4 1.4 subtract_convert_fusion.3
  44.8 0.9 pad_maximum_fusion.6.x_ref
  45.7 25.5 %shard_map.65 = bf16[64,16,128]{2,1,0:T(8,128)(2,1)} custom-call(bf16[64,16,128]{2,1,0:T(8,128)(2,1)} %pad_maximum_fusion.6.x_ref), custom_call_target="tpu_custom_call" | custom-call | tf_op jit(solution)/shard_map/pallas_call | solution.py:62
  71.2 2.0 %copy.48 = bf16[64,16,128]{0,2,1:T(8,128)(2,1)} copy(bf16[64,16,128]{2,1,0:T(8,128)(2,1)} %shard_map.65) | data formatting | bytes 524288 | tf_op jit(solution)/shard_map/pallas_call | solution.py:62
  73.2 2.7 %copy.49 = bf16[64,16,2,4,16]{1,0,4,3,2:T(8,128)(2,1)} copy(bf16[64,16,2,4,16]{0,1,3,2,4:T(8,128)(2,1)} %bitcast.63) | data formatting | bytes 524288 | tf_op jit(solution)/shard_map/transpose | solution.py:139
  75.9 4.7 %reshape.260 = bf16[1024,128,1]{0,1,2:T(8,128)(2,1)S(1)} reshape(bf16[64,16,2,4,16]{1,0,4,3,2:T(8,128)(2,1)} %copy.49) | data formatting | bytes 524288 | tf_op jit(solution)/shard_map/reshape | solution.py:140
  80.6 3.3 %fusion = f32[2,1024,128]{1,2,0:T(8,128)S(1)} fusion(bf16[1024,128,1]{0,1,2:T(8,128)(2,1)S(1)} %reshape.260, bf16[1,1024,1024]{2,1,0:T(8,128)(2,1)S(1)} %bitcast.52, bf16[1,1024,1024]{2,1,0:T(8,128)(2,1)} %bitcast.56), kind=kOutput, calls=%fused_computation.4 | convolution fusion | flops 538968064 | bytes 5505024 | tf_op jit(solution)/shard_map/sbj,jk->sbk/dot_general | solution.py:100
  83.9 0.1 fusion.12
  84.0 1.5 fusion.1
  85.5 0.8 slice_add_fusion
  86.3 2.0 %copy.52 = f32[1,1024,64]{2,1,0:T(8,128)} copy(f32[1,1024,64]{1,2,0:T(8,128)} %get-tuple-element.15) | data formatting | bytes 524288 | tf_op jit(solution)/shard_map/add | solution.py:155
  88.3 1.0 copy.50
  89.3 1.4 subtract_convert_fusion.1
  90.8 0.9 pad_maximum_fusion.7.x_ref
  91.6 32.0 %shard_map.66 = bf16[64,16,128]{2,1,0:T(8,128)(2,1)} custom-call(bf16[64,16,128]{2,1,0:T(8,128)(2,1)} %pad_maximum_fusion.7.x_ref), custom_call_target="tpu_custom_call" | custom-call | tf_op jit(solution)/shard_map/pallas_call | solution.py:62
  123.7 1.3 copy.56
  124.9 1.8 copy.57
  126.8 4.7 %reshape.262 = bf16[1024,128,1]{0,1,2:T(8,128)(2,1)S(1)} reshape(bf16[64,16,2,4,16]{1,0,4,3,2:T(8,128)(2,1)} %copy.57) | data formatting | bytes 524288 | tf_op jit(solution)/shard_map/reshape | solution.py:168
  131.5 2.1 %fusion.2 = f32[2,512,128]{1,2,0:T(8,128)S(1)} fusion(bf16[1024,128,1]{0,1,2:T(8,128)(2,1)S(1)} %reshape.262, bf16[1,1024,1024]{2,1,0:T(8,128)(2,1)S(1)} %bitcast.54, bf16[1,1024,1024]{2,1,0:T(8,128)(2,1)} %bitcast.57), kind=kOutput, calls=%fused_computation.12 | convolution fusion | flops 272629760 | bytes 4980736 | tf_op jit(solution)/shard_map/sia,ak->sik/dot_general | solution.py:100
  133.7 0.8 convert_element_type.115.x_ref
  134.4 25.1 %shard_map.67 = bf16[64,4,128]{2,1,0:T(4,128)(2,1)} custom-call(bf16[64,4,128]{2,1,0:T(4,128)(2,1)} %convert_element_type.115.x_ref), custom_call_target="tpu_custom_call" | custom-call | tf_op jit(solution)/shard_map/pallas_call | solution.py:62
  159.5 1.0 copy.59
  160.5 0.4 copy.60
  160.9 0.6 reshape.256
  161.4 0.7 multiply_convert_fusion.x_ref
  162.2 29.4 %shard_map.68 = bf16[8,4,8192]{2,1,0:T(4,128)(2,1)} custom-call(bf16[4,8192]{1,0:T(4,128)(2,1)} %multiply_convert_fusion.x_ref), custom_call_target="tpu_custom_call" | custom-call | tf_op jit(solution)/shard_map/pallas_call | solution.py:62
  191.6 1.2 reshape.255
  192.8 1.0 convolution_convert_fusion
  (21 shorter events, 0.2 us)
Async XLA Ops:
  0.0 192.8 %copy-start = (bf16[32,64]{1,0:T(8,128)(2,1)S(1)}, bf16[32,64]{1,0:T(8,128)(2,1)}, u32[]{:S(2)}) copy-start(bf16[32,64]{1,0:T(8,128)(2,1)} %param.11) | copy-start | bytes 12292
  0.0 31.3 %copy-start.5 = (bf16[2,4,16,1024]{3,2,1,0:T(8,128)(2,1)S(1)}, bf16[2,4,16,1024]{3,2,1,0:T(8,128)(2,1)}, u32[]{:S(2)}) copy-start(bf16[2,4,16,1024]{3,2,1,0:T(8,128)(2,1)} %param.9) | copy-start | bytes 786436
  35.9 2.4 %copy-start.4 = (bf16[512,64]{1,0:T(8,128)(2,1)S(1)}, bf16[512,64]{1,0:T(8,128)(2,1)}, u32[]{:S(2)}) copy-start(bf16[512,64]{1,0:T(8,128)(2,1)} %reshape.250) | copy-start | bytes 196612
  38.3 1.3 copy-start.1
  80.6 3.3 %copy-start.3 = (f32[2,1024,64]{1,2,0:T(8,128)S(1)}, f32[2,1024,64]{1,2,0:T(8,128)}, u32[]{:S(2)}) copy-start(f32[2,1024,64]{1,2,0:T(8,128)} %convert_bitcast_fusion) | copy-start | bytes 1572868
  80.6 3.4 %copy-start.2 = (bf16[32,32,1024]{2,1,0:T(8,128)(2,1)S(1)}, bf16[32,32,1024]{2,1,0:T(8,128)(2,1)}, u32[]{:S(2)}) copy-start(bf16[32,32,1024]{2,1,0:T(8,128)(2,1)} %copy-done.1) | copy-start | bytes 6291460
  133.5 27.9 %copy-start.6 = (bf16[4,8192]{1,0:T(4,128)(2,1)S(1)}, bf16[4,8192]{1,0:T(4,128)(2,1)}, u32[]{:S(2)}) copy-start(bf16[4,8192]{1,0:T(4,128)(2,1)} %param.8) | copy-start | bytes 196612
  133.5 27.9 %copy-start.7 = (f32[4]{0:T(128)S(1)}, f32[4]{0:T(128)}, u32[]{:S(2)}) copy-start(f32[4]{0:T(128)} %param.10) | copy-start | bytes 52

commit v3 on v1

--- a/solution.py
+++ b/solution.py
@@ -74,6 +74,103 @@
     )(x)
 
 
+def _final_kernel(x_ref, y_ref, land, gathered, send_sem, recv_sem, fsend_sem, frecv_sem, local_sem):
+    count = land.shape[0]
+    groups = gathered.shape[0]
+    me = lax.axis_index("ctx")
+    mine = lax.axis_index("tp")
+    barrier = pltpu.get_barrier_semaphore()
+
+    def greet(step, carry):
+        peer = lax.rem(me + step, count)
+        pl.semaphore_signal(barrier, 1, device_id={"ctx": peer}, device_id_type=MESH)
+        return carry
+
+    def greet_tp(step, carry):
+        peer = lax.rem(mine + step, groups)
+        pl.semaphore_signal(barrier, 1, device_id={"tp": peer}, device_id_type=MESH)
+        return carry
+
+    lax.fori_loop(1, count, greet, 0)
+    lax.fori_loop(1, groups, greet_tp, 0)
+    pl.semaphore_wait(barrier, count + groups - 2)
+
+    def outgoing(peer):
+        return pltpu.make_async_remote_copy(
+            src_ref=x_ref.at[peer], dst_ref=land.at[me], send_sem=send_sem.at[peer],
+            recv_sem=recv_sem.at[me], device_id={"ctx": peer}, device_id_type=MESH)
+
+    def incoming(source):
+        return pltpu.make_async_remote_copy(
+            src_ref=x_ref.at[source], dst_ref=land.at[source], send_sem=send_sem.at[source],
+            recv_sem=recv_sem.at[source], device_id={"ctx": source}, device_id_type=MESH)
+
+    def send(step, carry):
+        outgoing(lax.rem(me + step, count)).start()
+        return carry
+
+    lax.fori_loop(1, count, send, 0)
+    local = pltpu.make_async_copy(x_ref.at[me], land.at[me], local_sem.at[0])
+    local.start()
+
+    def finish(step, carry):
+        outgoing(lax.rem(me + step, count)).wait_send()
+        incoming(lax.rem(me + count - step, count)).wait_recv()
+        return carry
+
+    lax.fori_loop(1, count, finish, 0)
+    local.wait()
+
+    def forward(peer):
+        return pltpu.make_async_remote_copy(
+            src_ref=land, dst_ref=gathered.at[mine], send_sem=fsend_sem.at[peer],
+            recv_sem=frecv_sem.at[mine], device_id={"tp": peer}, device_id_type=MESH)
+
+    def collected(source):
+        return pltpu.make_async_remote_copy(
+            src_ref=land, dst_ref=gathered.at[source], send_sem=fsend_sem.at[source],
+            recv_sem=frecv_sem.at[source], device_id={"tp": source}, device_id_type=MESH)
+
+    def send_tp(step, carry):
+        forward(lax.rem(mine + step, groups)).start()
+        return carry
+
+    lax.fori_loop(1, groups, send_tp, 0)
+    own = pltpu.make_async_copy(land, gathered.at[mine], local_sem.at[1])
+    own.start()
+
+    def finish_tp(step, carry):
+        forward(lax.rem(mine + step, groups)).wait_send()
+        collected(lax.rem(mine + groups - step, groups)).wait_recv()
+        return carry
+
+    lax.fori_loop(1, groups, finish_tp, 0)
+    own.wait()
+    y_ref[...] = gathered[...]
+
+
+def exchange_and_gather(x, collective):
+    count = lax.axis_size("ctx")
+    groups = lax.axis_size("tp")
+    full = (groups,) + tuple(x.shape)
+    return pl.pallas_call(
+        _final_kernel,
+        out_shape=jax.ShapeDtypeStruct(full, x.dtype),
+        in_specs=[pl.BlockSpec(memory_space=pltpu.VMEM)],
+        out_specs=pl.BlockSpec(memory_space=pltpu.VMEM),
+        scratch_shapes=[
+            pltpu.VMEM(x.shape, x.dtype),
+            pltpu.VMEM(full, x.dtype),
+            pltpu.SemaphoreType.DMA((count,)),
+            pltpu.SemaphoreType.DMA((count,)),
+            pltpu.SemaphoreType.DMA((groups,)),
+            pltpu.SemaphoreType.DMA((groups,)),
+            pltpu.SemaphoreType.DMA((2,)),
+        ],
+        compiler_params=pltpu.CompilerParams(collective_id=collective, has_side_effects=True),
+    )(x)
+
+
 def fourier_tables(length_all):
     split = 1 << (int(math.log2(length_all)) // 2)
     rows_hi = length_all // split
@@ -117,13 +214,15 @@
     positions = jnp.arange(block_order, dtype=jnp.int32)
     local_ticks = ctx_index * slab_width + jnp.arange(slab_width, dtype=jnp.int32)
 
-    outgoing = product.reshape(channels, rows_here, ctx_count, slab_width).transpose(2, 0, 1, 3)
-    arrived = exchange(outgoing.reshape(ctx_count, channels, -1), "ctx", False, 0)
-    grid_rows = (
-        arrived.reshape(ctx_count, channels, rows_here, slab_width)
+    both_rows = jnp.concatenate([product, q_feature], axis=0)
+    outgoing = both_rows.reshape(2 * channels, rows_here, ctx_count, slab_width).transpose(2, 0, 1, 3)
+    arrived = exchange(outgoing.reshape(ctx_count, 2 * channels, -1), "ctx", False, 0)
+    arrived_rows = (
+        arrived.reshape(ctx_count, 2 * channels, rows_here, slab_width)
         .transpose(1, 0, 2, 3)
-        .reshape(channels, half_rows, slab_width)
-    )
+        .reshape(2 * channels, half_rows, slab_width)
+    )
+    grid_rows, gate_rows = arrived_rows[:channels], arrived_rows[channels:]
     first_real = contract("cij,ia->caj", grid_rows, cosine_half)
     first_imag = -contract("cij,ia->caj", grid_rows, sine_half)
     twist_cosine, twist_sine = twist_tables(positions, local_ticks, length_all)
@@ -171,23 +270,25 @@
         "ia,caj->cij", sine_half, columns[1]
     )
     spatial = (summed * (1.0 / length_all)).astype(jnp.bfloat16)
-
-    outgoing = spatial.reshape(channels, ctx_count, rows_here, slab_width).transpose(1, 0, 2, 3)
-    arrived = exchange(outgoing.reshape(ctx_count, channels, -1), "ctx", False, 3)
-    convolved = (
-        arrived.reshape(ctx_count, channels, rows_here, slab_width)
-        .transpose(1, 2, 0, 3)
-        .reshape(channels, tokens)
-    )
-    gated_rows = (
-        q_feature.astype(jnp.float32)
-        * (convolved.astype(jnp.float32) + skip_gain[:, None] * product.astype(jnp.float32))
+    gated = (
+        gate_rows.astype(jnp.float32)
+        * (spatial.astype(jnp.float32) + skip_gain[:, None, None] * grid_rows.astype(jnp.float32))
     ).astype(jnp.bfloat16)
-    gated_all = exchange(gated_rows, "tp", True, 4).reshape(tp_count * channels, tokens)
+
+    outgoing = gated.reshape(channels, ctx_count, rows_here, slab_width).transpose(1, 0, 2, 3)
+    gathered = exchange_and_gather(outgoing.reshape(ctx_count, channels, -1), 3)
     outs_here = out_weight.shape[1] // tp_count
     tp_index = lax.axis_index("tp")
     my_weight = lax.dynamic_slice_in_dim(out_weight, tp_index * outs_here, outs_here, 1)
-    return jnp.dot(my_weight.T, gated_all, preferred_element_type=jnp.float32).astype(jnp.bfloat16)
+    mixed = contract(
+        "sce,spck->epk", my_weight.reshape(tp_count, channels, outs_here), gathered
+    )
+    return (
+        mixed.reshape(outs_here, ctx_count, rows_here, slab_width)
+        .transpose(0, 2, 1, 3)
+        .reshape(outs_here, tokens)
+        .astype(jnp.bfloat16)
+    )
 
 
 def solution(mesh):

time: 189 us -> 192 us (1.016)
  local copies, waits for them, and re-layouts: 30.5 us -> 38 us
  Pallas kernels: 138 us -> 134 us
    pallas_call x5 -> x3, Pallas kernels: 138 us -> 77.1 us  [exchange(): pl.pallas_call(functools.partial(_exchange_kernel, axis, gather), out_sha...]
    pallas_call x0 -> x1, Pallas kernels: none -> 57.4 us  [exchange_and_gather(): pl.pallas_call(_final_kernel, out_shape=jax.ShapeDtypeStruct(full, x.dtyp...]
    dot_general x0 -> x1, local copies, waits for them, and re-layouts: none -> 2.75 us  [contract(): return jnp.einsum(form, left, right, preferred_element_type=jnp.float32)]
    convert_element_type x4 -> x5, local copies, waits for them, and re-layouts: 2.15 us -> 4.6 us  [the longest x2 2.97 us: local(): return mixed.reshape(outs_here, ctx_count, rows_here, slab_width).transpo...]
    dot_general x10 -> x11, matrix products: 8.93 us -> 11 us  [contract(): return jnp.einsum(form, left, right, preferred_element_type=jnp.float32)]
where the time goes in v3:
time: 192 us
  Pallas kernels  134 us (70%)
  local copies, waits for them, and re-layouts  38 us (20%)
  matrix products  11.6 us (6%)
  other arithmetic  7.29 us (4%)
    pallas_call x3, Pallas kernels, exchange(): pl.pallas_call(functools.partial(_exchange_kernel, axis, gather), out_sha...  77.1 us
    pallas_call x1, Pallas kernels, exchange_and_gather(): pl.pallas_call(_final_kernel, out_shape=jax.ShapeDtypeStruct(full, x.dtyp...  57.4 us
    dot_general x11, matrix products, contract(): return jnp.einsum(form, left, right, preferred_element_type=jnp.float32)  11 us

profile of v3, /device:TPU:64, one launch (start us, length us, event | category | flops | bytes accessed | tf_op | source)
XLA Modules:
  0.0 191.7 jit_solution(10209935910022472463)
XLA Ops:
  0.0 0.7 copy-done
  0.8 0.9 multiply_convert_fusion
  1.7 0.9 pad_maximum_fusion.2
  2.6 0.8 reshape.283
  3.8 0.8 copy.46.x_ref
  4.6 25.4 %shard_map.64 = bf16[64,8,128]{2,1,0:T(8,128)(2,1)} custom-call(bf16[64,8,128]{2,1,0:T(8,128)(2,1)} %copy.46.x_ref), custom_call_target="tpu_custom_call" | custom-call | tf_op jit(solution)/shard_map/pallas_call | solution.py:62
  30.1 1.1 copy.47
  31.6 1.0 copy.65
  33.1 0.5 fusion.75
  33.6 0.6 fusion.78
  34.2 1.4 add_convert_fusion
  35.9 1.0 copy-done.1
  37.9 0.8 stack.19
  39.2 0.8 stack.18
  40.0 1.1 copy.52
  41.2 1.1 pad_maximum_fusion
  42.2 1.0 copy.54.x_ref
  43.2 25.9 %shard_map.65 = bf16[64,16,128]{2,1,0:T(8,128)(2,1)} custom-call(bf16[64,16,128]{2,1,0:T(8,128)(2,1)} %copy.54.x_ref), custom_call_target="tpu_custom_call" | custom-call | tf_op jit(solution)/shard_map/pallas_call | solution.py:62
  69.1 1.3 copy.55
  70.4 0.7 fusion.86
  71.6 1.8 squeeze.15
  73.4 1.2 fusion.6
  74.6 1.4 copy.56
  76.0 1.8 squeeze.14
  77.8 2.2 %fusion.18 = f32[4,16,1024]{2,1,0:T(8,128)S(1)} fusion(f32[4,16,1024]{2,1,0:T(8,128)} %fusion.6, bf16[4,16,1024]{2,1,0:T(8,128)(2,1)S(1)} %squeeze.14, bf16[1024,1024]{1,0:T(8,128)(2,1)} %bitcast.142), kind=kOutput, calls=%fused_computation.21 | convolution fusion | flops 134283264 | bytes 2752512 | tf_op jit(solution)/shard_map/caj,jb->cab/dot_general | solution.py:197
  80.6 0.6 fusion.48
  81.6 0.5 fusion.24
  82.5 0.5 fusion
  82.9 0.5 subtract_convert_fusion.1
  83.5 0.8 stack.22
  84.7 0.8 stack.21
  85.6 1.1 copy.58
  86.6 1.1 pad_maximum_fusion.1
  87.7 1.0 copy.60.x_ref
  88.7 25.8 %shard_map.66 = bf16[64,16,128]{2,1,0:T(8,128)(2,1)} custom-call(bf16[64,16,128]{2,1,0:T(8,128)(2,1)} %copy.60.x_ref), custom_call_target="tpu_custom_call" | custom-call | tf_op jit(solution)/shard_map/pallas_call | solution.py:62
  114.5 1.3 copy.61
  115.8 0.7 fusion.85
  116.5 1.4 copy.62
  117.9 2.4 %squeeze.16 = bf16[4,1024,16]{1,2,0:T(8,128)(2,1)} reshape(bf16[1,4,64,16,16]{3,2,4,1,0:T(8,128)(2,1)S(1)} %copy.62) | data formatting | bytes 262144 | tf_op jit(solution)/shard_map/squeeze | solution.py:269
  120.4 2.4 %fusion.38 = f32[4,16,512]{2,1,0:T(8,128)} fusion(bf16[4,1024,16]{1,2,0:T(8,128)(2,1)} %squeeze.16, bf16[1024,1024]{1,0:T(8,128)(2,1)} %bitcast.143), kind=kOutput, calls=%fused_computation.34 | convolution fusion | flops 67108864 | bytes 1310720 | tf_op jit(solution)/shard_map/ia,caj->cij/dot_general | solution.py:197
  123.3 1.8 squeeze.17
  125.1 1.4 fusion.36
  127.1 0.7 copy.68.x_ref
  127.9 57.4 %shard_map.67 = bf16[8,64,4,128]{3,2,1,0:T(4,128)(2,1)} custom-call(bf16[64,4,128]{2,1,0:T(4,128)(2,1)} %copy.68.x_ref), custom_call_target="tpu_custom_call" | custom-call | tf_op jit(solution)/shard_map/pallas_call | solution.py:156
  185.2 2.8 %copy.69 = bf16[64,128,4,8]{0,3,2,1:T(8,128)(2,1)S(1)} copy(bf16[64,128,4,8]{1,2,0,3:T(4,128)(2,1)} %bitcast.151) | data formatting | bytes 1048576 | tf_op jit(solution)/shard_map/sce,spck->epk/dot_general | solution.py:197
  188.0 0.7 fusion.17
  188.7 0.5 copy.71
  189.3 2.5 %convert_element_type.164 = bf16[8,8192]{1,0:T(8,128)(2,1)} reshape(bf16[8,8,64,16]{3,2,1,0:T(8,128)(2,1)S(1)} %copy.71) | data formatting | bytes 262144 | tf_op jit(solution)/shard_map/convert_element_type | solution.py:290
  (37 shorter events, 6.3 us)
Async XLA Ops:
  0.0 0.7 copy-start
  33.1 2.9 %copy-start.3 = (bf16[4,512,16]{1,2,0:T(8,128)(2,1)}, bf16[4,512,16]{1,2,0:T(8,128)(2,1)S(1)}, u32[]{:S(2)}) copy-start(bf16[4,512,16]{1,2,0:T(8,128)(2,1)S(1)} %copy.50) | copy-start | bytes 196612
  35.6 1.3 copy-start.1
  37.3 0.6 copy-start.6
  77.8 2.8 %copy-start.2 = (bf16[32,32,1024]{2,1,0:T(8,128)(2,1)S(1)}, bf16[32,32,1024]{2,1,0:T(8,128)(2,1)}, u32[]{:S(2)}) copy-start(bf16[32,32,1024]{2,1,0:T(8,128)(2,1)} %copy-done.1) | copy-start | bytes 6291460
  77.8 2.8 %copy-start.5 = (bf16[2,4,16,1024]{3,2,1,0:T(8,128)(2,1)S(1)}, bf16[2,4,16,1024]{3,2,1,0:T(8,128)(2,1)}, u32[]{:S(2)}) copy-start(bf16[2,4,16,1024]{3,2,1,0:T(8,128)(2,1)} %param.9) | copy-start | bytes 786436
  81.1 1.0 copy-start.7
  120.4 4.7 %copy-start.4 = (bf16[4,512,16]{1,2,0:T(8,128)(2,1)S(1)}, bf16[4,512,16]{1,2,0:T(8,128)(2,1)}, u32[]{:S(2)}) copy-start(bf16[4,512,16]{1,2,0:T(8,128)(2,1)} %copy-done.3) | copy-start | bytes 196612
  120.4 4.7 %copy-start.8 = (f32[4]{0:T(128)S(1)}, f32[4]{0:T(128)}, u32[]{:S(2)}) copy-start(f32[4]{0:T(128)} %param.10) | copy-start | bytes 52

commit v4 on v3

--- a/solution.py
+++ b/solution.py
@@ -74,11 +74,13 @@
     )(x)
 
 
-def _final_kernel(x_ref, y_ref, land, gathered, send_sem, recv_sem, fsend_sem, frecv_sem, local_sem):
+def _final_kernel(x_ref, y_ref, land, gathered, send_sem, recv_sem, right_sem, left_sem, line_sem, local_sem):
     count = land.shape[0]
     groups = gathered.shape[0]
     me = lax.axis_index("ctx")
     mine = lax.axis_index("tp")
+    has_right = mine < groups - 1
+    has_left = mine > 0
     barrier = pltpu.get_barrier_semaphore()
 
     def greet(step, carry):
@@ -86,14 +88,17 @@
         pl.semaphore_signal(barrier, 1, device_id={"ctx": peer}, device_id_type=MESH)
         return carry
 
-    def greet_tp(step, carry):
-        peer = lax.rem(mine + step, groups)
-        pl.semaphore_signal(barrier, 1, device_id={"tp": peer}, device_id_type=MESH)
-        return carry
-
     lax.fori_loop(1, count, greet, 0)
-    lax.fori_loop(1, groups, greet_tp, 0)
-    pl.semaphore_wait(barrier, count + groups - 2)
+
+    @pl.when(has_right)
+    def _():
+        pl.semaphore_signal(barrier, 1, device_id={"tp": mine + 1}, device_id_type=MESH)
+
+    @pl.when(has_left)
+    def _():
+        pl.semaphore_signal(barrier, 1, device_id={"tp": mine - 1}, device_id_type=MESH)
+
+    pl.semaphore_wait(barrier, count - 1 + has_right.astype(jnp.int32) + has_left.astype(jnp.int32))
 
     def outgoing(peer):
         return pltpu.make_async_remote_copy(
@@ -120,32 +125,63 @@
 
     lax.fori_loop(1, count, finish, 0)
     local.wait()
-
-    def forward(peer):
-        return pltpu.make_async_remote_copy(
-            src_ref=land, dst_ref=gathered.at[mine], send_sem=fsend_sem.at[peer],
-            recv_sem=frecv_sem.at[mine], device_id={"tp": peer}, device_id_type=MESH)
-
-    def collected(source):
-        return pltpu.make_async_remote_copy(
-            src_ref=land, dst_ref=gathered.at[source], send_sem=fsend_sem.at[source],
-            recv_sem=frecv_sem.at[source], device_id={"tp": source}, device_id_type=MESH)
-
-    def send_tp(step, carry):
-        forward(lax.rem(mine + step, groups)).start()
-        return carry
-
-    lax.fori_loop(1, groups, send_tp, 0)
     own = pltpu.make_async_copy(land, gathered.at[mine], local_sem.at[1])
     own.start()
-
-    def finish_tp(step, carry):
-        forward(lax.rem(mine + step, groups)).wait_send()
-        collected(lax.rem(mine + groups - step, groups)).wait_recv()
-        return carry
-
-    lax.fori_loop(1, groups, finish_tp, 0)
     own.wait()
+
+    def to_right(slot):
+        return pltpu.make_async_remote_copy(
+            src_ref=gathered.at[slot], dst_ref=gathered.at[slot], send_sem=right_sem.at[slot],
+            recv_sem=line_sem.at[slot], device_id={"tp": mine + 1}, device_id_type=MESH)
+
+    def to_left(slot):
+        return pltpu.make_async_remote_copy(
+            src_ref=gathered.at[slot], dst_ref=gathered.at[slot], send_sem=left_sem.at[slot],
+            recv_sem=line_sem.at[slot], device_id={"tp": mine - 1}, device_id_type=MESH)
+
+    @pl.when(has_right)
+    def _():
+        to_right(mine).start()
+
+    @pl.when(has_left)
+    def _():
+        to_left(mine).start()
+
+    def relay(step, carry):
+        @pl.when(step <= mine)
+        def _():
+            slot = mine - step
+            to_right(slot).wait_recv()
+
+            @pl.when(has_right)
+            def _():
+                to_right(slot).start()
+
+        @pl.when(step < groups - mine)
+        def _():
+            slot = mine + step
+            to_left(slot).wait_recv()
+
+            @pl.when(has_left)
+            def _():
+                to_left(slot).start()
+
+        return carry
+
+    lax.fori_loop(1, groups, relay, 0)
+
+    def drain(slot, carry):
+        @pl.when(has_right & (slot <= mine))
+        def _():
+            to_right(slot).wait_send()
+
+        @pl.when(has_left & (slot >= mine))
+        def _():
+            to_left(slot).wait_send()
+
+        return carry
+
+    lax.fori_loop(0, groups, drain, 0)
     y_ref[...] = gathered[...]
 
 
@@ -165,6 +201,7 @@
             pltpu.SemaphoreType.DMA((count,)),
             pltpu.SemaphoreType.DMA((groups,)),
             pltpu.SemaphoreType.DMA((groups,)),
+            pltpu.SemaphoreType.DMA((groups,)),
             pltpu.SemaphoreType.DMA((2,)),
         ],
         compiler_params=pltpu.CompilerParams(collective_id=collective, has_side_effects=True),

time: 192 us -> 193 us (level)
  the two profiles are of different devices: /device:TPU:64 before, /device:TPU:6 now
where the time goes in v4:
time: 193 us
  Pallas kernels  135 us (70%)
  local copies, waits for them, and re-layouts  38 us (20%)
  matrix products  11.6 us (6%)
  other arithmetic  7.29 us (4%)
    pallas_call x3, Pallas kernels, exchange(): pl.pallas_call(functools.partial(_exchange_kernel, axis, gather), out_sha...  73.3 us
    pallas_call x1, Pallas kernels, exchange_and_gather(): pl.pallas_call(_final_kernel, out_shape=jax.ShapeDtypeStruct(full, x.dtyp...  62.1 us
    dot_general x11, matrix products, contract(): return jnp.einsum(form, left, right, preferred_element_type=jnp.float32)  11 us

profile of v4, /device:TPU:6, one launch (start us, length us, event | category | flops | bytes accessed | tf_op | source)
XLA Modules:
  0.0 192.6 jit_solution(5546960806751316008)
XLA Ops:
  0.0 0.7 copy-done
  0.8 0.9 multiply_convert_fusion
  1.7 0.9 pad_maximum_fusion.2
  2.6 0.8 reshape.283
  3.8 0.8 copy.46.x_ref
  4.6 26.6 %shard_map.64 = bf16[64,8,128]{2,1,0:T(8,128)(2,1)} custom-call(bf16[64,8,128]{2,1,0:T(8,128)(2,1)} %copy.46.x_ref), custom_call_target="tpu_custom_call" | custom-call | tf_op jit(solution)/shard_map/pallas_call | solution.py:62
  31.2 1.1 copy.47
  32.8 1.0 copy.65
  34.3 0.5 fusion.75
  34.8 0.6 fusion.78
  35.4 1.4 add_convert_fusion
  37.1 1.0 copy-done.1
  39.1 0.8 stack.19
  40.4 0.8 stack.18
  41.2 1.1 copy.52
  42.3 1.1 pad_maximum_fusion
  43.4 1.0 copy.54.x_ref
  44.4 22.9 %shard_map.65 = bf16[64,16,128]{2,1,0:T(8,128)(2,1)} custom-call(bf16[64,16,128]{2,1,0:T(8,128)(2,1)} %copy.54.x_ref), custom_call_target="tpu_custom_call" | custom-call | tf_op jit(solution)/shard_map/pallas_call | solution.py:62
  67.3 1.3 copy.55
  68.6 0.7 fusion.86
  69.8 1.8 squeeze.15
  71.6 1.2 fusion.6
  72.7 1.4 copy.56
  74.2 1.8 squeeze.14
  76.0 2.2 %fusion.18 = f32[4,16,1024]{2,1,0:T(8,128)S(1)} fusion(f32[4,16,1024]{2,1,0:T(8,128)} %fusion.6, bf16[4,16,1024]{2,1,0:T(8,128)(2,1)S(1)} %squeeze.14, bf16[1024,1024]{1,0:T(8,128)(2,1)} %bitcast.142), kind=kOutput, calls=%fused_computation.21 | convolution fusion | flops 134283264 | bytes 2752512 | tf_op jit(solution)/shard_map/caj,jb->cab/dot_general | solution.py:234
  78.7 0.6 fusion.48
  79.8 0.5 fusion.24
  81.1 0.5 subtract_convert_fusion.1
  81.7 0.8 stack.22
  82.9 0.8 stack.21
  83.7 1.1 copy.58
  84.8 1.1 pad_maximum_fusion.1
  85.9 1.0 copy.60.x_ref
  86.8 23.8 %shard_map.66 = bf16[64,16,128]{2,1,0:T(8,128)(2,1)} custom-call(bf16[64,16,128]{2,1,0:T(8,128)(2,1)} %copy.60.x_ref), custom_call_target="tpu_custom_call" | custom-call | tf_op jit(solution)/shard_map/pallas_call | solution.py:62
  110.7 1.3 copy.61
  111.9 0.7 fusion.85
  112.7 1.4 copy.62
  114.1 2.4 %squeeze.16 = bf16[4,1024,16]{1,2,0:T(8,128)(2,1)} reshape(bf16[1,4,64,16,16]{3,2,4,1,0:T(8,128)(2,1)S(1)} %copy.62) | data formatting | bytes 262144 | tf_op jit(solution)/shard_map/squeeze | solution.py:306
  116.5 2.4 %fusion.38 = f32[4,16,512]{2,1,0:T(8,128)} fusion(bf16[4,1024,16]{1,2,0:T(8,128)(2,1)} %squeeze.16, bf16[1024,1024]{1,0:T(8,128)(2,1)} %bitcast.143), kind=kOutput, calls=%fused_computation.34 | convolution fusion | flops 67108864 | bytes 1310720 | tf_op jit(solution)/shard_map/ia,caj->cij/dot_general | solution.py:234
  118.9 0.5 copy.63
  119.4 1.8 squeeze.17
  121.2 1.4 fusion.36
  123.3 0.7 copy.68.x_ref
  124.0 62.1 %shard_map.67 = bf16[8,64,4,128]{3,2,1,0:T(4,128)(2,1)} custom-call(bf16[64,4,128]{2,1,0:T(4,128)(2,1)} %copy.68.x_ref), custom_call_target="tpu_custom_call" | custom-call | tf_op jit(solution)/shard_map/pallas_call | solution.py:192
  186.1 2.8 %copy.69 = bf16[64,128,4,8]{0,3,2,1:T(8,128)(2,1)S(1)} copy(bf16[64,128,4,8]{1,2,0,3:T(4,128)(2,1)} %bitcast.151) | data formatting | bytes 1048576 | tf_op jit(solution)/shard_map/sce,spck->epk/dot_general | solution.py:234
  188.9 0.7 fusion.17
  189.6 0.5 copy.71
  190.1 2.5 %convert_element_type.164 = bf16[8,8192]{1,0:T(8,128)(2,1)} reshape(bf16[8,8,64,16]{3,2,1,0:T(8,128)(2,1)S(1)} %copy.71) | data formatting | bytes 262144 | tf_op jit(solution)/shard_map/convert_element_type | solution.py:327
  (37 shorter events, 6.3 us)
Async XLA Ops:
  0.0 0.7 copy-start
  34.2 2.9 %copy-start.3 = (bf16[4,512,16]{1,2,0:T(8,128)(2,1)}, bf16[4,512,16]{1,2,0:T(8,128)(2,1)S(1)}, u32[]{:S(2)}) copy-start(bf16[4,512,16]{1,2,0:T(8,128)(2,1)S(1)} %copy.50) | copy-start | bytes 196612
  36.8 1.3 copy-start.1
  38.5 0.6 copy-start.6
  75.9 2.8 %copy-start.2 = (bf16[32,32,1024]{2,1,0:T(8,128)(2,1)S(1)}, bf16[32,32,1024]{2,1,0:T(8,128)(2,1)}, u32[]{:S(2)}) copy-start(bf16[32,32,1024]{2,1,0:T(8,128)(2,1)} %copy-done.1) | copy-start | bytes 6291460
  76.0 2.8 %copy-start.5 = (bf16[2,4,16,1024]{3,2,1,0:T(8,128)(2,1)S(1)}, bf16[2,4,16,1024]{3,2,1,0:T(8,128)(2,1)}, u32[]{:S(2)}) copy-start(bf16[2,4,16,1024]{3,2,1,0:T(8,128)(2,1)} %param.9) | copy-start | bytes 786436
  79.3 1.0 copy-start.7
  116.5 4.7 %copy-start.4 = (bf16[4,512,16]{1,2,0:T(8,128)(2,1)S(1)}, bf16[4,512,16]{1,2,0:T(8,128)(2,1)}, u32[]{:S(2)}) copy-start(bf16[4,512,16]{1,2,0:T(8,128)(2,1)} %copy-done.3) | copy-start | bytes 196612
  116.5 4.7 %copy-start.8 = (f32[4]{0:T(128)S(1)}, f32[4]{0:T(128)}, u32[]{:S(2)}) copy-start(f32[4]{0:T(128)} %param.10) | copy-start | bytes 52

commit v5 on v1

--- a/solution.py
+++ b/solution.py
@@ -124,13 +124,17 @@
         .transpose(1, 0, 2, 3)
         .reshape(channels, half_rows, slab_width)
     )
-    first_real = contract("cij,ia->caj", grid_rows, cosine_half)
-    first_imag = -contract("cij,ia->caj", grid_rows, sine_half)
+    both_full = jnp.stack([cosine_full, sine_full])
+    both_half = jnp.stack([cosine_half, sine_half])
+    first = contract("sia,cij->scaj", both_half, grid_rows)
     twist_cosine, twist_sine = twist_tables(positions, local_ticks, length_all)
-    spread_real = (first_real * twist_cosine + first_imag * twist_sine).astype(jnp.bfloat16)
-    spread_imag = (first_imag * twist_cosine - first_real * twist_sine).astype(jnp.bfloat16)
-
-    spread = jnp.stack([spread_real, spread_imag])
+    spread = jnp.stack(
+        [
+            first[0] * twist_cosine - first[1] * twist_sine,
+            -first[1] * twist_cosine - first[0] * twist_sine,
+        ]
+    ).astype(jnp.bfloat16)
+
     outgoing = spread.reshape(2, channels, ctx_count, slab_width, slab_width).transpose(2, 0, 1, 3, 4)
     arrived = exchange(outgoing.reshape(ctx_count, -1, 128), "ctx", False, 1)
     block = (
@@ -138,28 +142,28 @@
         .transpose(1, 2, 3, 0, 4)
         .reshape(2, channels, slab_width, block_order)
     )
-    block_real, block_imag = block[0], block[1]
-    freq_real = contract("caj,jb->cab", block_real, cosine_full) + contract(
-        "caj,jb->cab", block_imag, sine_full
-    )
-    freq_imag = contract("caj,jb->cab", block_imag, cosine_full) - contract(
-        "caj,jb->cab", block_real, sine_full
-    )
+    freq = contract("rcaj,sjb->srcab", block, both_full)
+    freq_real = freq[0, 0] + freq[1, 1]
+    freq_imag = freq[0, 1] - freq[1, 0]
     resp_real = spectrum[0].astype(jnp.float32)
     resp_imag = spectrum[1].astype(jnp.float32)
-    shaped_real = (freq_real * resp_real - freq_imag * resp_imag).astype(jnp.bfloat16)
-    shaped_imag = (freq_real * resp_imag + freq_imag * resp_real).astype(jnp.bfloat16)
-    inner_real = contract("cab,bj->caj", shaped_real, cosine_full) - contract(
-        "cab,bj->caj", shaped_imag, sine_full
-    )
-    inner_imag = contract("cab,bj->caj", shaped_imag, cosine_full) + contract(
-        "cab,bj->caj", shaped_real, sine_full
-    )
+    shaped = jnp.stack(
+        [
+            freq_real * resp_real - freq_imag * resp_imag,
+            freq_real * resp_imag + freq_imag * resp_real,
+        ]
+    ).astype(jnp.bfloat16)
+    inner = contract("rcab,sbj->srcaj", shaped, both_full)
+    inner_real = inner[0, 0] - inner[1, 1]
+    inner_imag = inner[0, 1] + inner[1, 0]
     twist_cosine, twist_sine = twist_tables(local_ticks, positions, length_all)
-    back_real = (inner_real * twist_cosine - inner_imag * twist_sine).astype(jnp.bfloat16)
-    back_imag = (inner_imag * twist_cosine + inner_real * twist_sine).astype(jnp.bfloat16)
-
-    back = jnp.stack([back_real, back_imag])
+    back = jnp.stack(
+        [
+            inner_real * twist_cosine - inner_imag * twist_sine,
+            inner_imag * twist_cosine + inner_real * twist_sine,
+        ]
+    ).astype(jnp.bfloat16)
+
     outgoing = back.reshape(2, channels, slab_width, ctx_count, slab_width).transpose(3, 0, 1, 2, 4)
     arrived = exchange(outgoing.reshape(ctx_count, -1, 128), "ctx", False, 2)
     columns = (
@@ -167,9 +171,8 @@
         .transpose(1, 2, 0, 3, 4)
         .reshape(2, channels, block_order, slab_width)
     )
-    summed = contract("ia,caj->cij", cosine_half, columns[0]) - contract(
-        "ia,caj->cij", sine_half, columns[1]
-    )
+    parts = contract("sia,rcaj->srcij", both_half, columns)
+    summed = parts[0, 0] - parts[1, 1]
     spatial = (summed * (1.0 / length_all)).astype(jnp.bfloat16)
 
     outgoing = spatial.reshape(channels, ctx_count, rows_here, slab_width).transpose(1, 0, 2, 3)

time: 189 us -> 186 us (0.984)
  matrix products: 11.7 us -> 7.38 us
  other arithmetic: 7.48 us -> 9.62 us
    reshape x1 -> x2, local copies, waits for them, and re-layouts: 0.19 us -> 7.43 us  [the longest x1 3.8 us: local(): block = arrived.reshape(ctx_count, 2, channels, slab_width, slab_width).t...]
    squeeze x4 -> x0, local copies, waits for them, and re-layouts: 7.17 us -> none  [the longest x2 3.58 us: local(): block_real, block_imag = (block[0], block[1])]
    slice x6 -> x0, local copies, waits for them, and re-layouts: 5.24 us -> none  [the longest x3 2.61 us: local(): block_real, block_imag = (block[0], block[1])]
    dot_general x10 -> x4, matrix products: 8.93 us -> 6.4 us  [contract(): return jnp.einsum(form, left, right, preferred_element_type=jnp.float32)]
    sub x0 -> x1, local copies, waits for them, and re-layouts: none -> 2.06 us  [local(): inner_real = inner[0, 0] - inner[1, 1]]
    transpose x0 -> x2, local copies, waits for them, and re-layouts: none -> 2.06 us  [the longest x1 1.05 us: local(): columns = arrived.reshape(ctx_count, 2, channels, slab_width, slab_width)...]
    unnamed x22 -> x26, local copies, waits for them, and re-layouts: 0.11 us -> 2.08 us
where the time goes in v5:
time: 186 us; the launch traced here: 185 us
  Pallas kernels  137 us (74%)
  local copies, waits for them, and re-layouts  30.5 us (16%)
  other arithmetic  9.62 us (5%)
  matrix products  7.38 us (4%)
    pallas_call x5, Pallas kernels, exchange(): pl.pallas_call(functools.partial(_exchange_kernel, axis, gather), out_sha...  137 us
    dot_general x4, matrix products, contract(): return jnp.einsum(form, left, right, preferred_element_type=jnp.float32)  6.4 us
    reshape x1, local copies, waits for them, and re-layouts, local(): block = arrived.reshape(ctx_count, 2, channels, slab_width, slab_width).t...  3.8 us

profile of v5, /device:TPU:64, one launch (start us, length us, event | category | flops | bytes accessed | tf_op | source)
XLA Modules:
  0.0 185.1 jit_solution(16705193019780067230)
XLA Ops:
  0.0 0.6 fusion.51
  0.6 0.5 fusion.48
  1.1 1.4 add_convert_fusion
  2.7 1.1 copy-done.1
  3.9 0.6 copy-done.3
  4.5 0.4 reshape.418
  4.9 0.2 copy.57
  5.1 0.7 copy.58.x_ref
  5.9 25.2 %shard_map.64 = bf16[64,4,128]{2,1,0:T(4,128)(2,1)} custom-call(bf16[64,4,128]{2,1,0:T(4,128)(2,1)} %copy.58.x_ref), custom_call_target="tpu_custom_call" | custom-call | tf_op jit(solution)/shard_map/pallas_call | solution.py:62
  31.1 1.0 copy.59
  32.1 0.3 copy.60
  32.4 0.5 fusion.8
  32.9 0.3 fusion.54
  33.4 0.8 stack.44
  34.2 0.4 copy.62
  34.6 0.8 stack.45
  35.5 0.4 copy.63
  36.0 1.0 copy.64.x_ref
  37.0 25.5 %shard_map.65 = bf16[64,16,128]{2,1,0:T(8,128)(2,1)} custom-call(bf16[64,16,128]{2,1,0:T(8,128)(2,1)} %copy.64.x_ref), custom_call_target="tpu_custom_call" | custom-call | tf_op jit(solution)/shard_map/pallas_call | solution.py:62
  62.5 1.3 copy.65
  63.8 1.0 copy.66
  64.8 3.8 %reshape.435 = bf16[2,4,16,1024,1]{3,2,1,0,4:T(8,128)(2,1)S(1)} reshape(bf16[2,4,16,64,16]{4,3,2,1,0:T(8,128)(2,1)S(1)} %copy.66) | data formatting | bytes 524288 | tf_op jit(solution)/shard_map/reshape | solution.py:143
  68.6 3.1 %fusion.6 = f32[2,2,4,16,1024]{4,3,2,1,0:T(8,128)S(1)} fusion(bf16[2,4,16,1024,1]{3,2,1,0,4:T(8,128)(2,1)S(1)} %reshape.435, bf16[1,1024,1024]{2,1,0:T(8,128)(2,1)} %bitcast.110, bf16[1,1024,1024]{2,1,0:T(8,128)(2,1)} %bitcast.113), kind=kOutput, calls=%fused_computation.13 | convolution fusion | flops 545259520 | bytes 5505024 | tf_op jit(solution)/shard_map/rcaj,sjb->srcab/dot_general | solution.py:100
  71.9 0.3 copy-done.4
  72.2 0.7 fusion.7
  73.0 0.7 add.146
  73.7 2.1 %sub.73 = f32[1,4,16,64,16]{4,3,2,1,0:T(8,128)} reshape(f32[1,1,4,16,1024]{4,3,2,1,0:T(8,128)S(1)} %get-tuple-element.14) | data formatting | bytes 524288 | tf_op jit(solution)/shard_map/sub | solution.py:157
  75.8 2.1 %fusion.28 = (f32[16,64,16]{2,1,0:T(8,128)S(1)}, f32[16,64,16]{2,1,0:T(8,128)S(1)}) fusion(s32[64,16]{1,0:T(8,128)S(1)} %multiply_add_fusion, s32[16]{0:T(128)S(1)} %iota_add_fusion), kind=kLoop, calls=%fused_computation.49 | loop fusion | flops 229376 | bytes 135232 | tf_op jit(solution)/shard_map/cos | solution.py:96
  77.9 3.3 %subtract_convert_fusion.1 = (bf16[1,4,16,64,16]{4,3,2,1,0:T(8,128)(2,1)}, bf16[1,4,16,64,16]{4,3,2,1,0:T(8,128)(2,1)S(1)}) fusion(f32[1,4,16,64,16]{4,3,2,1,0:T(8,128)S(1)} %add.146, f32[1,4,16,64,16]{4,3,2,1,0:T(8,128)} %sub.73, f32[16,64,16]{2,1,0:T(8,128)S(1)} %get-tuple-element.20, f32[16,64,16]{2,1,0:T(8,128)S(1)} %get-tuple-element.19), kind=kLoop, calls=%fused_computation.12 | loop fusion | flops 524288 | bytes 917504 | tf_op jit(solution)/shard_map/convert.3
  81.2 1.6 copy.67
  82.8 0.4 copy.68
  83.3 1.0 copy.69.x_ref
  84.3 32.0 %shard_map.66 = bf16[64,16,128]{2,1,0:T(8,128)(2,1)} custom-call(bf16[64,16,128]{2,1,0:T(8,128)(2,1)} %copy.69.x_ref), custom_call_target="tpu_custom_call" | custom-call | tf_op jit(solution)/shard_map/pallas_call | solution.py:62
  116.3 1.3 copy.70
  117.5 1.1 copy.71
  118.6 3.6 %reshape.437 = bf16[2,4,1024,16,1]{2,3,1,0,4:T(8,128)(2,1)S(1)} reshape(bf16[2,4,64,16,16]{3,2,4,1,0:T(8,128)(2,1)S(1)} %copy.71) | data formatting | bytes 524288 | tf_op jit(solution)/shard_map/reshape | solution.py:172
  122.2 2.1 %fusion.11 = f32[2,2,4,512,16]{3,4,0,2,1:T(8,128)S(1)} fusion(bf16[1,512,1024]{2,1,0:T(8,128)(2,1)S(1)} %copy-done.6, bf16[1,512,1024]{2,1,0:T(8,128)(2,1)} %copy-done.7, bf16[2,4,1024,16,1]{2,3,1,0,4:T(8,128)(2,1)S(1)} %reshape.437), kind=kOutput, calls=%fused_computation.16 | convolution fusion | flops 272629760 | bytes 2883584 | tf_op jit(solution)/shard_map/sia,rcaj->srcij/dot_general | solution.py:100
  124.3 0.3 copy.72
  124.6 0.3 copy.73
  125.0 0.7 copy.74.x_ref
  125.7 25.3 %shard_map.67 = bf16[64,4,128]{2,1,0:T(4,128)(2,1)} custom-call(bf16[64,4,128]{2,1,0:T(4,128)(2,1)} %copy.74.x_ref), custom_call_target="tpu_custom_call" | custom-call | tf_op jit(solution)/shard_map/pallas_call | solution.py:62
  151.0 1.0 copy.75
  152.0 0.3 copy.76
  152.3 0.6 reshape.430
  152.9 0.7 multiply_convert_fusion.x_ref
  153.7 29.3 %shard_map.68 = bf16[8,4,8192]{2,1,0:T(4,128)(2,1)} custom-call(bf16[4,8192]{1,0:T(4,128)(2,1)} %multiply_convert_fusion.x_ref), custom_call_target="tpu_custom_call" | custom-call | tf_op jit(solution)/shard_map/pallas_call | solution.py:62
  183.0 1.2 reshape.429
  184.2 1.0 convolution_convert_fusion
  (35 shorter events, 0.8 us)
Async XLA Ops:
  0.0 184.2 %copy-start = (bf16[32,64]{1,0:T(8,128)(2,1)S(1)}, bf16[32,64]{1,0:T(8,128)(2,1)}, u32[]{:S(2)}) copy-start(bf16[32,64]{1,0:T(8,128)(2,1)} %param.11) | copy-start | bytes 12292
  2.5 1.3 copy-start.1
  2.5 1.9 %copy-start.3 = (bf16[32,32,1024]{2,1,0:T(8,128)(2,1)}, bf16[32,32,1024]{2,1,0:T(8,128)(2,1)S(1)}, u32[]{:S(2)}) copy-start(bf16[32,32,1024]{2,1,0:T(8,128)(2,1)S(1)} %get-tuple-element.18) | copy-start | bytes 6291460
  2.6 1.9 %copy-start.9 = (bf16[4,8192]{1,0:T(4,128)(2,1)S(1)}, bf16[4,8192]{1,0:T(4,128)(2,1)}, u32[]{:S(2)}) copy-start(bf16[4,8192]{1,0:T(4,128)(2,1)} %param.7) | copy-start | bytes 196612
  2.6 1.9 %copy-start.10 = (bf16[4,8192]{1,0:T(4,128)(2,1)S(1)}, bf16[4,8192]{1,0:T(4,128)(2,1)}, u32[]{:S(2)}) copy-start(bf16[4,8192]{1,0:T(4,128)(2,1)} %param.6) | copy-start | bytes 196612
  2.7 29.7 %copy-start.5 = (bf16[1,512,1024]{2,1,0:T(8,128)(2,1)}, bf16[1,512,1024]{2,1,0:T(8,128)(2,1)S(1)}, u32[]{:S(2)}) copy-start(bf16[1,512,1024]{2,1,0:T(8,128)(2,1)S(1)} %slice_bitcast_fusion) | copy-start | bytes 3145732
  4.5 28.4 %copy-start.7 = (bf16[1,512,1024]{2,1,0:T(8,128)(2,1)}, bf16[1,512,1024]{2,1,0:T(8,128)(2,1)S(1)}, u32[]{:S(2)}) copy-start(bf16[1,512,1024]{2,1,0:T(8,128)(2,1)S(1)} %slice_bitcast_fusion.1) | copy-start | bytes 3145732
  68.6 3.1 %copy-start.8 = (bf16[2,4,16,1024]{3,2,1,0:T(8,128)(2,1)S(1)}, bf16[2,4,16,1024]{3,2,1,0:T(8,128)(2,1)}, u32[]{:S(2)}) copy-start(bf16[2,4,16,1024]{3,2,1,0:T(8,128)(2,1)} %param.9) | copy-start | bytes 786436
  68.6 3.3 %copy-start.2 = (bf16[32,32,1024]{2,1,0:T(8,128)(2,1)S(1)}, bf16[32,32,1024]{2,1,0:T(8,128)(2,1)}, u32[]{:S(2)}) copy-start(bf16[32,32,1024]{2,1,0:T(8,128)(2,1)} %copy-done.1) | copy-start | bytes 6291460
  68.6 3.6 %copy-start.4 = (bf16[32,32,1024]{2,1,0:T(8,128)(2,1)S(1)}, bf16[32,32,1024]{2,1,0:T(8,128)(2,1)}, u32[]{:S(2)}) copy-start(bf16[32,32,1024]{2,1,0:T(8,128)(2,1)} %copy-done.3) | copy-start | bytes 6291460
  118.6 3.6 %copy-start.6 = (bf16[1,512,1024]{2,1,0:T(8,128)(2,1)S(1)}, bf16[1,512,1024]{2,1,0:T(8,128)(2,1)}, u32[]{:S(2)}) copy-start(bf16[1,512,1024]{2,1,0:T(8,128)(2,1)} %copy-done.5) | copy-start | bytes 3145732
  124.3 28.6 %copy-start.11 = (bf16[4,8192]{1,0:T(4,128)(2,1)S(1)}, bf16[4,8192]{1,0:T(4,128)(2,1)}, u32[]{:S(2)}) copy-start(bf16[4,8192]{1,0:T(4,128)(2,1)} %param.8) | copy-start | bytes 196612
  124.3 28.6 %copy-start.12 = (f32[4]{0:T(128)S(1)}, f32[4]{0:T(128)}, u32[]{:S(2)}) copy-start(f32[4]{0:T(128)} %param.10) | copy-start | bytes 52

commit v6 on v5

--- a/solution.py
+++ b/solution.py
@@ -13,12 +13,13 @@
 
 def _exchange_kernel(axis, gather, x_ref, y_ref, land, send_sem, recv_sem, local_sem):
     count = land.shape[0]
-    me = lax.axis_index(axis)
+    me = lax.rem(lax.axis_index(axis), count)
+    base = lax.axis_index(axis) - me
     barrier = pltpu.get_barrier_semaphore()
 
     def greet(step, carry):
         peer = lax.rem(me + step, count)
-        pl.semaphore_signal(barrier, 1, device_id={axis: peer}, device_id_type=MESH)
+        pl.semaphore_signal(barrier, 1, device_id={axis: base + peer}, device_id_type=MESH)
         return carry
 
     lax.fori_loop(1, count, greet, 0)
@@ -30,12 +31,12 @@
     def outgoing(peer):
         return pltpu.make_async_remote_copy(
             src_ref=piece(peer), dst_ref=land.at[me], send_sem=send_sem.at[peer],
-            recv_sem=recv_sem.at[me], device_id={axis: peer}, device_id_type=MESH)
+            recv_sem=recv_sem.at[me], device_id={axis: base + peer}, device_id_type=MESH)
 
     def incoming(source):
         return pltpu.make_async_remote_copy(
             src_ref=piece(source), dst_ref=land.at[source], send_sem=send_sem.at[source],
-            recv_sem=recv_sem.at[source], device_id={axis: source}, device_id_type=MESH)
+            recv_sem=recv_sem.at[source], device_id={axis: base + source}, device_id_type=MESH)
 
     def send(step, carry):
         outgoing(lax.rem(me + step, count)).start()
@@ -56,7 +57,7 @@
 
 
 def exchange(x, axis, gather, collective):
-    count = lax.axis_size(axis)
+    count = lax.axis_size(axis) if gather else x.shape[0]
     chunk = x.shape if gather else x.shape[1:]
     full = (count,) + tuple(chunk)
     return pl.pallas_call(
@@ -106,28 +107,35 @@
     length_all = block_order * block_order
     ctx_count = lax.axis_size("ctx")
     tp_count = lax.axis_size("tp")
-    slab_width = block_order // ctx_count
+    halves = 2
+    group = ctx_count // halves
+    slab = block_order // group
+    freq_rows = block_order // ctx_count
+    half_freqs = block_order // halves
     rows_here = tokens // block_order
     half_rows = block_order // 2
     ctx_index = lax.axis_index("ctx")
+    half_index = ctx_index // group
+    group_index = ctx_index - half_index * group
     product = (k_feature.astype(jnp.float32) * v_feature.astype(jnp.float32)).astype(jnp.bfloat16)
     cosine_full, sine_full = fourier_tables(block_order)
-    cosine_half = cosine_full[:half_rows]
-    sine_half = sine_full[:half_rows]
+    both_full = jnp.stack([cosine_full, sine_full])
+    both_sub = lax.dynamic_slice_in_dim(both_full[:, :half_rows], half_index * half_freqs, half_freqs, 2)
+    my_freqs = half_index * half_freqs + jnp.arange(half_freqs, dtype=jnp.int32)
+    my_columns = group_index * slab + jnp.arange(slab, dtype=jnp.int32)
+    local_ticks = ctx_index * freq_rows + jnp.arange(freq_rows, dtype=jnp.int32)
     positions = jnp.arange(block_order, dtype=jnp.int32)
-    local_ticks = ctx_index * slab_width + jnp.arange(slab_width, dtype=jnp.int32)
-
-    outgoing = product.reshape(channels, rows_here, ctx_count, slab_width).transpose(2, 0, 1, 3)
+
+    outgoing = product.reshape(channels, rows_here, group, slab).transpose(2, 0, 1, 3)
+    outgoing = jnp.broadcast_to(outgoing[None], (halves,) + outgoing.shape)
     arrived = exchange(outgoing.reshape(ctx_count, channels, -1), "ctx", False, 0)
     grid_rows = (
-        arrived.reshape(ctx_count, channels, rows_here, slab_width)
+        arrived.reshape(ctx_count, channels, rows_here, slab)
         .transpose(1, 0, 2, 3)
-        .reshape(channels, half_rows, slab_width)
-    )
-    both_full = jnp.stack([cosine_full, sine_full])
-    both_half = jnp.stack([cosine_half, sine_half])
-    first = contract("sia,cij->scaj", both_half, grid_rows)
-    twist_cosine, twist_sine = twist_tables(positions, local_ticks, length_all)
+        .reshape(channels, half_rows, slab)
+    )
+    first = contract("sia,cij->scaj", both_sub, grid_rows)
+    twist_cosine, twist_sine = twist_tables(my_freqs, my_columns, length_all)
     spread = jnp.stack(
         [
             first[0] * twist_cosine - first[1] * twist_sine,
@@ -135,12 +143,12 @@
         ]
     ).astype(jnp.bfloat16)
 
-    outgoing = spread.reshape(2, channels, ctx_count, slab_width, slab_width).transpose(2, 0, 1, 3, 4)
-    arrived = exchange(outgoing.reshape(ctx_count, -1, 128), "ctx", False, 1)
+    outgoing = spread.reshape(2, channels, group, freq_rows, slab).transpose(2, 0, 1, 3, 4)
+    arrived = exchange(outgoing.reshape(group, -1, 128), "ctx", False, 1)
     block = (
-        arrived.reshape(ctx_count, 2, channels, slab_width, slab_width)
+        arrived.reshape(group, 2, channels, freq_rows, slab)
         .transpose(1, 2, 3, 0, 4)
-        .reshape(2, channels, slab_width, block_order)
+        .reshape(2, channels, freq_rows, block_order)
     )
     freq = contract("rcaj,sjb->srcab", block, both_full)
     freq_real = freq[0, 0] + freq[1, 1]
@@ -164,23 +172,25 @@
         ]
     ).astype(jnp.bfloat16)
 
-    outgoing = back.reshape(2, channels, slab_width, ctx_count, slab_width).transpose(3, 0, 1, 2, 4)
-    arrived = exchange(outgoing.reshape(ctx_count, -1, 128), "ctx", False, 2)
+    outgoing = back.reshape(2, channels, freq_rows, group, slab).transpose(3, 0, 1, 2, 4)
+    arrived = exchange(outgoing.reshape(group, -1, 128), "ctx", False, 2)
     columns = (
-        arrived.reshape(ctx_count, 2, channels, slab_width, slab_width)
+        arrived.reshape(group, 2, channels, freq_rows, slab)
         .transpose(1, 2, 0, 3, 4)
-        .reshape(2, channels, block_order, slab_width)
-    )
-    parts = contract("sia,rcaj->srcij", both_half, columns)
-    summed = parts[0, 0] - parts[1, 1]
-    spatial = (summed * (1.0 / length_all)).astype(jnp.bfloat16)
-
-    outgoing = spatial.reshape(channels, ctx_count, rows_here, slab_width).transpose(1, 0, 2, 3)
+        .reshape(2, channels, half_freqs, slab)
+    )
+    parts = contract("sia,rcaj->srcij", both_sub, columns)
+    partial = ((parts[0, 0] - parts[1, 1]) * (1.0 / length_all)).astype(jnp.bfloat16)
+
+    outgoing = partial.reshape(channels, ctx_count, rows_here, slab).transpose(1, 0, 2, 3)
     arrived = exchange(outgoing.reshape(ctx_count, channels, -1), "ctx", False, 3)
     convolved = (
-        arrived.reshape(ctx_count, channels, rows_here, slab_width)
+        arrived.reshape(halves, group, channels, rows_here, slab)
+        .astype(jnp.float32)
+        .sum(0)
         .transpose(1, 2, 0, 3)
         .reshape(channels, tokens)
+        .astype(jnp.bfloat16)
     )
     gated_rows = (
         q_feature.astype(jnp.float32)

time: 186 us -> 152 us (0.82)
  the two profiles are of different devices: /device:TPU:64 before, /device:TPU:70 now
where the time goes in v6:
time: 152 us; the launch traced here: 151 us
  Pallas kernels  108 us (71%)
  local copies, waits for them, and re-layouts  26.2 us (17%)
  other arithmetic  9.31 us (6%)
  matrix products  7.77 us (5%)
    pallas_call x5, Pallas kernels, exchange(): pl.pallas_call(functools.partial(_exchange_kernel, axis, gather), out_sha...  108 us
    dot_general x4, matrix products, contract(): return jnp.einsum(form, left, right, preferred_element_type=jnp.float32)  6.79 us
    reshape x3, local copies, waits for them, and re-layouts, local(): arrived.reshape(group, 2, channels, freq_rows, slab)  3.75 us
    unnamed x22, local copies, waits for them, and re-layouts  3.47 us
    another operation x3, other arithmetic  3.11 us

profile of v6, /device:TPU:70, one launch (start us, length us, event | category | flops | bytes accessed | tf_op | source)
XLA Modules:
  0.0 151.5 jit_solution(16601752348772904303)
XLA Ops:
  0.0 0.6 fusion.47
  0.6 0.5 fusion.44
  1.1 1.4 add_convert_fusion
  2.6 0.3 pad_slice_fusion
  2.8 1.0 copy-done.2
  3.9 0.7 copy-done.4
  4.6 1.6 %pad_slice_fusion.1 = bf16[2,512,1024]{2,1,0:T(8,128)(2,1)} fusion(bf16[1,1024,1024]{2,1,0:T(8,128)(2,1)S(1)} %bitcast.96), kind=kLoop, calls=%fused_computation.3 | loop fusion | bytes 4194304 | tf_op jit(solution)/shard_map/slice | solution.py:123
  6.2 0.2 reshape.439
  6.7 1.0 reshape.440.x_ref
  7.7 24.7 %shard_map.64 = bf16[64,4,256]{2,1,0:T(4,128)(2,1)} custom-call(bf16[64,4,256]{2,1,0:T(4,128)(2,1)} %reshape.440.x_ref), custom_call_target="tpu_custom_call" | custom-call | tf_op jit(solution)/shard_map/pallas_call | solution.py:63
  32.4 1.1 copy.36
  33.5 0.3 copy.37
  33.9 1.7 %convolution_bitcast_fusion.1 = f32[2,4,512,32]{2,3,0,1:T(8,128)S(1)} fusion(bf16[4,64,8,32]{3,2,1,0:T(8,128)(2,1)S(1)} %copy.37, bf16[2,512,1024]{2,1,0:T(8,128)(2,1)S(1)} %pad_slice_fusion, s32[]{:T(128)S(6)} %select_n.71, bf16[2,512,1024]{2,1,0:T(8,128)(2,1)} %pad_slice_fusion.1), kind=kOutput, calls=%fused_computation.12 | convolution fusion | flops 136314880 | bytes 3145732 | tf_op jit(solution)/shard_map/sia,cij->scaj/dot_general | solution.py:101
  35.6 0.3 fusion.49
  36.0 0.3 copy.39
  36.3 0.3 copy.40
  36.6 0.2 maximum_bitcast_fusion
  36.9 0.3 copy.41
  37.2 1.2 reshape.443.x_ref
  38.4 13.8 %shard_map.65 = bf16[32,32,128]{2,1,0:T(8,128)(2,1)} custom-call(bf16[32,32,128]{2,1,0:T(8,128)(2,1)} %reshape.443.x_ref), custom_call_target="tpu_custom_call" | custom-call | tf_op jit(solution)/shard_map/pallas_call | solution.py:63
  52.2 1.7 %reshape.444 = bf16[32,2,4,16,32]{4,3,2,1,0:T(8,128)(2,1)S(1)} reshape(bf16[32,32,128]{2,1,0:T(8,128)(2,1)} %shard_map.65) | data formatting | bytes 524288 | tf_op jit(solution)/shard_map/reshape | solution.py:149
  53.9 1.7 %copy.42 = bf16[2,4,16,32,32]{4,3,2,1,0:T(8,128)(2,1)} copy(bf16[2,4,16,32,32]{4,2,1,0,3:T(8,128)(2,1)S(1)} %bitcast.100) | data formatting | bytes 524288 | tf_op jit(solution)/shard_map/transpose | solution.py:150
  55.6 2.3 %reshape.455 = bf16[2,4,16,1024,1]{3,2,1,0,4:T(8,128)(2,1)S(1)} reshape(bf16[2,4,16,32,32]{4,3,2,1,0:T(8,128)(2,1)} %copy.42) | data formatting | bytes 524288 | tf_op jit(solution)/shard_map/reshape | solution.py:151
  57.9 3.1 %fusion.5 = f32[2,2,4,16,1024]{4,3,2,1,0:T(8,128)S(1)} fusion(bf16[2,4,16,1024,1]{3,2,1,0,4:T(8,128)(2,1)S(1)} %reshape.455, bf16[1,1024,1024]{2,1,0:T(8,128)(2,1)} %bitcast.94, bf16[1,1024,1024]{2,1,0:T(8,128)(2,1)} %bitcast.97), kind=kOutput, calls=%fused_computation.9 | convolution fusion | flops 545259520 | bytes 5505024 | tf_op jit(solution)/shard_map/rcaj,sjb->srcab/dot_general | solution.py:101
  61.2 0.3 copy-done.5
  61.5 0.7 fusion.8
  62.2 0.8 slice_subtract_fusion.1
  63.0 1.3 add.171
  64.3 1.3 sub.82
  65.6 1.1 fusion.34
  66.7 2.9 %subtract_convert_fusion.1 = (bf16[1,4,16,32,32]{4,2,1,0,3:T(8,128)(2,1)S(1)}, bf16[1,4,16,32,32]{4,2,1,0,3:T(8,128)(2,1)S(1)}) fusion(f32[1,4,16,32,32]{4,3,2,1,0:T(8,128)S(1)} %add.171, f32[1,4,16,32,32]{4,3,2,1,0:T(8,128)} %sub.82, f32[16,32,32]{2,0,1:T(8,128)S(1)} %get-tuple-element.20, f32[16,32,32]{2,0,1:T(8,128)S(1)} %get-tuple-element.19), kind=kLoop, calls=%fused_computation.19 | loop fusion | flops 524288 | bytes 917504 | tf_op jit(solution)/shard_map/convert.3
  69.6 0.2 maximum_bitcast_fusion.1
  69.8 1.2 reshape.446.x_ref
  71.0 12.4 %shard_map.66 = bf16[32,32,128]{2,1,0:T(8,128)(2,1)} custom-call(bf16[32,32,128]{2,1,0:T(8,128)(2,1)} %reshape.446.x_ref), custom_call_target="tpu_custom_call" | custom-call | tf_op jit(solution)/shard_map/pallas_call | solution.py:63
  83.5 1.9 %reshape.447 = bf16[32,2,4,16,32]{4,3,2,1,0:T(8,128)(2,1)S(1)} reshape(bf16[32,32,128]{2,1,0:T(8,128)(2,1)} %shard_map.66) | data formatting | bytes 524288 | tf_op jit(solution)/shard_map/reshape | solution.py:178
  85.6 1.4 copy-done.1
  87.0 1.2 convolution_bitcast_fusion
  88.3 0.3 copy.49
  88.5 0.4 copy.50
  88.9 0.8 copy.51.x_ref
  89.7 23.0 %shard_map.67 = bf16[64,4,256]{2,1,0:T(4,128)(2,1)} custom-call(bf16[64,4,256]{2,1,0:T(4,128)(2,1)} %copy.51.x_ref), custom_call_target="tpu_custom_call" | custom-call | tf_op jit(solution)/shard_map/pallas_call | solution.py:63
  112.8 1.2 convert_element_type.137
  114.2 0.3 copy.52
  114.5 0.3 reshape.451
  114.8 0.7 multiply_convert_fusion.x_ref
  115.6 33.8 %shard_map.68 = bf16[8,4,8192]{2,1,0:T(4,128)(2,1)} custom-call(bf16[4,8192]{1,0:T(4,128)(2,1)} %multiply_convert_fusion.x_ref), custom_call_target="tpu_custom_call" | custom-call | tf_op jit(solution)/shard_map/pallas_call | solution.py:63
  149.3 1.2 reshape.450
  150.5 1.0 convolution_convert_fusion
  (32 shorter events, 0.9 us)
Async XLA Ops:
  0.0 150.5 %copy-start = (bf16[32,64]{1,0:T(8,128)(2,1)S(1)}, bf16[32,64]{1,0:T(8,128)(2,1)}, u32[]{:S(2)}) copy-start(bf16[32,64]{1,0:T(8,128)(2,1)} %param.11) | copy-start | bytes 12292
  2.5 1.3 copy-start.2
  2.5 2.0 %copy-start.4 = (bf16[32,32,1024]{2,1,0:T(8,128)(2,1)}, bf16[32,32,1024]{2,1,0:T(8,128)(2,1)S(1)}, u32[]{:S(2)}) copy-start(bf16[32,32,1024]{2,1,0:T(8,128)(2,1)S(1)} %get-tuple-element.18) | copy-start | bytes 6291460
  4.6 1.6 %copy-start.7 = (bf16[4,8192]{1,0:T(4,128)(2,1)S(1)}, bf16[4,8192]{1,0:T(4,128)(2,1)}, u32[]{:S(2)}) copy-start(bf16[4,8192]{1,0:T(4,128)(2,1)} %param.7) | copy-start | bytes 196612
  4.6 1.6 %copy-start.8 = (bf16[4,8192]{1,0:T(4,128)(2,1)S(1)}, bf16[4,8192]{1,0:T(4,128)(2,1)}, u32[]{:S(2)}) copy-start(bf16[4,8192]{1,0:T(4,128)(2,1)} %param.6) | copy-start | bytes 196612
  57.9 3.1 %copy-start.6 = (bf16[2,4,16,1024]{3,2,1,0:T(8,128)(2,1)S(1)}, bf16[2,4,16,1024]{3,2,1,0:T(8,128)(2,1)}, u32[]{:S(2)}) copy-start(bf16[2,4,16,1024]{3,2,1,0:T(8,128)(2,1)} %param.9) | copy-start | bytes 786436
  57.9 3.3 %copy-start.3 = (bf16[32,32,1024]{2,1,0:T(8,128)(2,1)S(1)}, bf16[32,32,1024]{2,1,0:T(8,128)(2,1)}, u32[]{:S(2)}) copy-start(bf16[32,32,1024]{2,1,0:T(8,128)(2,1)} %copy-done.2) | copy-start | bytes 6291460
  57.9 3.6 %copy-start.5 = (bf16[32,32,1024]{2,1,0:T(8,128)(2,1)S(1)}, bf16[32,32,1024]{2,1,0:T(8,128)(2,1)}, u32[]{:S(2)}) copy-start(bf16[32,32,1024]{2,1,0:T(8,128)(2,1)} %copy-done.4) | copy-start | bytes 6291460
  85.4 1.6 %copy-start.1 = (bf16[2,512,1024]{2,1,0:T(8,128)(2,1)S(1)}, bf16[2,512,1024]{2,1,0:T(8,128)(2,1)}, u32[]{:S(2)}) copy-start(bf16[2,512,1024]{2,1,0:T(8,128)(2,1)} %pad_slice_fusion.1) | copy-start | bytes 6291460
  89.7 25.1 %copy-start.9 = (bf16[4,8192]{1,0:T(4,128)(2,1)S(1)}, bf16[4,8192]{1,0:T(4,128)(2,1)}, u32[]{:S(2)}) copy-start(bf16[4,8192]{1,0:T(4,128)(2,1)} %param.8) | copy-start | bytes 196612
  89.7 25.1 %copy-start.10 = (f32[4]{0:T(128)S(1)}, f32[4]{0:T(128)}, u32[]{:S(2)}) copy-start(f32[4]{0:T(128)} %param.10) | copy-start | bytes 52

commit v7 on v6

--- a/solution.py
+++ b/solution.py
@@ -26,7 +26,7 @@
     pl.semaphore_wait(barrier, count - 1)
 
     def piece(peer):
-        return x_ref if gather else x_ref.at[peer]
+        return x_ref if gather else x_ref.at[lax.rem(peer, x_ref.shape[0])]
 
     def outgoing(peer):
         return pltpu.make_async_remote_copy(
@@ -56,8 +56,8 @@
     y_ref[...] = land[...]
 
 
-def exchange(x, axis, gather, collective):
-    count = lax.axis_size(axis) if gather else x.shape[0]
+def exchange(x, axis, gather, collective, count=None):
+    count = count or (lax.axis_size(axis) if gather else x.shape[0])
     chunk = x.shape if gather else x.shape[1:]
     full = (count,) + tuple(chunk)
     return pl.pallas_call(
@@ -127,8 +127,7 @@
     positions = jnp.arange(block_order, dtype=jnp.int32)
 
     outgoing = product.reshape(channels, rows_here, group, slab).transpose(2, 0, 1, 3)
-    outgoing = jnp.broadcast_to(outgoing[None], (halves,) + outgoing.shape)
-    arrived = exchange(outgoing.reshape(ctx_count, channels, -1), "ctx", False, 0)
+    arrived = exchange(outgoing.reshape(group, channels, -1), "ctx", False, 0, ctx_count)
     grid_rows = (
         arrived.reshape(ctx_count, channels, rows_here, slab)
         .transpose(1, 0, 2, 3)

time: 152 us -> 152 us (level)
  no operation moved by 1% of the time
where the time goes in v7:
time: 152 us; the launch traced here: 151 us
  Pallas kernels  108 us (71%)
  local copies, waits for them, and re-layouts  26 us (17%)
  other arithmetic  9.31 us (6%)
  matrix products  7.77 us (5%)
    pallas_call x5, Pallas kernels, exchange(): pl.pallas_call(functools.partial(_exchange_kernel, axis, gather), out_sha...  108 us
    dot_general x4, matrix products, contract(): return jnp.einsum(form, left, right, preferred_element_type=jnp.float32)  6.8 us
    reshape x3, local copies, waits for them, and re-layouts, local(): arrived.reshape(group, 2, channels, freq_rows, slab)  3.75 us
    unnamed x22, local copies, waits for them, and re-layouts  3.47 us
    another operation x3, other arithmetic  3.11 us

profile of v7, /device:TPU:70, one launch (start us, length us, event | category | flops | bytes accessed | tf_op | source)
XLA Modules:
  0.0 151.2 jit_solution(18367620383901295751)
XLA Ops:
  0.0 0.6 fusion.47
  0.6 0.5 fusion.44
  1.1 1.4 add_convert_fusion
  2.6 0.3 pad_slice_fusion
  2.8 1.0 copy-done.2
  3.9 0.7 copy-done.4
  4.6 1.6 %pad_slice_fusion.1 = bf16[2,512,1024]{2,1,0:T(8,128)(2,1)} fusion(bf16[1,1024,1024]{2,1,0:T(8,128)(2,1)S(1)} %bitcast.96), kind=kLoop, calls=%fused_computation.3 | loop fusion | bytes 4194304 | tf_op jit(solution)/shard_map/slice | solution.py:123
  6.2 0.2 reshape.438
  6.6 0.8 reshape.439.x_ref
  7.4 24.7 %shard_map.64 = bf16[64,4,256]{2,1,0:T(4,128)(2,1)} custom-call(bf16[32,4,256]{2,1,0:T(4,128)(2,1)} %reshape.439.x_ref), custom_call_target="tpu_custom_call" | custom-call | tf_op jit(solution)/shard_map/pallas_call | solution.py:63
  32.1 1.1 copy.36
  33.2 0.3 copy.37
  33.5 1.7 %convolution_bitcast_fusion.1 = f32[2,4,512,32]{2,3,0,1:T(8,128)S(1)} fusion(bf16[4,64,8,32]{3,2,1,0:T(8,128)(2,1)S(1)} %copy.37, bf16[2,512,1024]{2,1,0:T(8,128)(2,1)S(1)} %pad_slice_fusion, s32[]{:T(128)S(6)} %select_n.71, bf16[2,512,1024]{2,1,0:T(8,128)(2,1)} %pad_slice_fusion.1), kind=kOutput, calls=%fused_computation.12 | convolution fusion | flops 136314880 | bytes 3145732 | tf_op jit(solution)/shard_map/sia,cij->scaj/dot_general | solution.py:101
  35.3 0.3 fusion.49
  35.7 0.3 copy.39
  36.0 0.3 copy.40
  36.3 0.2 maximum_bitcast_fusion
  36.5 0.3 copy.41
  36.8 1.2 reshape.442.x_ref
  38.0 13.8 %shard_map.65 = bf16[32,32,128]{2,1,0:T(8,128)(2,1)} custom-call(bf16[32,32,128]{2,1,0:T(8,128)(2,1)} %reshape.442.x_ref), custom_call_target="tpu_custom_call" | custom-call | tf_op jit(solution)/shard_map/pallas_call | solution.py:63
  51.9 1.7 %reshape.443 = bf16[32,2,4,16,32]{4,3,2,1,0:T(8,128)(2,1)S(1)} reshape(bf16[32,32,128]{2,1,0:T(8,128)(2,1)} %shard_map.65) | data formatting | bytes 524288 | tf_op jit(solution)/shard_map/reshape | solution.py:148
  53.5 1.7 %copy.42 = bf16[2,4,16,32,32]{4,3,2,1,0:T(8,128)(2,1)} copy(bf16[2,4,16,32,32]{4,2,1,0,3:T(8,128)(2,1)S(1)} %bitcast.100) | data formatting | bytes 524288 | tf_op jit(solution)/shard_map/transpose | solution.py:149
  55.2 2.3 %reshape.454 = bf16[2,4,16,1024,1]{3,2,1,0,4:T(8,128)(2,1)S(1)} reshape(bf16[2,4,16,32,32]{4,3,2,1,0:T(8,128)(2,1)} %copy.42) | data formatting | bytes 524288 | tf_op jit(solution)/shard_map/reshape | solution.py:150
  57.6 3.1 %fusion.5 = f32[2,2,4,16,1024]{4,3,2,1,0:T(8,128)S(1)} fusion(bf16[2,4,16,1024,1]{3,2,1,0,4:T(8,128)(2,1)S(1)} %reshape.454, bf16[1,1024,1024]{2,1,0:T(8,128)(2,1)} %bitcast.94, bf16[1,1024,1024]{2,1,0:T(8,128)(2,1)} %bitcast.97), kind=kOutput, calls=%fused_computation.9 | convolution fusion | flops 545259520 | bytes 5505024 | tf_op jit(solution)/shard_map/rcaj,sjb->srcab/dot_general | solution.py:101
  60.8 0.3 copy-done.5
  61.1 0.7 fusion.8
  61.9 0.8 slice_subtract_fusion.1
  62.6 1.3 add.171
  63.9 1.3 sub.82
  65.2 1.1 fusion.34
  66.3 2.9 %subtract_convert_fusion.1 = (bf16[1,4,16,32,32]{4,2,1,0,3:T(8,128)(2,1)S(1)}, bf16[1,4,16,32,32]{4,2,1,0,3:T(8,128)(2,1)S(1)}) fusion(f32[1,4,16,32,32]{4,3,2,1,0:T(8,128)S(1)} %add.171, f32[1,4,16,32,32]{4,3,2,1,0:T(8,128)} %sub.82, f32[16,32,32]{2,0,1:T(8,128)S(1)} %get-tuple-element.20, f32[16,32,32]{2,0,1:T(8,128)S(1)} %get-tuple-element.19), kind=kLoop, calls=%fused_computation.19 | loop fusion | flops 524288 | bytes 917504 | tf_op jit(solution)/shard_map/convert.3
  69.2 0.2 maximum_bitcast_fusion.1
  69.5 1.2 reshape.445.x_ref
  70.7 12.4 %shard_map.66 = bf16[32,32,128]{2,1,0:T(8,128)(2,1)} custom-call(bf16[32,32,128]{2,1,0:T(8,128)(2,1)} %reshape.445.x_ref), custom_call_target="tpu_custom_call" | custom-call | tf_op jit(solution)/shard_map/pallas_call | solution.py:63
  83.1 1.9 %reshape.446 = bf16[32,2,4,16,32]{4,3,2,1,0:T(8,128)(2,1)S(1)} reshape(bf16[32,32,128]{2,1,0:T(8,128)(2,1)} %shard_map.66) | data formatting | bytes 524288 | tf_op jit(solution)/shard_map/reshape | solution.py:177
  85.2 1.4 copy-done.1
  86.6 1.2 convolution_bitcast_fusion
  87.9 0.3 copy.49
  88.2 0.4 copy.50
  88.6 0.8 copy.51.x_ref
  89.4 23.0 %shard_map.67 = bf16[64,4,256]{2,1,0:T(4,128)(2,1)} custom-call(bf16[64,4,256]{2,1,0:T(4,128)(2,1)} %copy.51.x_ref), custom_call_target="tpu_custom_call" | custom-call | tf_op jit(solution)/shard_map/pallas_call | solution.py:63
  112.4 1.2 convert_element_type.137
  113.9 0.3 copy.52
  114.2 0.3 reshape.450
  114.5 0.7 multiply_convert_fusion.x_ref
  115.2 33.8 %shard_map.68 = bf16[8,4,8192]{2,1,0:T(4,128)(2,1)} custom-call(bf16[4,8192]{1,0:T(4,128)(2,1)} %multiply_convert_fusion.x_ref), custom_call_target="tpu_custom_call" | custom-call | tf_op jit(solution)/shard_map/pallas_call | solution.py:63
  149.0 1.2 reshape.449
  150.2 1.0 convolution_convert_fusion
  (31 shorter events, 0.8 us)
Async XLA Ops:
  0.0 150.2 %copy-start = (bf16[32,64]{1,0:T(8,128)(2,1)S(1)}, bf16[32,64]{1,0:T(8,128)(2,1)}, u32[]{:S(2)}) copy-start(bf16[32,64]{1,0:T(8,128)(2,1)} %param.11) | copy-start | bytes 12292
  2.5 1.3 copy-start.2
  2.5 2.0 %copy-start.4 = (bf16[32,32,1024]{2,1,0:T(8,128)(2,1)}, bf16[32,32,1024]{2,1,0:T(8,128)(2,1)S(1)}, u32[]{:S(2)}) copy-start(bf16[32,32,1024]{2,1,0:T(8,128)(2,1)S(1)} %get-tuple-element.18) | copy-start | bytes 6291460
  4.6 1.6 %copy-start.7 = (bf16[4,8192]{1,0:T(4,128)(2,1)S(1)}, bf16[4,8192]{1,0:T(4,128)(2,1)}, u32[]{:S(2)}) copy-start(bf16[4,8192]{1,0:T(4,128)(2,1)} %param.7) | copy-start | bytes 196612
  4.6 1.6 %copy-start.8 = (bf16[4,8192]{1,0:T(4,128)(2,1)S(1)}, bf16[4,8192]{1,0:T(4,128)(2,1)}, u32[]{:S(2)}) copy-start(bf16[4,8192]{1,0:T(4,128)(2,1)} %param.6) | copy-start | bytes 196612
  57.5 3.1 %copy-start.6 = (bf16[2,4,16,1024]{3,2,1,0:T(8,128)(2,1)S(1)}, bf16[2,4,16,1024]{3,2,1,0:T(8,128)(2,1)}, u32[]{:S(2)}) copy-start(bf16[2,4,16,1024]{3,2,1,0:T(8,128)(2,1)} %param.9) | copy-start | bytes 786436
  57.6 3.3 %copy-start.3 = (bf16[32,32,1024]{2,1,0:T(8,128)(2,1)S(1)}, bf16[32,32,1024]{2,1,0:T(8,128)(2,1)}, u32[]{:S(2)}) copy-start(bf16[32,32,1024]{2,1,0:T(8,128)(2,1)} %copy-done.2) | copy-start | bytes 6291460
  57.6 3.6 %copy-start.5 = (bf16[32,32,1024]{2,1,0:T(8,128)(2,1)S(1)}, bf16[32,32,1024]{2,1,0:T(8,128)(2,1)}, u32[]{:S(2)}) copy-start(bf16[32,32,1024]{2,1,0:T(8,128)(2,1)} %copy-done.4) | copy-start | bytes 6291460
  85.0 1.6 %copy-start.1 = (bf16[2,512,1024]{2,1,0:T(8,128)(2,1)S(1)}, bf16[2,512,1024]{2,1,0:T(8,128)(2,1)}, u32[]{:S(2)}) copy-start(bf16[2,512,1024]{2,1,0:T(8,128)(2,1)} %pad_slice_fusion.1) | copy-start | bytes 6291460
  89.4 25.1 %copy-start.9 = (bf16[4,8192]{1,0:T(4,128)(2,1)S(1)}, bf16[4,8192]{1,0:T(4,128)(2,1)}, u32[]{:S(2)}) copy-start(bf16[4,8192]{1,0:T(4,128)(2,1)} %param.8) | copy-start | bytes 196612
  89.4 25.1 %copy-start.10 = (f32[4]{0:T(128)S(1)}, f32[4]{0:T(128)}, u32[]{:S(2)}) copy-start(f32[4]{0:T(128)} %param.10) | copy-start | bytes 52

commit v8 on v7

--- a/solution.py
+++ b/solution.py
@@ -171,6 +171,7 @@
         ]
     ).astype(jnp.bfloat16)
 
+    back = lax.optimization_barrier(back)
     outgoing = back.reshape(2, channels, freq_rows, group, slab).transpose(3, 0, 1, 2, 4)
     arrived = exchange(outgoing.reshape(group, -1, 128), "ctx", False, 2)
     columns = (

time: 152 us -> 148 us (0.974)
  other arithmetic: 9.31 us -> 4.81 us
    another operation x3 -> x4, other arithmetic: 3.11 us -> 0.35 us
    reshape x0 -> x2, local copies, waits for them, and re-layouts: none -> 2.15 us  [local(): back.reshape(2, channels, freq_rows, group, slab).transpose(3, 0, 1, 2, 4)]
where the time goes in v8:
time: 148 us; the launch traced here: 147 us
  Pallas kernels  108 us (73%)
  local copies, waits for them, and re-layouts  26.6 us (18%)
  matrix products  7.78 us (5%)
  other arithmetic  4.81 us (3%)
    pallas_call x5, Pallas kernels, exchange(): pl.pallas_call(functools.partial(_exchange_kernel, axis, gather), out_sha...  108 us
    dot_general x4, matrix products, contract(): return jnp.einsum(form, left, right, preferred_element_type=jnp.float32)  6.8 us
    reshape x3, local copies, waits for them, and re-layouts, local(): arrived.reshape(group, 2, channels, freq_rows, slab)  3.53 us
    unnamed x22, local copies, waits for them, and re-layouts  3.47 us

profile of v8, /device:TPU:70, one launch (start us, length us, event | category | flops | bytes accessed | tf_op | source)
XLA Modules:
  0.0 147.3 jit_solution(13573931278525302938)
XLA Ops:
  0.0 0.6 fusion.49
  0.6 0.5 fusion.46
  1.1 1.4 add_convert_fusion
  2.6 0.3 pad_slice_fusion
  2.8 1.0 copy-done.2
  3.9 0.7 copy-done.4
  4.6 1.6 %pad_slice_fusion.1 = bf16[2,512,1024]{2,1,0:T(8,128)(2,1)} fusion(bf16[1,1024,1024]{2,1,0:T(8,128)(2,1)S(1)} %bitcast.107), kind=kLoop, calls=%fused_computation.3 | loop fusion | bytes 4194304 | tf_op jit(solution)/shard_map/slice | solution.py:123
  6.2 0.2 reshape.406
  6.6 0.8 reshape.407.x_ref
  7.4 24.7 %shard_map.64 = bf16[64,4,256]{2,1,0:T(4,128)(2,1)} custom-call(bf16[32,4,256]{2,1,0:T(4,128)(2,1)} %reshape.407.x_ref), custom_call_target="tpu_custom_call" | custom-call | tf_op jit(solution)/shard_map/pallas_call | solution.py:63
  32.1 1.1 copy.30
  33.2 0.3 copy.31
  33.5 1.7 %convolution_bitcast_fusion.1 = f32[2,4,512,32]{2,3,0,1:T(8,128)S(1)} fusion(bf16[4,64,8,32]{3,2,1,0:T(8,128)(2,1)S(1)} %copy.31, bf16[2,512,1024]{2,1,0:T(8,128)(2,1)S(1)} %pad_slice_fusion, s32[]{:T(128)S(6)} %select_n.69, bf16[2,512,1024]{2,1,0:T(8,128)(2,1)} %pad_slice_fusion.1), kind=kOutput, calls=%fused_computation.12 | convolution fusion | flops 136314880 | bytes 3145732 | tf_op jit(solution)/shard_map/sia,cij->scaj/dot_general | solution.py:101
  35.3 0.3 fusion.54
  35.7 0.3 copy.33
  36.0 0.3 copy.34
  36.3 0.2 maximum_bitcast_fusion
  36.5 0.3 copy.35
  36.8 1.2 reshape.410.x_ref
  38.0 13.8 %shard_map.65 = bf16[32,32,128]{2,1,0:T(8,128)(2,1)} custom-call(bf16[32,32,128]{2,1,0:T(8,128)(2,1)} %reshape.410.x_ref), custom_call_target="tpu_custom_call" | custom-call | tf_op jit(solution)/shard_map/pallas_call | solution.py:63
  51.9 1.7 %reshape.411 = bf16[32,2,4,16,32]{4,3,2,1,0:T(8,128)(2,1)S(1)} reshape(bf16[32,32,128]{2,1,0:T(8,128)(2,1)} %shard_map.65) | data formatting | bytes 524288 | tf_op jit(solution)/shard_map/reshape | solution.py:148
  53.5 1.7 %copy.36 = bf16[2,4,16,32,32]{4,3,2,1,0:T(8,128)(2,1)} copy(bf16[2,4,16,32,32]{4,2,1,0,3:T(8,128)(2,1)S(1)} %bitcast.111) | data formatting | bytes 524288 | tf_op jit(solution)/shard_map/transpose | solution.py:149
  55.2 2.3 %reshape.423 = bf16[2,4,16,1024,1]{3,2,1,0,4:T(8,128)(2,1)S(1)} reshape(bf16[2,4,16,32,32]{4,3,2,1,0:T(8,128)(2,1)} %copy.36) | data formatting | bytes 524288 | tf_op jit(solution)/shard_map/reshape | solution.py:150
  57.6 3.1 %fusion.5 = f32[2,2,4,16,1024]{4,3,2,1,0:T(8,128)S(1)} fusion(bf16[2,4,16,1024,1]{3,2,1,0,4:T(8,128)(2,1)S(1)} %reshape.423, bf16[1,1024,1024]{2,1,0:T(8,128)(2,1)} %bitcast.105, bf16[1,1024,1024]{2,1,0:T(8,128)(2,1)} %bitcast.108), kind=kOutput, calls=%fused_computation.9 | convolution fusion | flops 545259520 | bytes 5505024 | tf_op jit(solution)/shard_map/rcaj,sjb->srcab/dot_general | solution.py:101
  60.7 0.1 fusion.15
  60.8 0.3 copy-done.5
  61.1 0.7 fusion.8
  61.9 0.3 fusion.52
  62.4 0.8 reshape.413
  63.1 1.4 copy.53
  64.5 2.5 %reshape.414.x_ref = bf16[32,32,128]{2,1,0:T(8,128)(2,1)} reshape(bf16[32,2,4,16,32]{4,3,2,1,0:T(8,128)(2,1)} %bitcast.112) | data formatting | bytes 524288 | tf_op jit(solution)/shard_map/reshape | solution.py:176
  67.0 12.5 %shard_map.66 = bf16[32,32,128]{2,1,0:T(8,128)(2,1)} custom-call(bf16[32,32,128]{2,1,0:T(8,128)(2,1)} %reshape.414.x_ref), custom_call_target="tpu_custom_call" | custom-call | tf_op jit(solution)/shard_map/pallas_call | solution.py:63
  79.5 1.7 %reshape.415 = bf16[32,2,4,16,32]{4,3,2,1,0:T(8,128)(2,1)S(1)} reshape(bf16[32,32,128]{2,1,0:T(8,128)(2,1)} %shard_map.66) | data formatting | bytes 524288 | tf_op jit(solution)/shard_map/reshape | solution.py:178
  81.2 0.2 copy.38
  81.4 1.4 copy-done.1
  82.8 1.2 convolution_bitcast_fusion
  84.1 0.3 copy.40
  84.4 0.4 copy.41
  84.7 0.8 copy.42.x_ref
  85.5 23.0 %shard_map.67 = bf16[64,4,256]{2,1,0:T(4,128)(2,1)} custom-call(bf16[64,4,256]{2,1,0:T(4,128)(2,1)} %copy.42.x_ref), custom_call_target="tpu_custom_call" | custom-call | tf_op jit(solution)/shard_map/pallas_call | solution.py:63
  108.6 1.2 convert_element_type.134
  109.8 0.1 reduce
  110.0 0.3 copy.43
  110.3 0.3 reshape.419
  110.6 0.7 multiply_convert_fusion.x_ref
  111.4 33.8 %shard_map.68 = bf16[8,4,8192]{2,1,0:T(4,128)(2,1)} custom-call(bf16[4,8192]{1,0:T(4,128)(2,1)} %multiply_convert_fusion.x_ref), custom_call_target="tpu_custom_call" | custom-call | tf_op jit(solution)/shard_map/pallas_call | solution.py:63
  145.2 1.2 reshape.418
  146.3 1.0 convolution_convert_fusion
  (29 shorter events, 0.5 us)
Async XLA Ops:
  0.0 146.3 %copy-start = (bf16[32,64]{1,0:T(8,128)(2,1)S(1)}, bf16[32,64]{1,0:T(8,128)(2,1)}, u32[]{:S(2)}) copy-start(bf16[32,64]{1,0:T(8,128)(2,1)} %param.11) | copy-start | bytes 12292
  2.5 1.3 copy-start.2
  2.5 2.0 %copy-start.4 = (bf16[32,32,1024]{2,1,0:T(8,128)(2,1)}, bf16[32,32,1024]{2,1,0:T(8,128)(2,1)S(1)}, u32[]{:S(2)}) copy-start(bf16[32,32,1024]{2,1,0:T(8,128)(2,1)S(1)} %get-tuple-element.16) | copy-start | bytes 6291460
  4.6 1.6 %copy-start.7 = (bf16[4,8192]{1,0:T(4,128)(2,1)S(1)}, bf16[4,8192]{1,0:T(4,128)(2,1)}, u32[]{:S(2)}) copy-start(bf16[4,8192]{1,0:T(4,128)(2,1)} %param.7) | copy-start | bytes 196612
  4.6 1.6 %copy-start.8 = (bf16[4,8192]{1,0:T(4,128)(2,1)S(1)}, bf16[4,8192]{1,0:T(4,128)(2,1)}, u32[]{:S(2)}) copy-start(bf16[4,8192]{1,0:T(4,128)(2,1)} %param.6) | copy-start | bytes 196612
  57.5 3.1 %copy-start.6 = (bf16[2,4,16,1024]{3,2,1,0:T(8,128)(2,1)S(1)}, bf16[2,4,16,1024]{3,2,1,0:T(8,128)(2,1)}, u32[]{:S(2)}) copy-start(bf16[2,4,16,1024]{3,2,1,0:T(8,128)(2,1)} %param.9) | copy-start | bytes 786436
  57.6 3.3 %copy-start.3 = (bf16[32,32,1024]{2,1,0:T(8,128)(2,1)S(1)}, bf16[32,32,1024]{2,1,0:T(8,128)(2,1)}, u32[]{:S(2)}) copy-start(bf16[32,32,1024]{2,1,0:T(8,128)(2,1)} %copy-done.2) | copy-start | bytes 6291460
  57.6 3.6 %copy-start.5 = (bf16[32,32,1024]{2,1,0:T(8,128)(2,1)S(1)}, bf16[32,32,1024]{2,1,0:T(8,128)(2,1)}, u32[]{:S(2)}) copy-start(bf16[32,32,1024]{2,1,0:T(8,128)(2,1)} %copy-done.4) | copy-start | bytes 6291460
  81.2 1.6 %copy-start.1 = (bf16[2,512,1024]{2,1,0:T(8,128)(2,1)S(1)}, bf16[2,512,1024]{2,1,0:T(8,128)(2,1)}, u32[]{:S(2)}) copy-start(bf16[2,512,1024]{2,1,0:T(8,128)(2,1)} %pad_slice_fusion.1) | copy-start | bytes 6291460
  85.5 25.1 %copy-start.9 = (bf16[4,8192]{1,0:T(4,128)(2,1)S(1)}, bf16[4,8192]{1,0:T(4,128)(2,1)}, u32[]{:S(2)}) copy-start(bf16[4,8192]{1,0:T(4,128)(2,1)} %param.8) | copy-start | bytes 196612
  85.5 25.1 %copy-start.10 = (f32[4]{0:T(128)S(1)}, f32[4]{0:T(128)}, u32[]{:S(2)}) copy-start(f32[4]{0:T(128)} %param.10) | copy-start | bytes 52

commit v9 on v8

--- a/solution.py
+++ b/solution.py
@@ -120,7 +120,7 @@
     product = (k_feature.astype(jnp.float32) * v_feature.astype(jnp.float32)).astype(jnp.bfloat16)
     cosine_full, sine_full = fourier_tables(block_order)
     both_full = jnp.stack([cosine_full, sine_full])
-    both_sub = lax.dynamic_slice_in_dim(both_full[:, :half_rows], half_index * half_freqs, half_freqs, 2)
+    both_sub = lax.dynamic_slice_in_dim(both_full, half_index * half_freqs, half_freqs, 1)[:, :, :half_rows]
     my_freqs = half_index * half_freqs + jnp.arange(half_freqs, dtype=jnp.int32)
     my_columns = group_index * slab + jnp.arange(slab, dtype=jnp.int32)
     local_ticks = ctx_index * freq_rows + jnp.arange(freq_rows, dtype=jnp.int32)
@@ -133,7 +133,7 @@
         .transpose(1, 0, 2, 3)
         .reshape(channels, half_rows, slab)
     )
-    first = contract("sia,cij->scaj", both_sub, grid_rows)
+    first = contract("sai,cij->scaj", both_sub, grid_rows)
     twist_cosine, twist_sine = twist_tables(my_freqs, my_columns, length_all)
     spread = jnp.stack(
         [
@@ -179,7 +179,7 @@
         .transpose(1, 2, 0, 3, 4)
         .reshape(2, channels, half_freqs, slab)
     )
-    parts = contract("sia,rcaj->srcij", both_sub, columns)
+    parts = contract("sai,rcaj->srcij", both_sub, columns)
     partial = ((parts[0, 0] - parts[1, 1]) * (1.0 / length_all)).astype(jnp.bfloat16)
 
     outgoing = partial.reshape(channels, ctx_count, rows_here, slab).transpose(1, 0, 2, 3)

time: 148 us -> 144 us (0.973)
  local copies, waits for them, and re-layouts: 26.6 us -> 22.6 us
    unnamed x22 -> x16, local copies, waits for them, and re-layouts: 3.47 us -> 1.43 us
    slice x2 -> x0, local copies, waits for them, and re-layouts: 1.87 us -> none  [local(): both_full[:, :half_rows]]
where the time goes in v9:
time: 144 us; the launch traced here: 143 us
  Pallas kernels  108 us (75%)
  local copies, waits for them, and re-layouts  22.6 us (16%)
  matrix products  6.78 us (5%)
  other arithmetic  6.05 us (4%)
    pallas_call x5, Pallas kernels, exchange(): pl.pallas_call(functools.partial(_exchange_kernel, axis, gather), out_sha...  108 us
    dot_general x4, matrix products, contract(): return jnp.einsum(form, left, right, preferred_element_type=jnp.float32)  5.8 us
    reshape x3, local copies, waits for them, and re-layouts, local(): arrived.reshape(group, 2, channels, freq_rows, slab)  3.53 us

profile of v9, /device:TPU:70, one launch (start us, length us, event | category | flops | bytes accessed | tf_op | source)
XLA Modules:
  0.0 143.5 jit_solution(15482807019310633095)
XLA Ops:
  0.0 0.6 fusion.50
  0.6 0.5 fusion.47
  1.1 0.0 copy-start.4
  1.2 2.6 %add_convert_fusion = (bf16[32,32,1024]{2,1,0:T(8,128)(2,1)S(1)}, bf16[32,32,1024]{2,1,0:T(8,128)(2,1)}) fusion(f32[32,1024]{1,0:T(8,128)S(1)} %get-tuple-element.23, f32[32,1024]{1,0:T(8,128)S(1)} %get-tuple-element.20, f32[32,1024]{1,0:T(8,128)S(1)} %get-tuple-element.24, f32[32,1024]{1,0:T(8,128)S(1)} %get-tuple-element.19), kind=kLoop, calls=%fused_computation.5 | loop fusion | flops 8388608 | bytes 4718592 | tf_op jit(solution)/shard_map/convert_element_type | solution.py:91
  3.9 0.2 reshape.406
  4.1 0.1 copy.29
  4.2 0.8 reshape.407.x_ref
  5.0 24.7 %shard_map.64 = bf16[64,4,256]{2,1,0:T(4,128)(2,1)} custom-call(bf16[32,4,256]{2,1,0:T(4,128)(2,1)} %reshape.407.x_ref), custom_call_target="tpu_custom_call" | custom-call | tf_op jit(solution)/shard_map/pallas_call | solution.py:63
  29.7 1.1 copy.30
  30.8 0.3 copy.31
  31.1 1.8 %convolution_bitcast_fusion.1 = f32[2,4,512,32]{2,3,0,1:T(8,128)S(1)} fusion(bf16[4,64,8,32]{3,2,1,0:T(8,128)(2,1)S(1)} %copy.31, s32[]{:T(128)S(6)} %select_n.69, bf16[1,1024,1024]{2,1,0:T(8,128)(2,1)} %bitcast.108, bf16[1,1024,1024]{2,1,0:T(8,128)(2,1)S(1)} %bitcast.104), kind=kOutput, calls=%fused_computation.12 | convolution fusion | flops 136314880 | bytes 4849668 | tf_op jit(solution)/shard_map/sai,cij->scaj/dot_general | solution.py:101
  32.9 0.3 fusion.55
  33.3 0.1 subtract_convert_fusion.3
  33.4 0.3 copy.33
  33.6 0.3 copy.34
  33.9 0.2 maximum_bitcast_fusion
  34.2 0.3 copy.35
  34.5 1.2 reshape.410.x_ref
  35.7 13.8 %shard_map.65 = bf16[32,32,128]{2,1,0:T(8,128)(2,1)} custom-call(bf16[32,32,128]{2,1,0:T(8,128)(2,1)} %reshape.410.x_ref), custom_call_target="tpu_custom_call" | custom-call | tf_op jit(solution)/shard_map/pallas_call | solution.py:63
  49.5 1.7 %reshape.411 = bf16[32,2,4,16,32]{4,3,2,1,0:T(8,128)(2,1)S(1)} reshape(bf16[32,32,128]{2,1,0:T(8,128)(2,1)} %shard_map.65) | data formatting | bytes 524288 | tf_op jit(solution)/shard_map/reshape | solution.py:148
  51.1 1.6 %copy.36 = bf16[2,4,16,32,32]{4,3,2,1,0:T(8,128)(2,1)} copy(bf16[2,4,16,32,32]{4,2,1,0,3:T(8,128)(2,1)S(1)} %bitcast.113) | data formatting | bytes 524288 | tf_op jit(solution)/shard_map/transpose | solution.py:149
  52.8 2.3 %reshape.423 = bf16[2,4,16,1024,1]{3,2,1,0,4:T(8,128)(2,1)S(1)} reshape(bf16[2,4,16,32,32]{4,3,2,1,0:T(8,128)(2,1)} %copy.36) | data formatting | bytes 524288 | tf_op jit(solution)/shard_map/reshape | solution.py:150
  55.1 2.8 %fusion.5 = f32[2,2,4,16,1024]{4,3,2,1,0:T(8,128)S(1)} fusion(bf16[2,4,16,1024,1]{3,2,1,0,4:T(8,128)(2,1)S(1)} %reshape.423, bf16[1,1024,1024]{2,1,0:T(8,128)(2,1)S(1)} %bitcast.105, bf16[1,1024,1024]{2,1,0:T(8,128)(2,1)} %bitcast.109), kind=kOutput, calls=%fused_computation.9 | convolution fusion | flops 545259520 | bytes 5505024 | tf_op jit(solution)/shard_map/rcaj,sjb->srcab/dot_general | solution.py:101
  57.9 0.1 fusion.16
  58.1 0.7 fusion.8
  58.8 0.3 fusion.53
  59.2 0.1 subtract_convert_fusion.1
  59.3 0.8 reshape.413
  60.1 1.4 copy.53
  61.5 2.5 %reshape.414.x_ref = bf16[32,32,128]{2,1,0:T(8,128)(2,1)} reshape(bf16[32,2,4,16,32]{4,3,2,1,0:T(8,128)(2,1)} %bitcast.114) | data formatting | bytes 524288 | tf_op jit(solution)/shard_map/reshape | solution.py:176
  64.0 12.4 %shard_map.66 = bf16[32,32,128]{2,1,0:T(8,128)(2,1)} custom-call(bf16[32,32,128]{2,1,0:T(8,128)(2,1)} %reshape.414.x_ref), custom_call_target="tpu_custom_call" | custom-call | tf_op jit(solution)/shard_map/pallas_call | solution.py:63
  76.4 1.7 %reshape.415 = bf16[32,2,4,16,32]{4,3,2,1,0:T(8,128)(2,1)S(1)} reshape(bf16[32,32,128]{2,1,0:T(8,128)(2,1)} %shard_map.66) | data formatting | bytes 524288 | tf_op jit(solution)/shard_map/reshape | solution.py:178
  78.1 0.2 copy.38
  78.3 1.4 copy-done.2
  79.7 0.5 convolution_bitcast_fusion
  80.3 0.3 copy.40
  80.6 0.4 copy.41
  80.9 0.8 copy.42.x_ref
  81.7 23.0 %shard_map.67 = bf16[64,4,256]{2,1,0:T(4,128)(2,1)} custom-call(bf16[64,4,256]{2,1,0:T(4,128)(2,1)} %copy.42.x_ref), custom_call_target="tpu_custom_call" | custom-call | tf_op jit(solution)/shard_map/pallas_call | solution.py:63
  104.8 1.2 convert_element_type.134
  106.0 0.1 reduce
  106.2 0.1 convert_bitcast_fusion
  106.2 0.3 copy.43
  106.5 0.3 reshape.419
  106.8 0.7 multiply_convert_fusion.x_ref
  107.6 33.8 %shard_map.68 = bf16[8,4,8192]{2,1,0:T(4,128)(2,1)} custom-call(bf16[4,8192]{1,0:T(4,128)(2,1)} %multiply_convert_fusion.x_ref), custom_call_target="tpu_custom_call" | custom-call | tf_op jit(solution)/shard_map/pallas_call | solution.py:63
  141.3 1.2 reshape.418
  142.5 1.0 convolution_convert_fusion
  (21 shorter events, 0.2 us)
Async XLA Ops:
  0.0 142.5 %copy-start = (bf16[32,64]{1,0:T(8,128)(2,1)S(1)}, bf16[32,64]{1,0:T(8,128)(2,1)}, u32[]{:S(2)}) copy-start(bf16[32,64]{1,0:T(8,128)(2,1)} %param.11) | copy-start | bytes 12292
  1.1 2.7 %copy-start.4 = (bf16[4,8192]{1,0:T(4,128)(2,1)S(1)}, bf16[4,8192]{1,0:T(4,128)(2,1)}, u32[]{:S(2)}) copy-start(bf16[4,8192]{1,0:T(4,128)(2,1)} %param.7) | copy-start | bytes 196612
  1.1 2.7 %copy-start.5 = (bf16[4,8192]{1,0:T(4,128)(2,1)S(1)}, bf16[4,8192]{1,0:T(4,128)(2,1)}, u32[]{:S(2)}) copy-start(bf16[4,8192]{1,0:T(4,128)(2,1)} %param.6) | copy-start | bytes 196612
  55.1 2.8 %copy-start.3 = (bf16[2,4,16,1024]{3,2,1,0:T(8,128)(2,1)S(1)}, bf16[2,4,16,1024]{3,2,1,0:T(8,128)(2,1)}, u32[]{:S(2)}) copy-start(bf16[2,4,16,1024]{3,2,1,0:T(8,128)(2,1)} %param.9) | copy-start | bytes 786436
  55.1 2.9 %copy-start.1 = (bf16[32,32,1024]{2,1,0:T(8,128)(2,1)S(1)}, bf16[32,32,1024]{2,1,0:T(8,128)(2,1)}, u32[]{:S(2)}) copy-start(bf16[32,32,1024]{2,1,0:T(8,128)(2,1)} %get-tuple-element.16) | copy-start | bytes 6291460
  78.1 1.6 %copy-start.2 = (bf16[32,32,1024]{2,1,0:T(8,128)(2,1)S(1)}, bf16[32,32,1024]{2,1,0:T(8,128)(2,1)}, u32[]{:S(2)}) copy-start(bf16[32,32,1024]{2,1,0:T(8,128)(2,1)} %get-tuple-element.16) | copy-start | bytes 6291460
  81.7 25.1 %copy-start.6 = (bf16[4,8192]{1,0:T(4,128)(2,1)S(1)}, bf16[4,8192]{1,0:T(4,128)(2,1)}, u32[]{:S(2)}) copy-start(bf16[4,8192]{1,0:T(4,128)(2,1)} %param.8) | copy-start | bytes 196612
  81.7 25.1 %copy-start.7 = (f32[4]{0:T(128)S(1)}, f32[4]{0:T(128)}, u32[]{:S(2)}) copy-start(f32[4]{0:T(128)} %param.10) | copy-start | bytes 52

commit v10 on v9

--- a/solution.py
+++ b/solution.py
@@ -111,6 +111,7 @@
     group = ctx_count // halves
     slab = block_order // group
     freq_rows = block_order // ctx_count
+    lanes = channels * freq_rows
     half_freqs = block_order // halves
     rows_here = tokens // block_order
     half_rows = block_order // 2
@@ -160,23 +161,24 @@
             freq_real * resp_imag + freq_imag * resp_real,
         ]
     ).astype(jnp.bfloat16)
-    inner = contract("rcab,sbj->srcaj", shaped, both_full)
-    inner_real = inner[0, 0] - inner[1, 1]
-    inner_imag = inner[0, 1] + inner[1, 0]
-    twist_cosine, twist_sine = twist_tables(local_ticks, positions, length_all)
-    back = jnp.stack(
+    inner = contract("sjb,kb->sjk", both_full, shaped.reshape(2 * lanes, block_order))
+    inner_real = inner[0, :, :lanes] - inner[1, :, lanes:]
+    inner_imag = inner[0, :, lanes:] + inner[1, :, :lanes]
+    twist_cosine, twist_sine = twist_tables(positions, local_ticks, length_all)
+    twist_cosine = jnp.tile(twist_cosine, (1, channels))
+    twist_sine = jnp.tile(twist_sine, (1, channels))
+    back = jnp.concatenate(
         [
             inner_real * twist_cosine - inner_imag * twist_sine,
             inner_imag * twist_cosine + inner_real * twist_sine,
-        ]
-    ).astype(jnp.bfloat16)
-
-    back = lax.optimization_barrier(back)
-    outgoing = back.reshape(2, channels, freq_rows, group, slab).transpose(3, 0, 1, 2, 4)
-    arrived = exchange(outgoing.reshape(group, -1, 128), "ctx", False, 2)
+        ],
+        axis=1,
+    ).astype(jnp.bfloat16)
+
+    arrived = exchange(back.reshape(group, slab, 2 * lanes), "ctx", False, 2)
     columns = (
-        arrived.reshape(group, 2, channels, freq_rows, slab)
-        .transpose(1, 2, 0, 3, 4)
+        arrived.reshape(group, slab, 2, channels, freq_rows)
+        .transpose(2, 3, 0, 4, 1)
         .reshape(2, channels, half_freqs, slab)
     )
     parts = contract("sai,rcaj->srcij", both_sub, columns)

time: 144 us -> 151 us (1.049)
  local copies, waits for them, and re-layouts: 22.6 us -> 26.2 us
  other arithmetic: 6.05 us -> 9.31 us
    reshape x3 -> x0, local copies, waits for them, and re-layouts: 4.68 us -> none  [the longest x1 2.53 us: local(): arrived = exchange(outgoing.reshape(group, -1, 128), 'ctx', False, 2)]
    another operation x2 -> x8, local copies, waits for them, and re-layouts: 0.55 us -> 4.08 us  [the longest x3 1.77 us: local(): twist_cosine = jnp.tile(twist_cosine, (1, channels))]
    unnamed x16 -> x20, local copies, waits for them, and re-layouts: 1.43 us -> 3.43 us
    add x0 -> x1, local copies, waits for them, and re-layouts: none -> 1.97 us  [local(): inner_imag = inner[0, :, lanes:] + inner[1, :, :lanes]]
    reshape x3 -> x1, local copies, waits for them, and re-layouts: 3.53 us -> 1.67 us  [local(): arrived.reshape(group, 2, channels, freq_rows, slab)]
where the time goes in v10:
time: 151 us; the launch traced here: 150 us
  Pallas kernels  108 us (72%)
  local copies, waits for them, and re-layouts  26.2 us (17%)
  other arithmetic  9.31 us (6%)
  matrix products  6.58 us (4%)
    pallas_call x5, Pallas kernels, exchange(): pl.pallas_call(functools.partial(_exchange_kernel, axis, gather), out_sha...  108 us
    dot_general x4, matrix products, contract(): return jnp.einsum(form, left, right, preferred_element_type=jnp.float32)  5.6 us
    unnamed x20, local copies, waits for them, and re-layouts  3.43 us

profile of v10, /device:TPU:70, one launch (start us, length us, event | category | flops | bytes accessed | tf_op | source)
XLA Modules:
  0.0 150.4 jit_solution(614262639061618677)
XLA Ops:
  0.0 0.9 multiply_convert_fusion.1
  1.0 1.0 fusion.46
  1.9 0.3 fusion.44
  2.3 0.6 fusion.41
  3.2 0.8 reshape.359.x_ref
  4.1 24.7 %shard_map.64 = bf16[64,4,256]{2,1,0:T(4,128)(2,1)} custom-call(bf16[32,4,256]{2,1,0:T(4,128)(2,1)} %reshape.359.x_ref), custom_call_target="tpu_custom_call" | custom-call | tf_op jit(solution)/shard_map/pallas_call | solution.py:63
  28.7 1.1 copy.37
  29.8 0.3 copy.38
  30.2 0.5 fusion.38
  30.7 0.3 tile.21
  31.0 1.4 copy.47
  32.5 0.3 tile.9
  32.8 1.4 copy.45
  34.2 1.4 add_convert_fusion
  35.6 0.7 convolution_bitcast_fusion.1
  36.4 0.6 copy-done.1
  37.0 0.3 copy.40
  37.3 0.3 copy.41
  37.6 0.2 maximum_bitcast_fusion
  37.8 0.3 copy.42
  38.1 1.2 reshape.362.x_ref
  39.4 13.8 %shard_map.65 = bf16[32,32,128]{2,1,0:T(8,128)(2,1)} custom-call(bf16[32,32,128]{2,1,0:T(8,128)(2,1)} %reshape.362.x_ref), custom_call_target="tpu_custom_call" | custom-call | tf_op jit(solution)/shard_map/pallas_call | solution.py:63
  53.2 1.7 %reshape.363 = bf16[32,2,4,16,32]{4,3,2,1,0:T(8,128)(2,1)S(1)} reshape(bf16[32,32,128]{2,1,0:T(8,128)(2,1)} %shard_map.65) | data formatting | bytes 524288 | tf_op jit(solution)/shard_map/reshape | solution.py:149
  54.9 1.6 %copy.43 = bf16[2,4,16,32,32]{4,3,2,1,0:T(8,128)(2,1)} copy(bf16[2,4,16,32,32]{4,2,1,0,3:T(8,128)(2,1)S(1)} %bitcast.97) | data formatting | bytes 524288 | tf_op jit(solution)/shard_map/transpose | solution.py:150
  56.5 2.3 %reshape.373 = bf16[2,4,16,1024,1]{3,2,1,0,4:T(8,128)(2,1)S(1)} reshape(bf16[2,4,16,32,32]{4,3,2,1,0:T(8,128)(2,1)} %copy.43) | data formatting | bytes 524288 | tf_op jit(solution)/shard_map/reshape | solution.py:151
  58.9 2.7 %fusion.3 = f32[2,2,4,16,1024]{4,3,2,1,0:T(8,128)S(1)} fusion(bf16[2,4,16,1024,1]{3,2,1,0,4:T(8,128)(2,1)S(1)} %reshape.373, bf16[1,1024,1024]{2,1,0:T(8,128)(2,1)S(1)} %bitcast.89, bf16[1,1024,1024]{2,1,0:T(8,128)(2,1)} %bitcast.93), kind=kOutput, calls=%fused_computation.9 | convolution fusion | flops 545259520 | bytes 5505024 | tf_op jit(solution)/shard_map/rcaj,sjb->srcab/dot_general | solution.py:101
  61.7 1.4 copy-done.2
  63.1 1.7 %fusion.2 = f32[2,1024,128]{1,2,0:T(8,128)S(1)} fusion(bf16[128,1024,1]{1,0,2:T(8,128)(2,1)S(1)} %bitcast.107, bf16[1,1024,1024]{2,1,0:T(8,128)(2,1)S(1)} %bitcast.90, bf16[1,1024,1024]{2,1,0:T(8,128)(2,1)S(1)} %bitcast.94), kind=kOutput, calls=%fused_computation.8 | convolution fusion | flops 538968064 | bytes 5505024 | tf_op jit(solution)/shard_map/sjb,kb->sjk/dot_general | solution.py:101
  64.8 0.8 slice_add_fusion
  65.6 2.0 %copy.46 = f32[1,1024,64]{2,1,0:T(8,128)} copy(f32[1,1024,64]{1,2,0:T(8,128)} %get-tuple-element.13) | data formatting | bytes 524288 | tf_op jit(solution)/shard_map/add | solution.py:166
  67.6 1.0 copy.44
  68.6 1.5 subtract_convert_fusion.1
  70.1 0.9 pad_maximum_fusion.4.x_ref
  71.0 12.6 %shard_map.66 = bf16[32,32,128]{2,1,0:T(8,128)(2,1)} custom-call(bf16[32,32,128]{2,1,0:T(8,128)(2,1)} %pad_maximum_fusion.4.x_ref), custom_call_target="tpu_custom_call" | custom-call | tf_op jit(solution)/shard_map/pallas_call | solution.py:63
  83.6 1.4 copy.50
  85.2 1.4 copy-done.3
  86.6 0.5 convolution_bitcast_fusion
  87.2 0.3 copy.53
  87.5 0.4 copy.54
  87.8 0.8 copy.55.x_ref
  88.7 22.9 %shard_map.67 = bf16[64,4,256]{2,1,0:T(4,128)(2,1)} custom-call(bf16[64,4,256]{2,1,0:T(4,128)(2,1)} %copy.55.x_ref), custom_call_target="tpu_custom_call" | custom-call | tf_op jit(solution)/shard_map/pallas_call | solution.py:63
  111.6 1.2 convert_element_type.140
  113.0 0.3 copy.56
  113.3 0.3 reshape.369
  113.6 0.7 multiply_convert_fusion.x_ref
  114.4 33.9 %shard_map.68 = bf16[8,4,8192]{2,1,0:T(4,128)(2,1)} custom-call(bf16[4,8192]{1,0:T(4,128)(2,1)} %multiply_convert_fusion.x_ref), custom_call_target="tpu_custom_call" | custom-call | tf_op jit(solution)/shard_map/pallas_call | solution.py:63
  148.2 1.2 reshape.368
  149.4 1.0 convolution_convert_fusion
  (32 shorter events, 1.0 us)
Async XLA Ops:
  0.0 149.4 %copy-start = (bf16[32,64]{1,0:T(8,128)(2,1)S(1)}, bf16[32,64]{1,0:T(8,128)(2,1)}, u32[]{:S(2)}) copy-start(bf16[32,64]{1,0:T(8,128)(2,1)} %param.11) | copy-start | bytes 12292
  35.6 1.3 copy-start.1
  35.6 1.3 copy-start.6
  58.9 2.7 %copy-start.7 = (bf16[2,4,16,1024]{3,2,1,0:T(8,128)(2,1)S(1)}, bf16[2,4,16,1024]{3,2,1,0:T(8,128)(2,1)}, u32[]{:S(2)}) copy-start(bf16[2,4,16,1024]{3,2,1,0:T(8,128)(2,1)} %param.9) | copy-start | bytes 786436
  61.6 1.6 %copy-start.2 = (bf16[32,32,1024]{2,1,0:T(8,128)(2,1)S(1)}, bf16[32,32,1024]{2,1,0:T(8,128)(2,1)}, u32[]{:S(2)}) copy-start(bf16[32,32,1024]{2,1,0:T(8,128)(2,1)} %copy-done.1) | copy-start | bytes 6291460
  64.8 3.8 %copy-start.4 = (f32[32,32,64]{2,1,0:T(8,128)S(1)}, f32[32,32,64]{2,1,0:T(8,128)}, u32[]{:S(2)}) copy-start(f32[32,32,64]{2,1,0:T(8,128)} %copy.47) | copy-start | bytes 786436
  64.8 3.8 %copy-start.5 = (f32[32,32,64]{2,1,0:T(8,128)S(1)}, f32[32,32,64]{2,1,0:T(8,128)}, u32[]{:S(2)}) copy-start(f32[32,32,64]{2,1,0:T(8,128)} %copy.45) | copy-start | bytes 786436
  85.0 1.6 %copy-start.3 = (bf16[32,32,1024]{2,1,0:T(8,128)(2,1)S(1)}, bf16[32,32,1024]{2,1,0:T(8,128)(2,1)}, u32[]{:S(2)}) copy-start(bf16[32,32,1024]{2,1,0:T(8,128)(2,1)} %copy-done.1) | copy-start | bytes 6291460
  88.7 25.0 %copy-start.8 = (bf16[4,8192]{1,0:T(4,128)(2,1)S(1)}, bf16[4,8192]{1,0:T(4,128)(2,1)}, u32[]{:S(2)}) copy-start(bf16[4,8192]{1,0:T(4,128)(2,1)} %param.8) | copy-start | bytes 196612
  88.7 25.0 %copy-start.9 = (f32[4]{0:T(128)S(1)}, f32[4]{0:T(128)}, u32[]{:S(2)}) copy-start(f32[4]{0:T(128)} %param.10) | copy-start | bytes 52

commit v11 on v9

--- a/solution.py
+++ b/solution.py
@@ -196,11 +196,15 @@
         q_feature.astype(jnp.float32)
         * (convolved.astype(jnp.float32) + skip_gain[:, None] * product.astype(jnp.float32))
     ).astype(jnp.bfloat16)
-    gated_all = exchange(gated_rows, "tp", True, 4).reshape(tp_count * channels, tokens)
+    token_block = tokens // tp_count
+    outgoing = gated_rows.reshape(channels, tp_count, token_block).transpose(1, 0, 2)
+    arrived = exchange(outgoing, "tp", False, 4)
+    block_mixed = jnp.dot(
+        out_weight.T, arrived.reshape(tp_count * channels, token_block), preferred_element_type=jnp.float32
+    ).astype(jnp.bfloat16)
     outs_here = out_weight.shape[1] // tp_count
-    tp_index = lax.axis_index("tp")
-    my_weight = lax.dynamic_slice_in_dim(out_weight, tp_index * outs_here, outs_here, 1)
-    return jnp.dot(my_weight.T, gated_all, preferred_element_type=jnp.float32).astype(jnp.bfloat16)
+    returned = exchange(block_mixed.reshape(tp_count, outs_here, token_block), "tp", False, 5)
+    return returned.transpose(1, 0, 2).reshape(outs_here, tokens)
 
 
 def solution(mesh):

time: 144 us -> 143 us (level)
  the two profiles are of different devices: /device:TPU:70 before, /device:TPU:6 now
where the time goes in v11:
time: 143 us; the launch traced here: 142 us
  Pallas kernels  105 us (73%)
  local copies, waits for them, and re-layouts  23.9 us (17%)
  matrix products  6.68 us (5%)
  other arithmetic  6.05 us (4%)
    pallas_call x6, Pallas kernels, exchange(): pl.pallas_call(functools.partial(_exchange_kernel, axis, gather), out_sha...  105 us
    dot_general x4, matrix products, contract(): return jnp.einsum(form, left, right, preferred_element_type=jnp.float32)  5.8 us
    reshape x3, local copies, waits for them, and re-layouts, local(): arrived.reshape(group, 2, channels, freq_rows, slab)  3.53 us
    unnamed x17, local copies, waits for them, and re-layouts  3 us

profile of v11, /device:TPU:6, one launch (start us, length us, event | category | flops | bytes accessed | tf_op | source)
XLA Modules:
  0.0 141.9 jit_solution(12605915287936440440)
XLA Ops:
  0.0 0.6 fusion.51
  0.6 0.5 fusion.48
  1.2 2.6 %add_convert_fusion = (bf16[32,32,1024]{2,1,0:T(8,128)(2,1)S(1)}, bf16[32,32,1024]{2,1,0:T(8,128)(2,1)}) fusion(f32[32,1024]{1,0:T(8,128)S(1)} %get-tuple-element.23, f32[32,1024]{1,0:T(8,128)S(1)} %get-tuple-element.20, f32[32,1024]{1,0:T(8,128)S(1)} %get-tuple-element.24, f32[32,1024]{1,0:T(8,128)S(1)} %get-tuple-element.19), kind=kLoop, calls=%fused_computation.4 | loop fusion | flops 8388608 | bytes 4718592 | tf_op jit(solution)/shard_map/convert_element_type | solution.py:91
  3.9 0.2 reshape.415
  4.1 0.1 copy.69
  4.2 0.8 reshape.416.x_ref
  5.0 26.5 %shard_map.64 = bf16[64,4,256]{2,1,0:T(4,128)(2,1)} custom-call(bf16[32,4,256]{2,1,0:T(4,128)(2,1)} %reshape.416.x_ref), custom_call_target="tpu_custom_call" | custom-call | tf_op jit(solution)/shard_map/pallas_call | solution.py:63
  31.5 1.1 copy.44
  32.6 0.3 copy.45
  33.0 1.8 %convolution_bitcast_fusion.1 = f32[2,4,512,32]{2,3,0,1:T(8,128)S(1)} fusion(bf16[4,64,8,32]{3,2,1,0:T(8,128)(2,1)S(1)} %copy.45, s32[]{:T(128)S(6)} %select_n.65, bf16[1,1024,1024]{2,1,0:T(8,128)(2,1)} %bitcast.121, bf16[1,1024,1024]{2,1,0:T(8,128)(2,1)S(1)} %bitcast.117), kind=kOutput, calls=%fused_computation.11 | convolution fusion | flops 136314880 | bytes 4849668 | tf_op jit(solution)/shard_map/sai,cij->scaj/dot_general | solution.py:101
  34.8 0.3 fusion.56
  35.1 0.1 subtract_convert_fusion.3
  35.2 0.3 copy.47
  35.5 0.3 copy.48
  35.8 0.2 maximum_bitcast_fusion
  36.0 0.3 copy.49
  36.3 1.2 reshape.419.x_ref
  37.5 12.4 %shard_map.65 = bf16[32,32,128]{2,1,0:T(8,128)(2,1)} custom-call(bf16[32,32,128]{2,1,0:T(8,128)(2,1)} %reshape.419.x_ref), custom_call_target="tpu_custom_call" | custom-call | tf_op jit(solution)/shard_map/pallas_call | solution.py:63
  50.0 1.7 %reshape.420 = bf16[32,2,4,16,32]{4,3,2,1,0:T(8,128)(2,1)S(1)} reshape(bf16[32,32,128]{2,1,0:T(8,128)(2,1)} %shard_map.65) | data formatting | bytes 524288 | tf_op jit(solution)/shard_map/reshape | solution.py:148
  51.6 1.6 %copy.50 = bf16[2,4,16,32,32]{4,3,2,1,0:T(8,128)(2,1)} copy(bf16[2,4,16,32,32]{4,2,1,0,3:T(8,128)(2,1)S(1)} %bitcast.126) | data formatting | bytes 524288 | tf_op jit(solution)/shard_map/transpose | solution.py:149
  53.3 2.3 %reshape.435 = bf16[2,4,16,1024,1]{3,2,1,0,4:T(8,128)(2,1)S(1)} reshape(bf16[2,4,16,32,32]{4,3,2,1,0:T(8,128)(2,1)} %copy.50) | data formatting | bytes 524288 | tf_op jit(solution)/shard_map/reshape | solution.py:150
  55.6 2.8 %fusion.5 = f32[2,2,4,16,1024]{4,3,2,1,0:T(8,128)S(1)} fusion(bf16[2,4,16,1024,1]{3,2,1,0,4:T(8,128)(2,1)S(1)} %reshape.435, bf16[1,1024,1024]{2,1,0:T(8,128)(2,1)S(1)} %bitcast.118, bf16[1,1024,1024]{2,1,0:T(8,128)(2,1)} %bitcast.122), kind=kOutput, calls=%fused_computation.8 | convolution fusion | flops 545259520 | bytes 5505024 | tf_op jit(solution)/shard_map/rcaj,sjb->srcab/dot_general | solution.py:101
  58.4 0.1 fusion.17
  58.6 0.7 fusion.8
  59.3 0.3 fusion.54
  59.7 0.1 subtract_convert_fusion.1
  59.8 0.8 reshape.422
  60.6 1.4 copy.68
  62.0 2.5 %reshape.423.x_ref = bf16[32,32,128]{2,1,0:T(8,128)(2,1)} reshape(bf16[32,2,4,16,32]{4,3,2,1,0:T(8,128)(2,1)} %bitcast.127) | data formatting | bytes 524288 | tf_op jit(solution)/shard_map/reshape | solution.py:176
  64.5 12.4 %shard_map.66 = bf16[32,32,128]{2,1,0:T(8,128)(2,1)} custom-call(bf16[32,32,128]{2,1,0:T(8,128)(2,1)} %reshape.423.x_ref), custom_call_target="tpu_custom_call" | custom-call | tf_op jit(solution)/shard_map/pallas_call | solution.py:63
  76.9 1.7 %reshape.424 = bf16[32,2,4,16,32]{4,3,2,1,0:T(8,128)(2,1)S(1)} reshape(bf16[32,32,128]{2,1,0:T(8,128)(2,1)} %shard_map.66) | data formatting | bytes 524288 | tf_op jit(solution)/shard_map/reshape | solution.py:178
  78.6 0.2 copy.52
  78.8 1.4 copy-done.2
  80.2 0.5 convolution_bitcast_fusion
  80.8 0.3 copy.54
  81.1 0.4 copy.55
  81.4 0.8 copy.56.x_ref
  82.2 22.1 %shard_map.67 = bf16[64,4,256]{2,1,0:T(4,128)(2,1)} custom-call(bf16[64,4,256]{2,1,0:T(4,128)(2,1)} %copy.56.x_ref), custom_call_target="tpu_custom_call" | custom-call | tf_op jit(solution)/shard_map/pallas_call | solution.py:63
  104.4 1.2 convert_element_type.137
  105.6 0.1 reduce
  105.8 0.3 copy.57
  106.1 0.3 reshape.431
  106.4 0.7 multiply_convert_fusion
  107.2 18.5 %shard_map.68 = bf16[8,4,1024]{2,1,0:T(4,128)(2,1)} custom-call(bf16[8,4,1024]{2,1,0:T(4,128)(2,1)} %bitcast.135), custom_call_target="tpu_custom_call" | custom-call | tf_op jit(solution)/shard_map/pallas_call | solution.py:63
  125.7 0.9 reshape.428
  126.6 0.9 fusion.11.x_ref
  127.5 12.9 %shard_map.69 = bf16[8,8,1024]{2,1,0:T(8,128)(2,1)} custom-call(bf16[8,8,1024]{2,1,0:T(8,128)(2,1)} %fusion.11.x_ref), custom_call_target="tpu_custom_call" | custom-call | tf_op jit(solution)/shard_map/pallas_call | solution.py:63
  140.4 1.6 %copy.71 = bf16[8,8192]{1,0:T(8,128)(2,1)} copy(bf16[8,8192]{1,0:T(8,128)(2,1)} %bitcast.134) | data formatting | bytes 262144
  (23 shorter events, 0.2 us)
Async XLA Ops:
  0.0 126.6 %copy-start = (bf16[32,64]{1,0:T(8,128)(2,1)S(1)}, bf16[32,64]{1,0:T(8,128)(2,1)}, u32[]{:S(2)}) copy-start(bf16[32,64]{1,0:T(8,128)(2,1)} %param.11) | copy-start | bytes 12292
  1.1 2.7 %copy-start.4 = (bf16[4,8192]{1,0:T(4,128)(2,1)S(1)}, bf16[4,8192]{1,0:T(4,128)(2,1)}, u32[]{:S(2)}) copy-start(bf16[4,8192]{1,0:T(4,128)(2,1)} %param.7) | copy-start | bytes 196612
  1.1 2.7 %copy-start.5 = (bf16[4,8192]{1,0:T(4,128)(2,1)S(1)}, bf16[4,8192]{1,0:T(4,128)(2,1)}, u32[]{:S(2)}) copy-start(bf16[4,8192]{1,0:T(4,128)(2,1)} %param.6) | copy-start | bytes 196612
  55.6 2.8 %copy-start.3 = (bf16[2,4,16,1024]{3,2,1,0:T(8,128)(2,1)S(1)}, bf16[2,4,16,1024]{3,2,1,0:T(8,128)(2,1)}, u32[]{:S(2)}) copy-start(bf16[2,4,16,1024]{3,2,1,0:T(8,128)(2,1)} %param.9) | copy-start | bytes 786436
  55.6 2.9 %copy-start.1 = (bf16[32,32,1024]{2,1,0:T(8,128)(2,1)S(1)}, bf16[32,32,1024]{2,1,0:T(8,128)(2,1)}, u32[]{:S(2)}) copy-start(bf16[32,32,1024]{2,1,0:T(8,128)(2,1)} %get-tuple-element.16) | copy-start | bytes 6291460
  78.6 1.6 %copy-start.2 = (bf16[32,32,1024]{2,1,0:T(8,128)(2,1)S(1)}, bf16[32,32,1024]{2,1,0:T(8,128)(2,1)}, u32[]{:S(2)}) copy-start(bf16[32,32,1024]{2,1,0:T(8,128)(2,1)} %get-tuple-element.16) | copy-start | bytes 6291460
  82.2 24.2 %copy-start.6 = (bf16[4,8192]{1,0:T(4,128)(2,1)S(1)}, bf16[4,8192]{1,0:T(4,128)(2,1)}, u32[]{:S(2)}) copy-start(bf16[4,8192]{1,0:T(4,128)(2,1)} %param.8) | copy-start | bytes 196612
  82.2 24.2 %copy-start.7 = (f32[4]{0:T(128)S(1)}, f32[4]{0:T(128)}, u32[]{:S(2)}) copy-start(f32[4]{0:T(128)} %param.10) | copy-start | bytes 52

commit v12 on v11

--- a/solution.py
+++ b/solution.py
@@ -73,6 +73,75 @@
         ],
         compiler_params=pltpu.CompilerParams(collective_id=collective, has_side_effects=True),
     )(x)
+
+
+def _projection_kernel(x_ref, w_ref, y_ref, land, mixed, back, send_a, recv_a, send_b, recv_b, own):
+    count, channels = land.shape[0], land.shape[1]
+    outs_here = mixed.shape[1]
+    me = lax.axis_index("tp")
+    barrier = pltpu.get_barrier_semaphore()
+
+    def greet(step, carry):
+        pl.semaphore_signal(barrier, 1, device_id={"tp": lax.rem(me + step, count)}, device_id_type=MESH)
+        return carry
+
+    lax.fori_loop(1, count, greet, 0)
+    pl.semaphore_wait(barrier, count - 1)
+
+    def there(src, dst, sends, recvs, peer, slot):
+        return pltpu.make_async_remote_copy(
+            src_ref=src.at[peer], dst_ref=dst.at[slot], send_sem=sends.at[peer],
+            recv_sem=recvs.at[slot], device_id={"tp": peer}, device_id_type=MESH)
+
+    def trade(src, dst, sends, recvs, flag):
+        def send(step, carry):
+            there(src, dst, sends, recvs, lax.rem(me + step, count), me).start()
+            return carry
+
+        lax.fori_loop(1, count, send, 0)
+        local = pltpu.make_async_copy(src.at[me], dst.at[me], own.at[flag])
+        local.start()
+
+        def finish(step, carry):
+            there(src, dst, sends, recvs, lax.rem(me + step, count), me).wait_send()
+            source = lax.rem(me + count - step, count)
+            there(src, dst, sends, recvs, source, source).wait_recv()
+            return carry
+
+        lax.fori_loop(1, count, finish, 0)
+        local.wait()
+
+    trade(x_ref, land, send_a, recv_a, 0)
+    total = jnp.zeros((count * outs_here, land.shape[2]), jnp.float32)
+    for group_index in range(count):
+        for channel in range(channels):
+            row = land[group_index, channel : channel + 1, :].astype(jnp.float32)
+            total = total + w_ref[group_index * channels + channel] * row
+    for group_index in range(count):
+        mixed[group_index] = total[group_index * outs_here : (group_index + 1) * outs_here].astype(mixed.dtype)
+    trade(mixed, back, send_b, recv_b, 1)
+    y_ref[...] = back[...]
+
+
+def project_over_tp(x, weight, outs_here, collective):
+    count, channels, block = x.shape
+    return pl.pallas_call(
+        _projection_kernel,
+        out_shape=jax.ShapeDtypeStruct((count, outs_here, block), x.dtype),
+        in_specs=[pl.BlockSpec(memory_space=pltpu.VMEM)] * 2,
+        out_specs=pl.BlockSpec(memory_space=pltpu.VMEM),
+        scratch_shapes=[
+            pltpu.VMEM(x.shape, x.dtype),
+            pltpu.VMEM((count, outs_here, block), x.dtype),
+            pltpu.VMEM((count, outs_here, block), x.dtype),
+            pltpu.SemaphoreType.DMA((count,)),
+            pltpu.SemaphoreType.DMA((count,)),
+            pltpu.SemaphoreType.DMA((count,)),
+            pltpu.SemaphoreType.DMA((count,)),
+            pltpu.SemaphoreType.DMA((2,)),
+        ],
+        compiler_params=pltpu.CompilerParams(collective_id=collective, has_side_effects=True),
+    )(x, weight)
 
 
 def fourier_tables(length_all):
@@ -198,12 +267,9 @@
     ).astype(jnp.bfloat16)
     token_block = tokens // tp_count
     outgoing = gated_rows.reshape(channels, tp_count, token_block).transpose(1, 0, 2)
-    arrived = exchange(outgoing, "tp", False, 4)
-    block_mixed = jnp.dot(
-        out_weight.T, arrived.reshape(tp_count * channels, token_block), preferred_element_type=jnp.float32
-    ).astype(jnp.bfloat16)
     outs_here = out_weight.shape[1] // tp_count
-    returned = exchange(block_mixed.reshape(tp_count, outs_here, token_block), "tp", False, 5)
+    weight_columns = out_weight.astype(jnp.float32).reshape(tp_count * channels, tp_count * outs_here, 1)
+    returned = project_over_tp(outgoing, weight_columns, outs_here, 4)
     return returned.transpose(1, 0, 2).reshape(outs_here, tokens)
 
 

time: 143 us -> 138 us (0.965)
  Pallas kernels: 105 us -> 101 us
    pallas_call x6 -> x4, Pallas kernels: 105 us -> 73.8 us  [exchange(): pl.pallas_call(functools.partial(_exchange_kernel, axis, gather), out_sha...]
    pallas_call x0 -> x1, Pallas kernels: none -> 27.2 us  [project_over_tp(): pl.pallas_call(_projection_kernel, out_shape=jax.ShapeDtypeStruct((count,...]
where the time goes in v12:
time: 138 us; the launch traced here: 137 us
  Pallas kernels  101 us (73%)
  local copies, waits for them, and re-layouts  24.4 us (18%)
  other arithmetic  6.02 us (4%)
  matrix products  5.47 us (4%)
    pallas_call x4, Pallas kernels, exchange(): pl.pallas_call(functools.partial(_exchange_kernel, axis, gather), out_sha...  73.8 us
    pallas_call x1, Pallas kernels, project_over_tp(): pl.pallas_call(_projection_kernel, out_shape=jax.ShapeDtypeStruct((count,...  27.2 us
    dot_general x4, matrix products, contract(): return jnp.einsum(form, left, right, preferred_element_type=jnp.float32)  5.47 us
    reshape x3, local copies, waits for them, and re-layouts, local(): arrived.reshape(group, 2, channels, freq_rows, slab)  3.53 us
    unnamed x17, local copies, waits for them, and re-layouts  3 us

profile of v12, /device:TPU:6, one launch (start us, length us, event | category | flops | bytes accessed | tf_op | source)
XLA Modules:
  0.0 137.3 jit_solution(9865616758082315359)
XLA Ops:
  0.0 0.6 fusion.50
  0.6 0.5 fusion.47
  1.1 0.0 copy-start.3
  1.2 2.6 %add_convert_fusion = (bf16[32,32,1024]{2,1,0:T(8,128)(2,1)S(1)}, bf16[32,32,1024]{2,1,0:T(8,128)(2,1)}) fusion(f32[32,1024]{1,0:T(8,128)S(1)} %get-tuple-element.23, f32[32,1024]{1,0:T(8,128)S(1)} %get-tuple-element.20, f32[32,1024]{1,0:T(8,128)S(1)} %get-tuple-element.24, f32[32,1024]{1,0:T(8,128)S(1)} %get-tuple-element.19), kind=kLoop, calls=%fused_computation.4 | loop fusion | flops 8388608 | bytes 4718592 | tf_op jit(solution)/shard_map/convert_element_type | solution.py:160
  3.8 0.2 reshape.414
  4.0 0.1 copy.72
  4.1 0.8 reshape.415.x_ref
  5.0 26.5 %shard_map.64 = bf16[64,4,256]{2,1,0:T(4,128)(2,1)} custom-call(bf16[32,4,256]{2,1,0:T(4,128)(2,1)} %reshape.415.x_ref), custom_call_target="tpu_custom_call" | custom-call | tf_op jit(solution)/shard_map/pallas_call | solution.py:63
  31.5 1.1 copy.46
  32.6 0.3 copy.47
  32.9 1.8 %convolution_bitcast_fusion.1 = f32[2,4,512,32]{2,3,0,1:T(8,128)S(1)} fusion(bf16[4,64,8,32]{3,2,1,0:T(8,128)(2,1)S(1)} %copy.47, s32[]{:T(128)S(6)} %select_n.65, bf16[1,1024,1024]{2,1,0:T(8,128)(2,1)} %bitcast.118, bf16[1,1024,1024]{2,1,0:T(8,128)(2,1)S(1)} %bitcast.114), kind=kOutput, calls=%fused_computation.11 | convolution fusion | flops 136314880 | bytes 4849668 | tf_op jit(solution)/shard_map/sai,cij->scaj/dot_general | solution.py:170
  34.7 0.3 fusion.55
  35.1 0.1 subtract_convert_fusion.3
  35.2 0.3 copy.49
  35.4 0.3 copy.50
  35.7 0.2 maximum_bitcast_fusion
  36.0 0.3 copy.51
  36.3 1.2 reshape.418.x_ref
  37.5 12.4 %shard_map.65 = bf16[32,32,128]{2,1,0:T(8,128)(2,1)} custom-call(bf16[32,32,128]{2,1,0:T(8,128)(2,1)} %reshape.418.x_ref), custom_call_target="tpu_custom_call" | custom-call | tf_op jit(solution)/shard_map/pallas_call | solution.py:63
  49.9 1.7 %reshape.419 = bf16[32,2,4,16,32]{4,3,2,1,0:T(8,128)(2,1)S(1)} reshape(bf16[32,32,128]{2,1,0:T(8,128)(2,1)} %shard_map.65) | data formatting | bytes 524288 | tf_op jit(solution)/shard_map/reshape | solution.py:217
  51.6 1.6 %copy.52 = bf16[2,4,16,32,32]{4,3,2,1,0:T(8,128)(2,1)} copy(bf16[2,4,16,32,32]{4,2,1,0,3:T(8,128)(2,1)S(1)} %bitcast.123) | data formatting | bytes 524288 | tf_op jit(solution)/shard_map/transpose | solution.py:218
  53.3 2.3 %reshape.436 = bf16[2,4,16,1024,1]{3,2,1,0,4:T(8,128)(2,1)S(1)} reshape(bf16[2,4,16,32,32]{4,3,2,1,0:T(8,128)(2,1)} %copy.52) | data formatting | bytes 524288 | tf_op jit(solution)/shard_map/reshape | solution.py:219
  55.6 2.5 %fusion.5 = f32[2,2,4,16,1024]{4,3,2,1,0:T(8,128)S(1)} fusion(bf16[2,4,16,1024,1]{3,2,1,0,4:T(8,128)(2,1)S(1)} %reshape.436, bf16[1,1024,1024]{2,1,0:T(8,128)(2,1)S(1)} %bitcast.115, bf16[1,1024,1024]{2,1,0:T(8,128)(2,1)} %bitcast.119), kind=kOutput, calls=%fused_computation.8 | convolution fusion | flops 545259520 | bytes 5505024 | tf_op jit(solution)/shard_map/rcaj,sjb->srcab/dot_general | solution.py:170
  58.1 0.1 fusion.16
  58.2 0.7 fusion.8
  59.0 0.3 fusion.53
  59.3 0.1 subtract_convert_fusion.1
  59.5 0.8 reshape.421
  60.2 1.4 %copy.71 = bf16[2,4,16,32,32]{4,2,1,0,3:T(8,128)(2,1)} copy(bf16[2,4,16,32,32]{4,3,2,1,0:T(8,128)(2,1)S(1)} %reshape.421) | data formatting | bytes 524288 | tf_op jit(solution)/shard_map/reshape | solution.py:244
  61.6 2.5 %reshape.422.x_ref = bf16[32,32,128]{2,1,0:T(8,128)(2,1)} reshape(bf16[32,2,4,16,32]{4,3,2,1,0:T(8,128)(2,1)} %bitcast.124) | data formatting | bytes 524288 | tf_op jit(solution)/shard_map/reshape | solution.py:245
  64.1 12.4 %shard_map.66 = bf16[32,32,128]{2,1,0:T(8,128)(2,1)} custom-call(bf16[32,32,128]{2,1,0:T(8,128)(2,1)} %reshape.422.x_ref), custom_call_target="tpu_custom_call" | custom-call | tf_op jit(solution)/shard_map/pallas_call | solution.py:63
  76.6 1.7 %reshape.423 = bf16[32,2,4,16,32]{4,3,2,1,0:T(8,128)(2,1)S(1)} reshape(bf16[32,32,128]{2,1,0:T(8,128)(2,1)} %shard_map.66) | data formatting | bytes 524288 | tf_op jit(solution)/shard_map/reshape | solution.py:247
  78.3 0.2 copy.54
  78.5 1.4 %copy-done.1 = bf16[32,32,1024]{2,1,0:T(8,128)(2,1)S(1)} copy-done((bf16[32,32,1024]{2,1,0:T(8,128)(2,1)S(1)}, bf16[32,32,1024]{2,1,0:T(8,128)(2,1)}, u32[]{:S(2)}) %copy-start.1) | copy-done | bytes 2097176
  79.9 0.5 convolution_bitcast_fusion
  80.4 0.3 copy.56
  80.7 0.3 copy.57
  81.0 0.8 copy.58.x_ref
  81.9 22.4 %shard_map.67 = bf16[64,4,256]{2,1,0:T(4,128)(2,1)} custom-call(bf16[64,4,256]{2,1,0:T(4,128)(2,1)} %copy.58.x_ref), custom_call_target="tpu_custom_call" | custom-call | tf_op jit(solution)/shard_map/pallas_call | solution.py:63
  104.3 1.3 convert_element_type.132
  105.5 0.1 reduce
  105.7 0.1 convert_bitcast_fusion
  105.7 0.3 copy.59
  106.0 0.3 reshape.430
  106.3 0.7 multiply_convert_fusion
  107.1 1.4 %copy.60.w_ref = f32[32,64,1]{2,1,0:T(8,128)} copy(f32[32,64,1]{1,0,2:T(8,128)S(1)} %bitcast_convert_fusion) | data formatting | bytes 16384 | tf_op jit(solution)/shard_map/reshape | solution.py:271
  108.5 27.2 %shard_map.68 = bf16[8,8,1024]{2,1,0:T(8,128)(2,1)} custom-call(bf16[8,4,1024]{2,1,0:T(4,128)(2,1)} %bitcast.132, f32[32,64,1]{2,1,0:T(8,128)} %copy.60.w_ref), custom_call_target="tpu_custom_call" | custom-call | tf_op jit(solution)/shard_map/pallas_call | solution.py:128
  135.7 1.6 %copy.74 = bf16[8,8192]{1,0:T(8,128)(2,1)} copy(bf16[8,8192]{1,0:T(8,128)(2,1)} %bitcast.131) | data formatting | bytes 262144
  (22 shorter events, 0.2 us)
Async XLA Ops:
  1.1 2.6 %copy-start.3 = (bf16[4,8192]{1,0:T(4,128)(2,1)S(1)}, bf16[4,8192]{1,0:T(4,128)(2,1)}, u32[]{:S(2)}) copy-start(bf16[4,8192]{1,0:T(4,128)(2,1)} %param.7) | copy-start | bytes 196612
  1.1 2.6 %copy-start.4 = (bf16[4,8192]{1,0:T(4,128)(2,1)S(1)}, bf16[4,8192]{1,0:T(4,128)(2,1)}, u32[]{:S(2)}) copy-start(bf16[4,8192]{1,0:T(4,128)(2,1)} %param.6) | copy-start | bytes 196612
  55.6 2.5 %copy-start.2 = (bf16[2,4,16,1024]{3,2,1,0:T(8,128)(2,1)S(1)}, bf16[2,4,16,1024]{3,2,1,0:T(8,128)(2,1)}, u32[]{:S(2)}) copy-start(bf16[2,4,16,1024]{3,2,1,0:T(8,128)(2,1)} %param.9) | copy-start | bytes 786436
  55.6 2.6 %copy-start = (bf16[32,32,1024]{2,1,0:T(8,128)(2,1)S(1)}, bf16[32,32,1024]{2,1,0:T(8,128)(2,1)}, u32[]{:S(2)}) copy-start(bf16[32,32,1024]{2,1,0:T(8,128)(2,1)} %get-tuple-element.16) | copy-start | bytes 6291460
  78.3 1.6 %copy-start.1 = (bf16[32,32,1024]{2,1,0:T(8,128)(2,1)S(1)}, bf16[32,32,1024]{2,1,0:T(8,128)(2,1)}, u32[]{:S(2)}) copy-start(bf16[32,32,1024]{2,1,0:T(8,128)(2,1)} %get-tuple-element.16) | copy-start | bytes 6291460
  81.9 24.4 %copy-start.5 = (bf16[4,8192]{1,0:T(4,128)(2,1)S(1)}, bf16[4,8192]{1,0:T(4,128)(2,1)}, u32[]{:S(2)}) copy-start(bf16[4,8192]{1,0:T(4,128)(2,1)} %param.8) | copy-start | bytes 196612
  81.9 24.4 %copy-start.7 = (f32[4]{0:T(128)S(1)}, f32[4]{0:T(128)}, u32[]{:S(2)}) copy-start(f32[4]{0:T(128)} %param.10) | copy-start | bytes 52
  104.2 2.8 %copy-start.6 = (bf16[32,64]{1,0:T(8,128)(2,1)S(1)}, bf16[32,64]{1,0:T(8,128)(2,1)}, u32[]{:S(2)}) copy-start(bf16[32,64]{1,0:T(8,128)(2,1)} %param.11) | copy-start | bytes 12292

commit v13 on v12

--- a/solution.py
+++ b/solution.py
@@ -116,7 +116,8 @@
     for group_index in range(count):
         for channel in range(channels):
             row = land[group_index, channel : channel + 1, :].astype(jnp.float32)
-            total = total + w_ref[group_index * channels + channel] * row
+            column = group_index * channels + channel
+            total = total + w_ref[:, column : column + 1] * row
     for group_index in range(count):
         mixed[group_index] = total[group_index * outs_here : (group_index + 1) * outs_here].astype(mixed.dtype)
     trade(mixed, back, send_b, recv_b, 1)
@@ -268,7 +269,7 @@
     token_block = tokens // tp_count
     outgoing = gated_rows.reshape(channels, tp_count, token_block).transpose(1, 0, 2)
     outs_here = out_weight.shape[1] // tp_count
-    weight_columns = out_weight.astype(jnp.float32).reshape(tp_count * channels, tp_count * outs_here, 1)
+    weight_columns = out_weight.astype(jnp.float32).T
     returned = project_over_tp(outgoing, weight_columns, outs_here, 4)
     return returned.transpose(1, 0, 2).reshape(outs_here, tokens)
 

time: 138 us -> 137 us (level)
    reshape x1 -> x0, local copies, waits for them, and re-layouts: 1.38 us -> none  [local(): out_weight.astype(jnp.float32)]
where the time goes in v13:
time: 137 us; the launch traced here: 136 us
  Pallas kernels  100 us (73%)
  local copies, waits for them, and re-layouts  23.7 us (17%)
  other arithmetic  6.01 us (4%)
  matrix products  5.47 us (4%)
    pallas_call x4, Pallas kernels, exchange(): pl.pallas_call(functools.partial(_exchange_kernel, axis, gather), out_sha...  73.5 us
    pallas_call x1, Pallas kernels, project_over_tp(): pl.pallas_call(_projection_kernel, out_shape=jax.ShapeDtypeStruct((count,...  26.8 us
    dot_general x4, matrix products, contract(): return jnp.einsum(form, left, right, preferred_element_type=jnp.float32)  5.47 us
    reshape x3, local copies, waits for them, and re-layouts, local(): arrived.reshape(group, 2, channels, freq_rows, slab)  3.53 us
    unnamed x17, local copies, waits for them, and re-layouts  3 us

profile of v13, /device:TPU:6, one launch (start us, length us, event | category | flops | bytes accessed | tf_op | source)
XLA Modules:
  0.0 135.9 jit_solution(272298318788619300)
XLA Ops:
  0.0 0.6 fusion.50
  0.6 0.5 fusion.47
  1.1 0.0 copy-start.3
  1.2 2.6 %add_convert_fusion = (bf16[32,32,1024]{2,1,0:T(8,128)(2,1)S(1)}, bf16[32,32,1024]{2,1,0:T(8,128)(2,1)}) fusion(f32[32,1024]{1,0:T(8,128)S(1)} %get-tuple-element.23, f32[32,1024]{1,0:T(8,128)S(1)} %get-tuple-element.20, f32[32,1024]{1,0:T(8,128)S(1)} %get-tuple-element.24, f32[32,1024]{1,0:T(8,128)S(1)} %get-tuple-element.19), kind=kLoop, calls=%fused_computation.4 | loop fusion | flops 8388608 | bytes 4718592 | tf_op jit(solution)/shard_map/convert_element_type | solution.py:161
  3.8 0.2 reshape.409
  4.0 0.1 copy.89
  4.1 0.8 reshape.410.x_ref
  5.0 26.5 %shard_map.64 = bf16[64,4,256]{2,1,0:T(4,128)(2,1)} custom-call(bf16[32,4,256]{2,1,0:T(4,128)(2,1)} %reshape.410.x_ref), custom_call_target="tpu_custom_call" | custom-call | tf_op jit(solution)/shard_map/pallas_call | solution.py:63
  31.5 1.1 copy.63
  32.6 0.3 copy.64
  32.9 1.8 %convolution_bitcast_fusion.1 = f32[2,4,512,32]{2,3,0,1:T(8,128)S(1)} fusion(bf16[4,64,8,32]{3,2,1,0:T(8,128)(2,1)S(1)} %copy.64, s32[]{:T(128)S(6)} %select_n.65, bf16[1,1024,1024]{2,1,0:T(8,128)(2,1)} %bitcast.116, bf16[1,1024,1024]{2,1,0:T(8,128)(2,1)S(1)} %bitcast.112), kind=kOutput, calls=%fused_computation.11 | convolution fusion | flops 136314880 | bytes 4849668 | tf_op jit(solution)/shard_map/sai,cij->scaj/dot_general | solution.py:171
  34.7 0.3 fusion.55
  35.1 0.1 subtract_convert_fusion.3
  35.2 0.3 copy.66
  35.4 0.3 copy.67
  35.7 0.2 maximum_bitcast_fusion
  36.0 0.3 copy.68
  36.3 1.2 reshape.413.x_ref
  37.5 12.4 %shard_map.65 = bf16[32,32,128]{2,1,0:T(8,128)(2,1)} custom-call(bf16[32,32,128]{2,1,0:T(8,128)(2,1)} %reshape.413.x_ref), custom_call_target="tpu_custom_call" | custom-call | tf_op jit(solution)/shard_map/pallas_call | solution.py:63
  49.9 1.7 %reshape.414 = bf16[32,2,4,16,32]{4,3,2,1,0:T(8,128)(2,1)S(1)} reshape(bf16[32,32,128]{2,1,0:T(8,128)(2,1)} %shard_map.65) | data formatting | bytes 524288 | tf_op jit(solution)/shard_map/reshape | solution.py:218
  51.6 1.6 %copy.69 = bf16[2,4,16,32,32]{4,3,2,1,0:T(8,128)(2,1)} copy(bf16[2,4,16,32,32]{4,2,1,0,3:T(8,128)(2,1)S(1)} %bitcast.121) | data formatting | bytes 524288 | tf_op jit(solution)/shard_map/transpose | solution.py:219
  53.3 2.3 %reshape.427 = bf16[2,4,16,1024,1]{3,2,1,0,4:T(8,128)(2,1)S(1)} reshape(bf16[2,4,16,32,32]{4,3,2,1,0:T(8,128)(2,1)} %copy.69) | data formatting | bytes 524288 | tf_op jit(solution)/shard_map/reshape | solution.py:220
  55.6 2.5 %fusion.5 = f32[2,2,4,16,1024]{4,3,2,1,0:T(8,128)S(1)} fusion(bf16[2,4,16,1024,1]{3,2,1,0,4:T(8,128)(2,1)S(1)} %reshape.427, bf16[1,1024,1024]{2,1,0:T(8,128)(2,1)S(1)} %bitcast.113, bf16[1,1024,1024]{2,1,0:T(8,128)(2,1)} %bitcast.117), kind=kOutput, calls=%fused_computation.8 | convolution fusion | flops 545259520 | bytes 5505024 | tf_op jit(solution)/shard_map/rcaj,sjb->srcab/dot_general | solution.py:171
  58.1 0.1 fusion.16
  58.2 0.7 fusion.8
  59.0 0.3 fusion.53
  59.3 0.1 subtract_convert_fusion.1
  59.5 0.8 reshape.416
  60.2 1.4 %copy.88 = bf16[2,4,16,32,32]{4,2,1,0,3:T(8,128)(2,1)} copy(bf16[2,4,16,32,32]{4,3,2,1,0:T(8,128)(2,1)S(1)} %reshape.416) | data formatting | bytes 524288 | tf_op jit(solution)/shard_map/reshape | solution.py:245
  61.6 2.5 %reshape.417.x_ref = bf16[32,32,128]{2,1,0:T(8,128)(2,1)} reshape(bf16[32,2,4,16,32]{4,3,2,1,0:T(8,128)(2,1)} %bitcast.122) | data formatting | bytes 524288 | tf_op jit(solution)/shard_map/reshape | solution.py:246
  64.1 12.4 %shard_map.66 = bf16[32,32,128]{2,1,0:T(8,128)(2,1)} custom-call(bf16[32,32,128]{2,1,0:T(8,128)(2,1)} %reshape.417.x_ref), custom_call_target="tpu_custom_call" | custom-call | tf_op jit(solution)/shard_map/pallas_call | solution.py:63
  76.6 1.7 %reshape.418 = bf16[32,2,4,16,32]{4,3,2,1,0:T(8,128)(2,1)S(1)} reshape(bf16[32,32,128]{2,1,0:T(8,128)(2,1)} %shard_map.66) | data formatting | bytes 524288 | tf_op jit(solution)/shard_map/reshape | solution.py:248
  78.3 0.2 copy.71
  78.5 1.4 %copy-done.1 = bf16[32,32,1024]{2,1,0:T(8,128)(2,1)S(1)} copy-done((bf16[32,32,1024]{2,1,0:T(8,128)(2,1)S(1)}, bf16[32,32,1024]{2,1,0:T(8,128)(2,1)}, u32[]{:S(2)}) %copy-start.1) | copy-done | bytes 2097176
  79.9 0.5 convolution_bitcast_fusion
  80.4 0.3 copy.73
  80.7 0.3 copy.74
  81.0 0.8 copy.75.x_ref
  81.9 22.2 %shard_map.67 = bf16[64,4,256]{2,1,0:T(4,128)(2,1)} custom-call(bf16[64,4,256]{2,1,0:T(4,128)(2,1)} %copy.75.x_ref), custom_call_target="tpu_custom_call" | custom-call | tf_op jit(solution)/shard_map/pallas_call | solution.py:63
  104.0 1.3 convert_element_type.132
  105.3 0.1 reduce
  105.4 0.1 convert_bitcast_fusion
  105.5 0.3 copy.76
  105.8 0.3 reshape.423
  106.1 0.7 multiply_convert_fusion
  106.8 0.7 copy.77
  107.5 26.8 %shard_map.68 = bf16[8,8,1024]{2,1,0:T(8,128)(2,1)} custom-call(bf16[8,4,1024]{2,1,0:T(4,128)(2,1)} %bitcast.130, f32[64,32]{1,0:T(8,128)} %bitcast.131), custom_call_target="tpu_custom_call" | custom-call | tf_op jit(solution)/shard_map/pallas_call | solution.py:129
  134.4 1.6 %copy.91 = bf16[8,8192]{1,0:T(8,128)(2,1)} copy(bf16[8,8192]{1,0:T(8,128)(2,1)} %bitcast.129) | data formatting | bytes 262144
  (21 shorter events, 0.2 us)
Async XLA Ops:
  1.1 2.6 %copy-start.3 = (bf16[4,8192]{1,0:T(4,128)(2,1)S(1)}, bf16[4,8192]{1,0:T(4,128)(2,1)}, u32[]{:S(2)}) copy-start(bf16[4,8192]{1,0:T(4,128)(2,1)} %param.7) | copy-start | bytes 196612
  1.1 2.6 %copy-start.4 = (bf16[4,8192]{1,0:T(4,128)(2,1)S(1)}, bf16[4,8192]{1,0:T(4,128)(2,1)}, u32[]{:S(2)}) copy-start(bf16[4,8192]{1,0:T(4,128)(2,1)} %param.6) | copy-start | bytes 196612
  55.6 2.5 %copy-start.2 = (bf16[2,4,16,1024]{3,2,1,0:T(8,128)(2,1)S(1)}, bf16[2,4,16,1024]{3,2,1,0:T(8,128)(2,1)}, u32[]{:S(2)}) copy-start(bf16[2,4,16,1024]{3,2,1,0:T(8,128)(2,1)} %param.9) | copy-start | bytes 786436
  55.6 2.6 %copy-start = (bf16[32,32,1024]{2,1,0:T(8,128)(2,1)S(1)}, bf16[32,32,1024]{2,1,0:T(8,128)(2,1)}, u32[]{:S(2)}) copy-start(bf16[32,32,1024]{2,1,0:T(8,128)(2,1)} %get-tuple-element.16) | copy-start | bytes 6291460
  78.3 1.6 %copy-start.1 = (bf16[32,32,1024]{2,1,0:T(8,128)(2,1)S(1)}, bf16[32,32,1024]{2,1,0:T(8,128)(2,1)}, u32[]{:S(2)}) copy-start(bf16[32,32,1024]{2,1,0:T(8,128)(2,1)} %get-tuple-element.16) | copy-start | bytes 6291460
  81.9 24.2 %copy-start.5 = (bf16[4,8192]{1,0:T(4,128)(2,1)S(1)}, bf16[4,8192]{1,0:T(4,128)(2,1)}, u32[]{:S(2)}) copy-start(bf16[4,8192]{1,0:T(4,128)(2,1)} %param.8) | copy-start | bytes 196612
  81.9 24.2 %copy-start.7 = (f32[4]{0:T(128)S(1)}, f32[4]{0:T(128)}, u32[]{:S(2)}) copy-start(f32[4]{0:T(128)} %param.10) | copy-start | bytes 52
  104.0 2.8 %copy-start.6 = (bf16[32,64]{1,0:T(8,128)(2,1)S(1)}, bf16[32,64]{1,0:T(8,128)(2,1)}, u32[]{:S(2)}) copy-start(bf16[32,64]{1,0:T(8,128)(2,1)} %param.11) | copy-start | bytes 12292

commit v14 on v13

--- a/solution.py
+++ b/solution.py
@@ -121,14 +121,16 @@
     for group_index in range(count):
         mixed[group_index] = total[group_index * outs_here : (group_index + 1) * outs_here].astype(mixed.dtype)
     trade(mixed, back, send_b, recv_b, 1)
-    y_ref[...] = back[...]
+    block = land.shape[2]
+    for group_index in range(count):
+        y_ref[:, group_index * block : (group_index + 1) * block] = back[group_index]
 
 
 def project_over_tp(x, weight, outs_here, collective):
     count, channels, block = x.shape
     return pl.pallas_call(
         _projection_kernel,
-        out_shape=jax.ShapeDtypeStruct((count, outs_here, block), x.dtype),
+        out_shape=jax.ShapeDtypeStruct((outs_here, count * block), x.dtype),
         in_specs=[pl.BlockSpec(memory_space=pltpu.VMEM)] * 2,
         out_specs=pl.BlockSpec(memory_space=pltpu.VMEM),
         scratch_shapes=[
@@ -270,8 +272,7 @@
     outgoing = gated_rows.reshape(channels, tp_count, token_block).transpose(1, 0, 2)
     outs_here = out_weight.shape[1] // tp_count
     weight_columns = out_weight.astype(jnp.float32).T
-    returned = project_over_tp(outgoing, weight_columns, outs_here, 4)
-    return returned.transpose(1, 0, 2).reshape(outs_here, tokens)
+    return project_over_tp(outgoing, weight_columns, outs_here, 4)
 
 
 def solution(mesh):

time: 137 us -> 137 us (level)
  no operation moved by 1% of the time
where the time goes in v14:
time: 137 us; the launch traced here: 136 us
  Pallas kernels  100 us (73%)
  local copies, waits for them, and re-layouts  23.7 us (17%)
  other arithmetic  6.01 us (4%)
  matrix products  5.47 us (4%)
    pallas_call x4, Pallas kernels, exchange(): pl.pallas_call(functools.partial(_exchange_kernel, axis, gather), out_sha...  73.5 us
    pallas_call x1, Pallas kernels, project_over_tp(): pl.pallas_call(_projection_kernel, out_shape=jax.ShapeDtypeStruct((outs_h...  26.8 us
    dot_general x4, matrix products, contract(): return jnp.einsum(form, left, right, preferred_element_type=jnp.float32)  5.47 us
    reshape x3, local copies, waits for them, and re-layouts, local(): arrived.reshape(group, 2, channels, freq_rows, slab)  3.53 us
    unnamed x17, local copies, waits for them, and re-layouts  3 us

profile of v14, /device:TPU:6, one launch (start us, length us, event | category | flops | bytes accessed | tf_op | source)
XLA Modules:
  0.0 135.9 jit_solution(8054394930906942541)
XLA Ops:
  0.0 0.6 fusion.50
  0.6 0.5 fusion.47
  1.1 0.0 copy-start.3
  1.2 2.6 %add_convert_fusion = (bf16[32,32,1024]{2,1,0:T(8,128)(2,1)S(1)}, bf16[32,32,1024]{2,1,0:T(8,128)(2,1)}) fusion(f32[32,1024]{1,0:T(8,128)S(1)} %get-tuple-element.23, f32[32,1024]{1,0:T(8,128)S(1)} %get-tuple-element.20, f32[32,1024]{1,0:T(8,128)S(1)} %get-tuple-element.24, f32[32,1024]{1,0:T(8,128)S(1)} %get-tuple-element.19), kind=kLoop, calls=%fused_computation.4 | loop fusion | flops 8388608 | bytes 4718592 | tf_op jit(solution)/shard_map/convert_element_type | solution.py:163
  3.8 0.2 reshape.406
  4.0 0.1 copy.89
  4.1 0.8 reshape.407.x_ref
  5.0 26.5 %shard_map.64 = bf16[64,4,256]{2,1,0:T(4,128)(2,1)} custom-call(bf16[32,4,256]{2,1,0:T(4,128)(2,1)} %reshape.407.x_ref), custom_call_target="tpu_custom_call" | custom-call | tf_op jit(solution)/shard_map/pallas_call | solution.py:63
  31.5 1.1 copy.63
  32.6 0.3 copy.64
  32.9 1.8 %convolution_bitcast_fusion.1 = f32[2,4,512,32]{2,3,0,1:T(8,128)S(1)} fusion(bf16[4,64,8,32]{3,2,1,0:T(8,128)(2,1)S(1)} %copy.64, s32[]{:T(128)S(6)} %select_n.65, bf16[1,1024,1024]{2,1,0:T(8,128)(2,1)} %bitcast.113, bf16[1,1024,1024]{2,1,0:T(8,128)(2,1)S(1)} %bitcast.109), kind=kOutput, calls=%fused_computation.11 | convolution fusion | flops 136314880 | bytes 4849668 | tf_op jit(solution)/shard_map/sai,cij->scaj/dot_general | solution.py:173
  34.7 0.3 fusion.55
  35.1 0.1 subtract_convert_fusion.3
  35.2 0.3 copy.66
  35.4 0.3 copy.67
  35.7 0.2 maximum_bitcast_fusion
  36.0 0.3 copy.68
  36.3 1.2 reshape.410.x_ref
  37.5 12.4 %shard_map.65 = bf16[32,32,128]{2,1,0:T(8,128)(2,1)} custom-call(bf16[32,32,128]{2,1,0:T(8,128)(2,1)} %reshape.410.x_ref), custom_call_target="tpu_custom_call" | custom-call | tf_op jit(solution)/shard_map/pallas_call | solution.py:63
  49.9 1.7 %reshape.411 = bf16[32,2,4,16,32]{4,3,2,1,0:T(8,128)(2,1)S(1)} reshape(bf16[32,32,128]{2,1,0:T(8,128)(2,1)} %shard_map.65) | data formatting | bytes 524288 | tf_op jit(solution)/shard_map/reshape | solution.py:220
  51.6 1.6 %copy.69 = bf16[2,4,16,32,32]{4,3,2,1,0:T(8,128)(2,1)} copy(bf16[2,4,16,32,32]{4,2,1,0,3:T(8,128)(2,1)S(1)} %bitcast.118) | data formatting | bytes 524288 | tf_op jit(solution)/shard_map/transpose | solution.py:221
  53.3 2.3 %reshape.423 = bf16[2,4,16,1024,1]{3,2,1,0,4:T(8,128)(2,1)S(1)} reshape(bf16[2,4,16,32,32]{4,3,2,1,0:T(8,128)(2,1)} %copy.69) | data formatting | bytes 524288 | tf_op jit(solution)/shard_map/reshape | solution.py:222
  55.6 2.5 %fusion.5 = f32[2,2,4,16,1024]{4,3,2,1,0:T(8,128)S(1)} fusion(bf16[2,4,16,1024,1]{3,2,1,0,4:T(8,128)(2,1)S(1)} %reshape.423, bf16[1,1024,1024]{2,1,0:T(8,128)(2,1)S(1)} %bitcast.110, bf16[1,1024,1024]{2,1,0:T(8,128)(2,1)} %bitcast.114), kind=kOutput, calls=%fused_computation.8 | convolution fusion | flops 545259520 | bytes 5505024 | tf_op jit(solution)/shard_map/rcaj,sjb->srcab/dot_general | solution.py:173
  58.1 0.1 fusion.16
  58.2 0.7 fusion.8
  59.0 0.3 fusion.53
  59.3 0.1 subtract_convert_fusion.1
  59.5 0.8 reshape.413
  60.2 1.4 %copy.88 = bf16[2,4,16,32,32]{4,2,1,0,3:T(8,128)(2,1)} copy(bf16[2,4,16,32,32]{4,3,2,1,0:T(8,128)(2,1)S(1)} %reshape.413) | data formatting | bytes 524288 | tf_op jit(solution)/shard_map/reshape | solution.py:247
  61.6 2.5 %reshape.414.x_ref = bf16[32,32,128]{2,1,0:T(8,128)(2,1)} reshape(bf16[32,2,4,16,32]{4,3,2,1,0:T(8,128)(2,1)} %bitcast.119) | data formatting | bytes 524288 | tf_op jit(solution)/shard_map/reshape | solution.py:248
  64.1 12.4 %shard_map.66 = bf16[32,32,128]{2,1,0:T(8,128)(2,1)} custom-call(bf16[32,32,128]{2,1,0:T(8,128)(2,1)} %reshape.414.x_ref), custom_call_target="tpu_custom_call" | custom-call | tf_op jit(solution)/shard_map/pallas_call | solution.py:63
  76.6 1.7 %reshape.415 = bf16[32,2,4,16,32]{4,3,2,1,0:T(8,128)(2,1)S(1)} reshape(bf16[32,32,128]{2,1,0:T(8,128)(2,1)} %shard_map.66) | data formatting | bytes 524288 | tf_op jit(solution)/shard_map/reshape | solution.py:250
  78.3 0.2 copy.71
  78.5 1.4 %copy-done.1 = bf16[32,32,1024]{2,1,0:T(8,128)(2,1)S(1)} copy-done((bf16[32,32,1024]{2,1,0:T(8,128)(2,1)S(1)}, bf16[32,32,1024]{2,1,0:T(8,128)(2,1)}, u32[]{:S(2)}) %copy-start.1) | copy-done | bytes 2097176
  79.9 0.5 convolution_bitcast_fusion
  80.4 0.3 copy.73
  80.7 0.3 copy.74
  81.0 0.8 copy.75.x_ref
  81.9 22.2 %shard_map.67 = bf16[64,4,256]{2,1,0:T(4,128)(2,1)} custom-call(bf16[64,4,256]{2,1,0:T(4,128)(2,1)} %copy.75.x_ref), custom_call_target="tpu_custom_call" | custom-call | tf_op jit(solution)/shard_map/pallas_call | solution.py:63
  104.0 1.3 convert_element_type.132
  105.3 0.1 reduce
  105.4 0.1 convert_bitcast_fusion
  105.5 0.3 copy.76
  105.8 0.3 reshape.419
  106.1 0.7 multiply_convert_fusion
  106.8 0.7 copy.77
  107.5 26.8 %shard_map.68 = bf16[8,8192]{1,0:T(8,128)(2,1)} custom-call(bf16[8,4,1024]{2,1,0:T(4,128)(2,1)} %bitcast.126, f32[64,32]{1,0:T(8,128)} %bitcast.127), custom_call_target="tpu_custom_call" | custom-call | tf_op jit(solution)/shard_map/pallas_call | solution.py:131
  134.4 1.6 %copy.91 = bf16[8,8192]{1,0:T(8,128)(2,1)} copy(bf16[8,8192]{1,0:T(8,128)(2,1)} %shard_map.68) | data formatting | bytes 262144
  (21 shorter events, 0.2 us)
Async XLA Ops:
  1.1 2.6 %copy-start.3 = (bf16[4,8192]{1,0:T(4,128)(2,1)S(1)}, bf16[4,8192]{1,0:T(4,128)(2,1)}, u32[]{:S(2)}) copy-start(bf16[4,8192]{1,0:T(4,128)(2,1)} %param.7) | copy-start | bytes 196612
  1.1 2.6 %copy-start.4 = (bf16[4,8192]{1,0:T(4,128)(2,1)S(1)}, bf16[4,8192]{1,0:T(4,128)(2,1)}, u32[]{:S(2)}) copy-start(bf16[4,8192]{1,0:T(4,128)(2,1)} %param.6) | copy-start | bytes 196612
  55.6 2.5 %copy-start.2 = (bf16[2,4,16,1024]{3,2,1,0:T(8,128)(2,1)S(1)}, bf16[2,4,16,1024]{3,2,1,0:T(8,128)(2,1)}, u32[]{:S(2)}) copy-start(bf16[2,4,16,1024]{3,2,1,0:T(8,128)(2,1)} %param.9) | copy-start | bytes 786436
  55.6 2.6 %copy-start = (bf16[32,32,1024]{2,1,0:T(8,128)(2,1)S(1)}, bf16[32,32,1024]{2,1,0:T(8,128)(2,1)}, u32[]{:S(2)}) copy-start(bf16[32,32,1024]{2,1,0:T(8,128)(2,1)} %get-tuple-element.16) | copy-start | bytes 6291460
  78.3 1.6 %copy-start.1 = (bf16[32,32,1024]{2,1,0:T(8,128)(2,1)S(1)}, bf16[32,32,1024]{2,1,0:T(8,128)(2,1)}, u32[]{:S(2)}) copy-start(bf16[32,32,1024]{2,1,0:T(8,128)(2,1)} %get-tuple-element.16) | copy-start | bytes 6291460
  81.9 24.2 %copy-start.5 = (bf16[4,8192]{1,0:T(4,128)(2,1)S(1)}, bf16[4,8192]{1,0:T(4,128)(2,1)}, u32[]{:S(2)}) copy-start(bf16[4,8192]{1,0:T(4,128)(2,1)} %param.8) | copy-start | bytes 196612
  81.9 24.2 %copy-start.7 = (f32[4]{0:T(128)S(1)}, f32[4]{0:T(128)}, u32[]{:S(2)}) copy-start(f32[4]{0:T(128)} %param.10) | copy-start | bytes 52
  104.0 2.8 %copy-start.6 = (bf16[32,64]{1,0:T(8,128)(2,1)S(1)}, bf16[32,64]{1,0:T(8,128)(2,1)}, u32[]{:S(2)}) copy-start(bf16[32,64]{1,0:T(8,128)(2,1)} %param.11) | copy-start | bytes 12292

commit v15 on v14

--- a/solution.py
+++ b/solution.py
@@ -112,12 +112,9 @@
         local.wait()
 
     trade(x_ref, land, send_a, recv_a, 0)
-    total = jnp.zeros((count * outs_here, land.shape[2]), jnp.float32)
-    for group_index in range(count):
-        for channel in range(channels):
-            row = land[group_index, channel : channel + 1, :].astype(jnp.float32)
-            column = group_index * channels + channel
-            total = total + w_ref[:, column : column + 1] * row
+    total = jnp.dot(
+        w_ref[...], land[...].reshape(count * channels, land.shape[2]), preferred_element_type=jnp.float32
+    )
     for group_index in range(count):
         mixed[group_index] = total[group_index * outs_here : (group_index + 1) * outs_here].astype(mixed.dtype)
     trade(mixed, back, send_b, recv_b, 1)
@@ -271,7 +268,7 @@
     token_block = tokens // tp_count
     outgoing = gated_rows.reshape(channels, tp_count, token_block).transpose(1, 0, 2)
     outs_here = out_weight.shape[1] // tp_count
-    weight_columns = out_weight.astype(jnp.float32).T
+    weight_columns = out_weight.T
     return project_over_tp(outgoing, weight_columns, outs_here, 4)
 
 

time: 137 us -> 136 us (level)
    unnamed x17 -> x18, local copies, waits for them, and re-layouts: 3 us -> 3.7 us
where the time goes in v15:
time: 136 us; the launch traced here: 135 us
  Pallas kernels  99.8 us (73%)
  local copies, waits for them, and re-layouts  23.7 us (17%)
  other arithmetic  6.01 us (4%)
  matrix products  5.47 us (4%)
    pallas_call x4, Pallas kernels, exchange(): pl.pallas_call(functools.partial(_exchange_kernel, axis, gather), out_sha...  73.5 us
    pallas_call x1, Pallas kernels, project_over_tp(): pl.pallas_call(_projection_kernel, out_shape=jax.ShapeDtypeStruct((outs_h...  26.3 us
    dot_general x4, matrix products, contract(): return jnp.einsum(form, left, right, preferred_element_type=jnp.float32)  5.47 us
    unnamed x18, local copies, waits for them, and re-layouts  3.7 us
    reshape x3, local copies, waits for them, and re-layouts, local(): arrived.reshape(group, 2, channels, freq_rows, slab)  3.53 us

profile of v15, /device:TPU:6, one launch (start us, length us, event | category | flops | bytes accessed | tf_op | source)
XLA Modules:
  0.0 135.4 jit_solution(7341377384448158047)
XLA Ops:
  0.0 0.6 fusion.50
  0.6 0.5 fusion.47
  1.1 0.0 copy-start.3
  1.2 2.6 %add_convert_fusion = (bf16[32,32,1024]{2,1,0:T(8,128)(2,1)S(1)}, bf16[32,32,1024]{2,1,0:T(8,128)(2,1)}) fusion(f32[32,1024]{1,0:T(8,128)S(1)} %get-tuple-element.23, f32[32,1024]{1,0:T(8,128)S(1)} %get-tuple-element.20, f32[32,1024]{1,0:T(8,128)S(1)} %get-tuple-element.24, f32[32,1024]{1,0:T(8,128)S(1)} %get-tuple-element.19), kind=kLoop, calls=%fused_computation.4 | loop fusion | flops 8388608 | bytes 4718592 | tf_op jit(solution)/shard_map/convert_element_type | solution.py:160
  3.8 0.2 reshape.406
  4.0 0.1 copy.73
  4.1 0.8 reshape.407.x_ref
  5.0 26.5 %shard_map.64 = bf16[64,4,256]{2,1,0:T(4,128)(2,1)} custom-call(bf16[32,4,256]{2,1,0:T(4,128)(2,1)} %reshape.407.x_ref), custom_call_target="tpu_custom_call" | custom-call | tf_op jit(solution)/shard_map/pallas_call | solution.py:63
  31.5 1.1 copy.47
  32.6 0.3 copy.48
  32.9 1.8 %convolution_bitcast_fusion.1 = f32[2,4,512,32]{2,3,0,1:T(8,128)S(1)} fusion(bf16[4,64,8,32]{3,2,1,0:T(8,128)(2,1)S(1)} %copy.48, s32[]{:T(128)S(6)} %select_n.65, bf16[1,1024,1024]{2,1,0:T(8,128)(2,1)} %bitcast.113, bf16[1,1024,1024]{2,1,0:T(8,128)(2,1)S(1)} %bitcast.109), kind=kOutput, calls=%fused_computation.11 | convolution fusion | flops 136314880 | bytes 4849668 | tf_op jit(solution)/shard_map/sai,cij->scaj/dot_general | solution.py:170
  34.7 0.3 fusion.55
  35.1 0.1 subtract_convert_fusion.3
  35.2 0.3 copy.50
  35.4 0.3 copy.51
  35.7 0.2 maximum_bitcast_fusion
  36.0 0.3 copy.52
  36.3 1.2 reshape.410.x_ref
  37.5 12.4 %shard_map.65 = bf16[32,32,128]{2,1,0:T(8,128)(2,1)} custom-call(bf16[32,32,128]{2,1,0:T(8,128)(2,1)} %reshape.410.x_ref), custom_call_target="tpu_custom_call" | custom-call | tf_op jit(solution)/shard_map/pallas_call | solution.py:63
  49.9 1.7 %reshape.411 = bf16[32,2,4,16,32]{4,3,2,1,0:T(8,128)(2,1)S(1)} reshape(bf16[32,32,128]{2,1,0:T(8,128)(2,1)} %shard_map.65) | data formatting | bytes 524288 | tf_op jit(solution)/shard_map/reshape | solution.py:217
  51.6 1.6 %copy.53 = bf16[2,4,16,32,32]{4,3,2,1,0:T(8,128)(2,1)} copy(bf16[2,4,16,32,32]{4,2,1,0,3:T(8,128)(2,1)S(1)} %bitcast.118) | data formatting | bytes 524288 | tf_op jit(solution)/shard_map/transpose | solution.py:218
  53.3 2.3 %reshape.423 = bf16[2,4,16,1024,1]{3,2,1,0,4:T(8,128)(2,1)S(1)} reshape(bf16[2,4,16,32,32]{4,3,2,1,0:T(8,128)(2,1)} %copy.53) | data formatting | bytes 524288 | tf_op jit(solution)/shard_map/reshape | solution.py:219
  55.6 2.5 %fusion.5 = f32[2,2,4,16,1024]{4,3,2,1,0:T(8,128)S(1)} fusion(bf16[2,4,16,1024,1]{3,2,1,0,4:T(8,128)(2,1)S(1)} %reshape.423, bf16[1,1024,1024]{2,1,0:T(8,128)(2,1)S(1)} %bitcast.110, bf16[1,1024,1024]{2,1,0:T(8,128)(2,1)} %bitcast.114), kind=kOutput, calls=%fused_computation.8 | convolution fusion | flops 545259520 | bytes 5505024 | tf_op jit(solution)/shard_map/rcaj,sjb->srcab/dot_general | solution.py:170
  58.1 0.1 fusion.16
  58.2 0.7 fusion.8
  59.0 0.3 fusion.53
  59.3 0.1 subtract_convert_fusion.1
  59.5 0.8 reshape.413
  60.2 1.4 %copy.72 = bf16[2,4,16,32,32]{4,2,1,0,3:T(8,128)(2,1)} copy(bf16[2,4,16,32,32]{4,3,2,1,0:T(8,128)(2,1)S(1)} %reshape.413) | data formatting | bytes 524288 | tf_op jit(solution)/shard_map/reshape | solution.py:244
  61.6 2.5 %reshape.414.x_ref = bf16[32,32,128]{2,1,0:T(8,128)(2,1)} reshape(bf16[32,2,4,16,32]{4,3,2,1,0:T(8,128)(2,1)} %bitcast.119) | data formatting | bytes 524288 | tf_op jit(solution)/shard_map/reshape | solution.py:245
  64.1 12.4 %shard_map.66 = bf16[32,32,128]{2,1,0:T(8,128)(2,1)} custom-call(bf16[32,32,128]{2,1,0:T(8,128)(2,1)} %reshape.414.x_ref), custom_call_target="tpu_custom_call" | custom-call | tf_op jit(solution)/shard_map/pallas_call | solution.py:63
  76.6 1.7 %reshape.415 = bf16[32,2,4,16,32]{4,3,2,1,0:T(8,128)(2,1)S(1)} reshape(bf16[32,32,128]{2,1,0:T(8,128)(2,1)} %shard_map.66) | data formatting | bytes 524288 | tf_op jit(solution)/shard_map/reshape | solution.py:247
  78.3 0.2 copy.55
  78.5 1.4 %copy-done.1 = bf16[32,32,1024]{2,1,0:T(8,128)(2,1)S(1)} copy-done((bf16[32,32,1024]{2,1,0:T(8,128)(2,1)S(1)}, bf16[32,32,1024]{2,1,0:T(8,128)(2,1)}, u32[]{:S(2)}) %copy-start.1) | copy-done | bytes 2097176
  79.9 0.5 convolution_bitcast_fusion
  80.4 0.3 copy.57
  80.7 0.3 copy.58
  81.0 0.8 copy.59.x_ref
  81.9 22.2 %shard_map.67 = bf16[64,4,256]{2,1,0:T(4,128)(2,1)} custom-call(bf16[64,4,256]{2,1,0:T(4,128)(2,1)} %copy.59.x_ref), custom_call_target="tpu_custom_call" | custom-call | tf_op jit(solution)/shard_map/pallas_call | solution.py:63
  104.0 1.3 convert_element_type.131
  105.3 0.1 reduce
  105.4 0.1 convert_bitcast_fusion
  105.5 0.3 copy.60
  105.8 0.3 reshape.419
  106.1 0.7 multiply_convert_fusion
  106.8 0.7 copy.61
  107.5 26.3 %shard_map.68 = bf16[8,8192]{1,0:T(8,128)(2,1)} custom-call(bf16[8,4,1024]{2,1,0:T(4,128)(2,1)} %bitcast.126, bf16[64,32]{1,0:T(8,128)(2,1)} %bitcast.127), custom_call_target="tpu_custom_call" | custom-call | tf_op jit(solution)/shard_map/pallas_call | solution.py:128
  133.8 1.6 %copy.75 = bf16[8,8192]{1,0:T(8,128)(2,1)} copy(bf16[8,8192]{1,0:T(8,128)(2,1)} %shard_map.68) | data formatting | bytes 262144
  (21 shorter events, 0.2 us)
Async XLA Ops:
  1.1 2.6 %copy-start.3 = (bf16[4,8192]{1,0:T(4,128)(2,1)S(1)}, bf16[4,8192]{1,0:T(4,128)(2,1)}, u32[]{:S(2)}) copy-start(bf16[4,8192]{1,0:T(4,128)(2,1)} %param.7) | copy-start | bytes 196612
  1.1 2.6 %copy-start.4 = (bf16[4,8192]{1,0:T(4,128)(2,1)S(1)}, bf16[4,8192]{1,0:T(4,128)(2,1)}, u32[]{:S(2)}) copy-start(bf16[4,8192]{1,0:T(4,128)(2,1)} %param.6) | copy-start | bytes 196612
  55.6 2.5 %copy-start.2 = (bf16[2,4,16,1024]{3,2,1,0:T(8,128)(2,1)S(1)}, bf16[2,4,16,1024]{3,2,1,0:T(8,128)(2,1)}, u32[]{:S(2)}) copy-start(bf16[2,4,16,1024]{3,2,1,0:T(8,128)(2,1)} %param.9) | copy-start | bytes 786436
  55.6 2.6 %copy-start = (bf16[32,32,1024]{2,1,0:T(8,128)(2,1)S(1)}, bf16[32,32,1024]{2,1,0:T(8,128)(2,1)}, u32[]{:S(2)}) copy-start(bf16[32,32,1024]{2,1,0:T(8,128)(2,1)} %get-tuple-element.16) | copy-start | bytes 6291460
  78.3 1.6 %copy-start.1 = (bf16[32,32,1024]{2,1,0:T(8,128)(2,1)S(1)}, bf16[32,32,1024]{2,1,0:T(8,128)(2,1)}, u32[]{:S(2)}) copy-start(bf16[32,32,1024]{2,1,0:T(8,128)(2,1)} %get-tuple-element.16) | copy-start | bytes 6291460
  81.9 24.2 %copy-start.5 = (bf16[4,8192]{1,0:T(4,128)(2,1)S(1)}, bf16[4,8192]{1,0:T(4,128)(2,1)}, u32[]{:S(2)}) copy-start(bf16[4,8192]{1,0:T(4,128)(2,1)} %param.8) | copy-start | bytes 196612
  81.9 24.2 %copy-start.7 = (f32[4]{0:T(128)S(1)}, f32[4]{0:T(128)}, u32[]{:S(2)}) copy-start(f32[4]{0:T(128)} %param.10) | copy-start | bytes 52
  104.0 2.8 %copy-start.6 = (bf16[32,64]{1,0:T(8,128)(2,1)S(1)}, bf16[32,64]{1,0:T(8,128)(2,1)}, u32[]{:S(2)}) copy-start(bf16[32,64]{1,0:T(8,128)(2,1)} %param.11) | copy-start | bytes 12292

commit v16 on v15

--- a/solution.py
+++ b/solution.py
@@ -22,11 +22,13 @@
         pl.semaphore_signal(barrier, 1, device_id={axis: base + peer}, device_id_type=MESH)
         return carry
 
+    def piece(peer):
+        return x_ref if gather else x_ref.at[lax.rem(peer, x_ref.shape[0])]
+
+    local = pltpu.make_async_copy(piece(me), land.at[me], local_sem)
+    local.start()
     lax.fori_loop(1, count, greet, 0)
     pl.semaphore_wait(barrier, count - 1)
-
-    def piece(peer):
-        return x_ref if gather else x_ref.at[lax.rem(peer, x_ref.shape[0])]
 
     def outgoing(peer):
         return pltpu.make_async_remote_copy(
@@ -43,8 +45,6 @@
         return carry
 
     lax.fori_loop(1, count, send, 0)
-    local = pltpu.make_async_copy(piece(me), land.at[me], local_sem)
-    local.start()
 
     def finish(step, carry):
         outgoing(lax.rem(me + step, count)).wait_send()

time: 136 us -> 136 us (level)
  no operation moved by 1% of the time
where the time goes in v16:
time: 136 us; the launch traced here: 135 us
  Pallas kernels  99.9 us (73%)
  local copies, waits for them, and re-layouts  23.7 us (17%)
  other arithmetic  6.01 us (4%)
  matrix products  5.48 us (4%)
    pallas_call x4, Pallas kernels, exchange(): pl.pallas_call(functools.partial(_exchange_kernel, axis, gather), out_sha...  73.6 us
    pallas_call x1, Pallas kernels, project_over_tp(): pl.pallas_call(_projection_kernel, out_shape=jax.ShapeDtypeStruct((outs_h...  26.3 us
    dot_general x4, matrix products, contract(): return jnp.einsum(form, left, right, preferred_element_type=jnp.float32)  5.48 us
    unnamed x18, local copies, waits for them, and re-layouts  3.7 us
    reshape x3, local copies, waits for them, and re-layouts, local(): arrived.reshape(group, 2, channels, freq_rows, slab)  3.53 us

profile of v16, /device:TPU:6, one launch (start us, length us, event | category | flops | bytes accessed | tf_op | source)
XLA Modules:
  0.0 135.4 jit_solution(9491643533349413353)
XLA Ops:
  0.0 0.6 fusion.50
  0.6 0.5 fusion.47
  1.1 0.0 copy-start.3
  1.2 2.6 %add_convert_fusion = (bf16[32,32,1024]{2,1,0:T(8,128)(2,1)S(1)}, bf16[32,32,1024]{2,1,0:T(8,128)(2,1)}) fusion(f32[32,1024]{1,0:T(8,128)S(1)} %get-tuple-element.23, f32[32,1024]{1,0:T(8,128)S(1)} %get-tuple-element.20, f32[32,1024]{1,0:T(8,128)S(1)} %get-tuple-element.24, f32[32,1024]{1,0:T(8,128)S(1)} %get-tuple-element.19), kind=kLoop, calls=%fused_computation.4 | loop fusion | flops 8388608 | bytes 4718592 | tf_op jit(solution)/shard_map/convert_element_type | solution.py:160
  3.8 0.2 reshape.406
  4.0 0.1 copy.73
  4.1 0.8 reshape.407.x_ref
  5.0 26.6 %shard_map.64 = bf16[64,4,256]{2,1,0:T(4,128)(2,1)} custom-call(bf16[32,4,256]{2,1,0:T(4,128)(2,1)} %reshape.407.x_ref), custom_call_target="tpu_custom_call" | custom-call | tf_op jit(solution)/shard_map/pallas_call | solution.py:63
  31.5 1.1 copy.47
  32.6 0.3 copy.48
  33.0 1.8 %convolution_bitcast_fusion.1 = f32[2,4,512,32]{2,3,0,1:T(8,128)S(1)} fusion(bf16[4,64,8,32]{3,2,1,0:T(8,128)(2,1)S(1)} %copy.48, s32[]{:T(128)S(6)} %select_n.65, bf16[1,1024,1024]{2,1,0:T(8,128)(2,1)} %bitcast.113, bf16[1,1024,1024]{2,1,0:T(8,128)(2,1)S(1)} %bitcast.109), kind=kOutput, calls=%fused_computation.11 | convolution fusion | flops 136314880 | bytes 4849668 | tf_op jit(solution)/shard_map/sai,cij->scaj/dot_general | solution.py:170
  34.8 0.3 fusion.55
  35.1 0.1 subtract_convert_fusion.3
  35.2 0.3 copy.50
  35.5 0.3 copy.51
  35.8 0.2 maximum_bitcast_fusion
  36.0 0.3 copy.52
  36.3 1.2 reshape.410.x_ref
  37.5 12.5 %shard_map.65 = bf16[32,32,128]{2,1,0:T(8,128)(2,1)} custom-call(bf16[32,32,128]{2,1,0:T(8,128)(2,1)} %reshape.410.x_ref), custom_call_target="tpu_custom_call" | custom-call | tf_op jit(solution)/shard_map/pallas_call | solution.py:63
  50.0 1.7 %reshape.411 = bf16[32,2,4,16,32]{4,3,2,1,0:T(8,128)(2,1)S(1)} reshape(bf16[32,32,128]{2,1,0:T(8,128)(2,1)} %shard_map.65) | data formatting | bytes 524288 | tf_op jit(solution)/shard_map/reshape | solution.py:217
  51.7 1.6 %copy.53 = bf16[2,4,16,32,32]{4,3,2,1,0:T(8,128)(2,1)} copy(bf16[2,4,16,32,32]{4,2,1,0,3:T(8,128)(2,1)S(1)} %bitcast.118) | data formatting | bytes 524288 | tf_op jit(solution)/shard_map/transpose | solution.py:218
  53.3 2.3 %reshape.423 = bf16[2,4,16,1024,1]{3,2,1,0,4:T(8,128)(2,1)S(1)} reshape(bf16[2,4,16,32,32]{4,3,2,1,0:T(8,128)(2,1)} %copy.53) | data formatting | bytes 524288 | tf_op jit(solution)/shard_map/reshape | solution.py:219
  55.7 2.5 %fusion.5 = f32[2,2,4,16,1024]{4,3,2,1,0:T(8,128)S(1)} fusion(bf16[2,4,16,1024,1]{3,2,1,0,4:T(8,128)(2,1)S(1)} %reshape.423, bf16[1,1024,1024]{2,1,0:T(8,128)(2,1)S(1)} %bitcast.110, bf16[1,1024,1024]{2,1,0:T(8,128)(2,1)} %bitcast.114), kind=kOutput, calls=%fused_computation.8 | convolution fusion | flops 545259520 | bytes 5505024 | tf_op jit(solution)/shard_map/rcaj,sjb->srcab/dot_general | solution.py:170
  58.2 0.1 fusion.16
  58.3 0.7 fusion.8
  59.0 0.3 fusion.53
  59.4 0.1 subtract_convert_fusion.1
  59.5 0.8 reshape.413
  60.3 1.4 %copy.72 = bf16[2,4,16,32,32]{4,2,1,0,3:T(8,128)(2,1)} copy(bf16[2,4,16,32,32]{4,3,2,1,0:T(8,128)(2,1)S(1)} %reshape.413) | data formatting | bytes 524288 | tf_op jit(solution)/shard_map/reshape | solution.py:244
  61.7 2.5 %reshape.414.x_ref = bf16[32,32,128]{2,1,0:T(8,128)(2,1)} reshape(bf16[32,2,4,16,32]{4,3,2,1,0:T(8,128)(2,1)} %bitcast.119) | data formatting | bytes 524288 | tf_op jit(solution)/shard_map/reshape | solution.py:245
  64.2 12.4 %shard_map.66 = bf16[32,32,128]{2,1,0:T(8,128)(2,1)} custom-call(bf16[32,32,128]{2,1,0:T(8,128)(2,1)} %reshape.414.x_ref), custom_call_target="tpu_custom_call" | custom-call | tf_op jit(solution)/shard_map/pallas_call | solution.py:63
  76.7 1.7 %reshape.415 = bf16[32,2,4,16,32]{4,3,2,1,0:T(8,128)(2,1)S(1)} reshape(bf16[32,32,128]{2,1,0:T(8,128)(2,1)} %shard_map.66) | data formatting | bytes 524288 | tf_op jit(solution)/shard_map/reshape | solution.py:247
  78.4 0.2 copy.55
  78.5 1.4 %copy-done.1 = bf16[32,32,1024]{2,1,0:T(8,128)(2,1)S(1)} copy-done((bf16[32,32,1024]{2,1,0:T(8,128)(2,1)S(1)}, bf16[32,32,1024]{2,1,0:T(8,128)(2,1)}, u32[]{:S(2)}) %copy-start.1) | copy-done | bytes 2097176
  79.9 0.5 convolution_bitcast_fusion
  80.5 0.3 copy.57
  80.8 0.3 copy.58
  81.1 0.8 copy.59.x_ref
  81.9 22.1 %shard_map.67 = bf16[64,4,256]{2,1,0:T(4,128)(2,1)} custom-call(bf16[64,4,256]{2,1,0:T(4,128)(2,1)} %copy.59.x_ref), custom_call_target="tpu_custom_call" | custom-call | tf_op jit(solution)/shard_map/pallas_call | solution.py:63
  104.1 1.3 convert_element_type.131
  105.3 0.1 reduce
  105.5 0.1 convert_bitcast_fusion
  105.5 0.3 copy.60
  105.9 0.3 reshape.419
  106.1 0.7 multiply_convert_fusion
  106.9 0.7 copy.61
  107.6 26.3 %shard_map.68 = bf16[8,8192]{1,0:T(8,128)(2,1)} custom-call(bf16[8,4,1024]{2,1,0:T(4,128)(2,1)} %bitcast.126, bf16[64,32]{1,0:T(8,128)(2,1)} %bitcast.127), custom_call_target="tpu_custom_call" | custom-call | tf_op jit(solution)/shard_map/pallas_call | solution.py:128
  133.9 1.6 %copy.75 = bf16[8,8192]{1,0:T(8,128)(2,1)} copy(bf16[8,8192]{1,0:T(8,128)(2,1)} %shard_map.68) | data formatting | bytes 262144
  (21 shorter events, 0.2 us)
Async XLA Ops:
  1.1 2.6 %copy-start.3 = (bf16[4,8192]{1,0:T(4,128)(2,1)S(1)}, bf16[4,8192]{1,0:T(4,128)(2,1)}, u32[]{:S(2)}) copy-start(bf16[4,8192]{1,0:T(4,128)(2,1)} %param.7) | copy-start | bytes 196612
  1.1 2.6 %copy-start.4 = (bf16[4,8192]{1,0:T(4,128)(2,1)S(1)}, bf16[4,8192]{1,0:T(4,128)(2,1)}, u32[]{:S(2)}) copy-start(bf16[4,8192]{1,0:T(4,128)(2,1)} %param.6) | copy-start | bytes 196612
  55.7 2.5 %copy-start.2 = (bf16[2,4,16,1024]{3,2,1,0:T(8,128)(2,1)S(1)}, bf16[2,4,16,1024]{3,2,1,0:T(8,128)(2,1)}, u32[]{:S(2)}) copy-start(bf16[2,4,16,1024]{3,2,1,0:T(8,128)(2,1)} %param.9) | copy-start | bytes 786436
  55.7 2.6 %copy-start = (bf16[32,32,1024]{2,1,0:T(8,128)(2,1)S(1)}, bf16[32,32,1024]{2,1,0:T(8,128)(2,1)}, u32[]{:S(2)}) copy-start(bf16[32,32,1024]{2,1,0:T(8,128)(2,1)} %get-tuple-element.16) | copy-start | bytes 6291460
  78.3 1.6 %copy-start.1 = (bf16[32,32,1024]{2,1,0:T(8,128)(2,1)S(1)}, bf16[32,32,1024]{2,1,0:T(8,128)(2,1)}, u32[]{:S(2)}) copy-start(bf16[32,32,1024]{2,1,0:T(8,128)(2,1)} %get-tuple-element.16) | copy-start | bytes 6291460
  81.9 24.2 %copy-start.5 = (bf16[4,8192]{1,0:T(4,128)(2,1)S(1)}, bf16[4,8192]{1,0:T(4,128)(2,1)}, u32[]{:S(2)}) copy-start(bf16[4,8192]{1,0:T(4,128)(2,1)} %param.8) | copy-start | bytes 196612
  81.9 24.2 %copy-start.7 = (f32[4]{0:T(128)S(1)}, f32[4]{0:T(128)}, u32[]{:S(2)}) copy-start(f32[4]{0:T(128)} %param.10) | copy-start | bytes 52
  104.1 2.8 %copy-start.6 = (bf16[32,64]{1,0:T(8,128)(2,1)S(1)}, bf16[32,64]{1,0:T(8,128)(2,1)}, u32[]{:S(2)}) copy-start(bf16[32,64]{1,0:T(8,128)(2,1)} %param.11) | copy-start | bytes 12292
